TPU v7x, 32 devices: a whole 2x2x4 slice. The times are simulated.
32 devices in a mesh: dp: 8 (over y, x, core), tensor: 4 (over z).
Axes of the slice: x: 2, y: 2, z: 4, core: 2. Of those that a mesh axis runs over, the one named last changes fastest.
Arguments:
- inputs: bfloat16 [8192, 2048], P(('dp', 'tensor')), may hold values from -6 to 6
- cotangent: bfloat16 [8192, 2048], P(('dp', 'tensor')), may hold values from -6 to 6
- attn_gain: bfloat16 [2048], P('dp'), may hold values from 0.5 to 1.5
- w_query: bfloat16 [2048, 2048], P('dp', 'tensor'), may hold values from -0.1875 to 0.1875
- w_key: bfloat16 [2048, 512], P('dp', 'tensor'), may hold values from -0.1875 to 0.1875
- w_value: bfloat16 [2048, 512], P('dp', 'tensor'), may hold values from -0.125 to 0.125
- w_out: bfloat16 [2048, 2048], P(('tensor', 'dp')), may hold values from -1 to 1
- mlp_gain: bfloat16 [2048], P('dp'), may hold values from 0.5 to 1.5
- w_gate: bfloat16 [2048, 8192], P('dp', 'tensor'), may hold values from -0.125 to 0.125
- w_up: bfloat16 [2048, 8192], P('dp', 'tensor'), may hold values from -0.125 to 0.125
- w_down: bfloat16 [8192, 2048], P(('tensor', 'dp')), may hold values from -0.125 to 0.125
- seq_lengths: int32 [12], replicated, may hold values from 256 to 1024, as said below
- group_perm: int32 [12], replicated, may hold values from 0 to 11, as said below
- group_starts: int32 [9], replicated, may hold values from 0 to 12, as said below
Outputs:
- outputs: bfloat16 [8192, 2048], P(('dp', 'tensor'))
- input_grad: bfloat16 [8192, 2048], P(('dp', 'tensor'))
- attn_gain_grad: float32 [2048], P('dp')
- w_query_grad: float32 [2048, 2048], P('dp', 'tensor')
- w_key_grad: float32 [2048, 512], P('dp', 'tensor')
- w_value_grad: float32 [2048, 512], P('dp', 'tensor')
- w_out_grad: float32 [2048, 2048], P(('tensor', 'dp'))
- mlp_gain_grad: float32 [2048], P('dp')
- w_gate_grad: float32 [2048, 8192], P('dp', 'tensor')
- w_up_grad: float32 [2048, 8192], P('dp', 'tensor')
- w_down_grad: float32 [8192, 2048], P(('tensor', 'dp'))
Inputs may be any that keep to these rules, and one draw needn't show every extreme that they name: `seq_lengths`: every length is a multiple of 128; the sequences of one group take at most 1024 rows together, and some sequence fills a group alone. `group_perm`: each sequence number appears once. `group_starts`: starts at 0, ends at 12, and rises by one or two from group to group: a group holds 1 to 2 sequences.
All inputs are finite; a program needn't handle non-finite values.
Results may differ from a plain program's by a relative error of at most 0.025.
Values may be sent and summed in bfloat16 or wider, within the bound.
A program may use at most 256 MiB of HBM per device.

v0:
```python
import math

import jax
import jax.numpy as jnp
from jax import lax
from jax.sharding import PartitionSpec as P

HEAD_SIZE = 64
MOST_SEQS = 2


norm_epsilon = 1e-05
rope_theta = 500000.0
rope_factor = 32.0
low_factor = 1.0
high_factor = 4.0
context_span = 8192.0
mask_fill = -1e30


def rotary_freqs(head_size):
    exponents = jnp.arange(0, head_size, 2).astype(jnp.float32) / head_size
    inverse = 1.0 / jnp.power(jnp.float32(rope_theta), exponents)
    wavelength = 2.0 * math.pi / inverse
    smooth = (context_span / wavelength - low_factor) / (high_factor - low_factor)
    blended = (1.0 - smooth) * inverse / rope_factor + smooth * inverse
    scaled = jnp.where(wavelength > context_span / low_factor, inverse / rope_factor, blended)
    return jnp.where(wavelength < context_span / high_factor, inverse, scaled)


def rotary_tables(positions, head_size):
    angles = positions.astype(jnp.float32)[:, None] * rotary_freqs(head_size)[None, :]
    angles = jnp.concatenate([angles, angles], axis=1)
    return (jnp.cos(angles)[:, None, :], jnp.sin(angles)[:, None, :])


def rotary(vectors, cosine, sine_table):
    half_size = vectors.shape[-1] // 2
    turned = jnp.concatenate([-vectors[..., half_size:], vectors[..., :half_size]], axis=-1)
    return vectors * cosine + turned * sine_table


def rotary_back(grads, cosine, sine_table):
    half_size = grads.shape[-1] // 2
    shifted = grads * sine_table
    return grads * cosine + jnp.concatenate(
        [shifted[..., half_size:], -shifted[..., :half_size]], axis=-1
    )


def group_layout(seq_lengths, group_perm, group_starts, group_id, row_total, slot_total):
    bounds = jnp.arange(group_starts.shape[0], dtype=jnp.int32)
    numbers = jnp.arange(group_perm.shape[0], dtype=jnp.int32)
    opening = jnp.sum(jnp.where(bounds == group_id, group_starts, 0))
    closing = jnp.sum(jnp.where(bounds == group_id + 1, group_starts, 0))
    row_ids = jnp.arange(row_total, dtype=jnp.int32)
    segment = jnp.zeros((row_total,), jnp.int32)
    offset = jnp.zeros((row_total,), jnp.int32)
    finish = jnp.zeros((), jnp.int32)
    for slot_id in range(slot_total):
        slot_place = opening + slot_id
        sequence = jnp.sum(jnp.where(numbers == slot_place, group_perm, 0))
        length = jnp.sum(jnp.where(numbers == sequence, seq_lengths, 0))
        length = jnp.where(slot_place < closing, length, 0)
        finish = finish + length
        passed = row_ids >= finish
        segment = segment + passed.astype(jnp.int32)
        offset = jnp.where(passed, finish, offset)
    return (segment, row_ids - offset)


def gain_norm(vectors, scales):
    return (
        vectors
        * lax.rsqrt(jnp.mean(vectors * vectors, axis=-1, keepdims=True) + norm_epsilon)
        * scales
    )


def project(left, right):
    return jnp.dot(left, right, preferred_element_type=jnp.float32)


def project_back(left, right):
    return lax.dot_general(
        left, right, (((1,), (1,)), ((), ())), preferred_element_type=jnp.float32
    )


def row_contract(left, right):
    return lax.dot_general(
        left, right, (((0,), (0,)), ((), ())), preferred_element_type=jnp.float32
    )


def block_scores(block_queries, key_rows, segment, first_row, block_span):
    scale_factor = block_queries.shape[-1] ** (-0.5)
    scores = (
        jnp.einsum("qcgd,kcd->cgqk", block_queries, key_rows, preferred_element_type=jnp.float32)
        * scale_factor
    )
    row_ids = jnp.arange(key_rows.shape[0], dtype=jnp.int32)
    query_ids = row_ids[first_row : first_row + block_span]
    query_segments = segment[first_row : first_row + block_span]
    allowed = (query_segments[:, None] == segment[None, :]) & (
        row_ids[None, :] <= query_ids[:, None]
    )
    return jnp.where(allowed, scores, mask_fill)


def attend(queries, key_rows, value_rows, segment):
    row_total, local_groups, members, head_size = queries.shape
    block_span = 512
    value_heads = value_rows.reshape(row_total, local_groups, head_size)
    pieces = []
    totals = []
    for first_row in range(0, row_total, block_span):
        block_queries = queries[first_row : first_row + block_span]
        scores = block_scores(block_queries, key_rows, segment, first_row, block_span)
        row_top = jnp.max(scores, axis=-1, keepdims=True)
        weights = jnp.exp(scores - row_top)
        total_weight = jnp.sum(weights, axis=-1, keepdims=True)
        chances = (weights / total_weight).astype(jnp.bfloat16)
        pieces.append(
            jnp.einsum("cgqk,kcd->qcgd", chances, value_heads, preferred_element_type=jnp.float32)
        )
        totals.append(row_top + jnp.log(total_weight))
    mixed_heads = jnp.concatenate(pieces, axis=0).reshape(
        row_total, local_groups * members * head_size
    )
    return (mixed_heads.astype(jnp.bfloat16), jnp.concatenate(totals, axis=2))


def attend_back(queries, key_rows, value_rows, segment, log_totals, mixed_grad):
    row_total, local_groups, members, head_size = queries.shape
    block_span = 512
    scale_factor = head_size ** (-0.5)
    value_heads = value_rows.reshape(row_total, local_groups, head_size)
    grad_heads = mixed_grad.reshape(row_total, local_groups, members, head_size)
    key_grad = jnp.zeros((row_total, local_groups, head_size), jnp.float32)
    value_grad = jnp.zeros((row_total, local_groups, head_size), jnp.float32)
    query_pieces = []
    for first_row in range(0, row_total, block_span):
        block_queries = queries[first_row : first_row + block_span]
        block_grad = grad_heads[first_row : first_row + block_span]
        scores = block_scores(block_queries, key_rows, segment, first_row, block_span)
        chances = jnp.exp(scores - log_totals[:, :, first_row : first_row + block_span])
        value_grad = value_grad + jnp.einsum(
            "cgqk,qcgd->kcd",
            chances.astype(jnp.bfloat16),
            block_grad,
            preferred_element_type=jnp.float32,
        )
        chances_grad = jnp.einsum(
            "qcgd,kcd->cgqk", block_grad, value_heads, preferred_element_type=jnp.float32
        )
        shared = jnp.sum(chances * chances_grad, axis=-1, keepdims=True)
        score_grad = (chances * (chances_grad - shared)).astype(jnp.bfloat16)
        query_pieces.append(
            jnp.einsum("cgqk,kcd->qcgd", score_grad, key_rows, preferred_element_type=jnp.float32)
            * scale_factor
        )
        key_grad = (
            key_grad
            + jnp.einsum(
                "cgqk,qcgd->kcd", score_grad, block_queries, preferred_element_type=jnp.float32
            )
            * scale_factor
        )
    query_grad = jnp.concatenate(query_pieces, axis=0).reshape(
        row_total, local_groups * members, head_size
    )
    return (query_grad, key_grad, value_grad)


def shards(
    inputs,
    cotangent,
    attn_gain,
    w_query,
    w_key,
    w_value,
    w_out,
    mlp_gain,
    w_gate,
    w_up,
    w_down,
    seq_lengths,
    group_perm,
    group_starts,
):
    tokens_dev = inputs.shape[0]
    group_rows = tokens_dev * lax.axis_size("tensor")
    segment, positions = group_layout(
        seq_lengths, group_perm, group_starts, lax.axis_index("dp"), group_rows, MOST_SEQS
    )
    cosine, sine_table = rotary_tables(positions, HEAD_SIZE)
    residual = inputs.astype(jnp.float32)
    gain_one, query_full, key_full, value_full, out_full = (
        lax.all_gather(attn_gain, "dp", axis=0, tiled=True),
        lax.all_gather(w_query, "dp", axis=0, tiled=True),
        lax.all_gather(w_key, "dp", axis=0, tiled=True),
        lax.all_gather(w_value, "dp", axis=0, tiled=True),
        lax.all_gather(w_out, "dp", axis=0, tiled=True),
    )
    normed_f, norm_one_back = jax.vjp(gain_norm, residual, gain_one.astype(jnp.float32))
    normed = normed_f.astype(jnp.bfloat16)
    normed_full = lax.all_gather(normed, "tensor", axis=0, tiled=True)
    local_heads = query_full.shape[1] // HEAD_SIZE
    local_groups = key_full.shape[1] // HEAD_SIZE
    members = local_heads // local_groups
    query_pre = project(normed_full, query_full).reshape(group_rows, local_heads, HEAD_SIZE)
    queries = (
        rotary(query_pre, cosine, sine_table)
        .astype(jnp.bfloat16)
        .reshape(group_rows, local_groups, members, HEAD_SIZE)
    )
    key_pre = project(normed_full, key_full).reshape(group_rows, local_groups, HEAD_SIZE)
    key_rows = rotary(key_pre, cosine, sine_table).astype(jnp.bfloat16)
    value_rows = project(normed_full, value_full).astype(jnp.bfloat16)
    mixed_heads, log_totals = attend(queries, key_rows, value_rows, segment)
    middle = residual + lax.psum_scatter(
        project(mixed_heads, out_full).astype(jnp.bfloat16),
        "tensor",
        scatter_dimension=0,
        tiled=True,
    ).astype(jnp.float32)
    gain_two, gate_full, up_full, down_full = (
        lax.all_gather(mlp_gain, "dp", axis=0, tiled=True),
        lax.all_gather(w_gate, "dp", axis=0, tiled=True),
        lax.all_gather(w_up, "dp", axis=0, tiled=True),
        lax.all_gather(w_down, "dp", axis=0, tiled=True),
    )
    normed_two_f, norm_two_back = jax.vjp(gain_norm, middle, gain_two.astype(jnp.float32))
    normed_two_full = lax.all_gather(
        normed_two_f.astype(jnp.bfloat16), "tensor", axis=0, tiled=True
    )
    gate_pre = project(normed_two_full, gate_full)
    up_pre = project(normed_two_full, up_full)
    active_f, active_back = jax.vjp(
        lambda gate_in, up_in: jax.nn.silu(gate_in) * up_in, gate_pre, up_pre
    )
    active = active_f.astype(jnp.bfloat16)
    outputs = (
        middle
        + lax.psum_scatter(
            project(active, down_full).astype(jnp.bfloat16),
            "tensor",
            scatter_dimension=0,
            tiled=True,
        ).astype(jnp.float32)
    ).astype(jnp.bfloat16)
    grad_full = lax.all_gather(cotangent, "tensor", axis=0, tiled=True)
    gate_back_w, up_back_w, down_back_w = (
        lax.all_gather(w_gate, "dp", axis=0, tiled=True),
        lax.all_gather(w_up, "dp", axis=0, tiled=True),
        lax.all_gather(w_down, "dp", axis=0, tiled=True),
    )
    active_grad = project_back(grad_full, down_back_w)
    down_grad = row_contract(active, grad_full)
    gate_grad_f, up_grad_f = active_back(active_grad)
    gate_grad = gate_grad_f.astype(jnp.bfloat16)
    up_grad = up_grad_f.astype(jnp.bfloat16)
    gate_weight_grad = row_contract(normed_two_full, gate_grad)
    up_weight_grad = row_contract(normed_two_full, up_grad)
    norm_two_grad = lax.psum_scatter(
        (project_back(gate_grad, gate_back_w) + project_back(up_grad, up_back_w)).astype(
            jnp.bfloat16
        ),
        "tensor",
        scatter_dimension=0,
        tiled=True,
    ).astype(jnp.float32)
    middle_back, gain_two_grad = norm_two_back(norm_two_grad)
    middle_grad = cotangent.astype(jnp.float32) + middle_back
    branch_full = lax.all_gather(middle_grad.astype(jnp.bfloat16), "tensor", axis=0, tiled=True)
    query_back_w, key_back_w, value_back_w, out_back_w = (
        lax.all_gather(w_query, "dp", axis=0, tiled=True),
        lax.all_gather(w_key, "dp", axis=0, tiled=True),
        lax.all_gather(w_value, "dp", axis=0, tiled=True),
        lax.all_gather(w_out, "dp", axis=0, tiled=True),
    )
    mixed_grad = project_back(branch_full, out_back_w).astype(jnp.bfloat16)
    out_grad = row_contract(mixed_heads, branch_full)
    query_turn_grad, key_turn_grad, value_grad_f = attend_back(
        queries, key_rows, value_rows, segment, log_totals, mixed_grad
    )
    query_grad = (
        rotary_back(query_turn_grad, cosine, sine_table)
        .reshape(group_rows, local_heads * HEAD_SIZE)
        .astype(jnp.bfloat16)
    )
    key_grad = (
        rotary_back(key_turn_grad, cosine, sine_table)
        .reshape(group_rows, local_groups * HEAD_SIZE)
        .astype(jnp.bfloat16)
    )
    value_grad = value_grad_f.reshape(group_rows, local_groups * HEAD_SIZE).astype(jnp.bfloat16)
    query_weight_grad = row_contract(normed_full, query_grad)
    key_weight_grad = row_contract(normed_full, key_grad)
    value_weight_grad = row_contract(normed_full, value_grad)
    norm_one_grad = lax.psum_scatter(
        (
            project_back(query_grad, query_back_w)
            + project_back(key_grad, key_back_w)
            + project_back(value_grad, value_back_w)
        ).astype(jnp.bfloat16),
        "tensor",
        scatter_dimension=0,
        tiled=True,
    ).astype(jnp.float32)
    residual_back, gain_one_grad = norm_one_back(norm_one_grad)
    input_grad = (middle_grad + residual_back).astype(jnp.bfloat16)
    summed = (
        lax.psum_scatter(
            gain_one_grad.astype(jnp.bfloat16), "dp", scatter_dimension=0, tiled=True
        ).astype(jnp.float32),
        lax.psum_scatter(
            query_weight_grad.astype(jnp.bfloat16), "dp", scatter_dimension=0, tiled=True
        ).astype(jnp.float32),
        lax.psum_scatter(
            key_weight_grad.astype(jnp.bfloat16), "dp", scatter_dimension=0, tiled=True
        ).astype(jnp.float32),
        lax.psum_scatter(
            value_weight_grad.astype(jnp.bfloat16), "dp", scatter_dimension=0, tiled=True
        ).astype(jnp.float32),
        lax.psum_scatter(
            out_grad.astype(jnp.bfloat16), "dp", scatter_dimension=0, tiled=True
        ).astype(jnp.float32),
        lax.psum_scatter(
            gain_two_grad.astype(jnp.bfloat16), "dp", scatter_dimension=0, tiled=True
        ).astype(jnp.float32),
        lax.psum_scatter(
            gate_weight_grad.astype(jnp.bfloat16), "dp", scatter_dimension=0, tiled=True
        ).astype(jnp.float32),
        lax.psum_scatter(
            up_weight_grad.astype(jnp.bfloat16), "dp", scatter_dimension=0, tiled=True
        ).astype(jnp.float32),
        lax.psum_scatter(
            down_grad.astype(jnp.bfloat16), "dp", scatter_dimension=0, tiled=True
        ).astype(jnp.float32),
    )
    gains_total = lax.psum((summed[0], summed[5]), "tensor")
    return (
        outputs,
        input_grad,
        gains_total[0],
        summed[1],
        summed[2],
        summed[3],
        summed[4],
        gains_total[1],
        summed[6],
        summed[7],
        summed[8],
    )


def solution(mesh):
    in_specs = (
        P(("dp", "tensor"), None),
        P(("dp", "tensor"), None),
        P("dp"),
        P("dp", "tensor"),
        P("dp", "tensor"),
        P("dp", "tensor"),
        P(("tensor", "dp"), None),
        P("dp"),
        P("dp", "tensor"),
        P("dp", "tensor"),
        P(("tensor", "dp"), None),
        P(),
        P(),
        P(),
    )
    out_specs = (
        P(("dp", "tensor"), None),
        P(("dp", "tensor"), None),
        P("dp"),
        P("dp", "tensor"),
        P("dp", "tensor"),
        P("dp", "tensor"),
        P(("tensor", "dp"), None),
        P("dp"),
        P("dp", "tensor"),
        P("dp", "tensor"),
        P(("tensor", "dp"), None),
    )
    return jax.shard_map(shards, mesh=mesh, in_specs=in_specs, out_specs=out_specs, check_vma=False)
```

profile of v0, /device:TPU:0, one launch (start us, length us, event | category | flops | bytes accessed | tf_op | source)
XLA Modules:
  0.0 1373.6 jit_solution(9857944345619936970)
XLA Ops:
  54.0 50.2 %all-gather.12.cloned.1.call-done = bf16[1024,2048]{1,0:T(8,128)(2,1)} async-done(((bf16[256,2048]{1,0:T(8,128)(2,1)}), bf16[1024,2048]{1,0:T(8,128)(2,1)}) %all-gather.12.cloned.1.call-update) | async-done | bytes 4194320 | tf_op jit(solution)/shard_map/all_gather | solution.py:208
  108.8 23.6 %all-gather.14.cloned.1.call-done = bf16[2048,512]{1,0:T(8,128)(2,1)} async-done(((bf16[256,512]{1,0:T(8,128)(2,1)}), bf16[2048,512]{1,0:T(8,128)(2,1)}) %all-gather.14.cloned.1.call-update) | async-done | bytes 2097168 | tf_op jit(solution)/shard_map/all_gather | solution.py:201
  205.5 67.4 %reduce-scatter.12.cloned.1.call-done = bf16[256,2048]{1,0:T(8,128)(2,1)} async-done(((bf16[1024,2048]{1,0:T(8,128)(2,1)}), bf16[256,2048]{1,0:T(8,128)(2,1)}) %reduce-scatter.12.cloned.1.call-update) | async-done | bytes 1048592 | tf_op jit(solution)/shard_map/reduce_scatter | solution.py:222
  279.4 50.0 %all-gather.22.cloned.1.call-done = bf16[2048,2048]{1,0:T(8,128)(2,1)} async-done(((bf16[256,2048]{1,0:T(8,128)(2,1)}), bf16[2048,2048]{1,0:T(8,128)(2,1)}) %all-gather.22.cloned.1.call-update) | async-done | bytes 8388624 | tf_op jit(solution)/shard_map/all_gather | solution.py:231
  329.4 82.8 %all-gather.18.cloned.1.call-done = bf16[1024,2048]{1,0:T(8,128)(2,1)} async-done(((bf16[256,2048]{1,0:T(8,128)(2,1)}), bf16[1024,2048]{1,0:T(8,128)(2,1)}) %all-gather.18.cloned.1.call-update) | async-done | bytes 4194320 | tf_op jit(solution)/shard_map/all_gather | solution.py:235
  412.2 14.9 %fusion.85 = f32[1024,2048]{1,0:T(8,128)} fusion(bf16[1024,2048]{1,0:T(8,128)(2,1)} %all-gather.18.cloned.1.call-done, bf16[2048,2048]{1,0:T(8,128)(2,1)} %all-gather.22.cloned.1.call-done), kind=kOutput, calls=%fused_computation.162 | convolution fusion | flops 8589934592 | bytes 20971520 | tf_op jit(solution)/shard_map/dot_general | solution.py:81
  427.1 39.8 %all-gather.20.cloned.1.call-done = bf16[2048,2048]{1,0:T(8,128)(2,1)} async-done(((bf16[256,2048]{1,0:T(8,128)(2,1)}), bf16[2048,2048]{1,0:T(8,128)(2,1)}) %all-gather.20.cloned.1.call-update) | async-done | bytes 8388624 | tf_op jit(solution)/shard_map/all_gather | solution.py:230
  466.8 14.4 %fusion.84 = f32[1024,2048]{1,0:T(8,128)} fusion(bf16[1024,2048]{1,0:T(8,128)(2,1)} %all-gather.18.cloned.1.call-done, bf16[2048,2048]{1,0:T(8,128)(2,1)} %all-gather.20.cloned.1.call-done), kind=kOutput, calls=%fused_computation.161 | convolution fusion | flops 8589934592 | bytes 20971520 | tf_op jit(solution)/shard_map/dot_general | solution.py:81
  481.3 67.9 %all-gather.26.cloned.1.call-done = bf16[1024,2048]{1,0:T(8,128)(2,1)} async-done(((bf16[256,2048]{1,0:T(8,128)(2,1)}), bf16[1024,2048]{1,0:T(8,128)(2,1)}) %all-gather.26.cloned.1.call-update) | async-done | bytes 4194320 | tf_op jit(solution)/shard_map/all_gather | solution.py:253
  549.2 54.7 %all-gather.24.cloned.1.call-done = bf16[2048,2048]{1,0:T(8,128)(2,1)} async-done(((bf16[256,2048]{1,0:T(8,128)(2,1)}), bf16[2048,2048]{1,0:T(8,128)(2,1)}) %all-gather.24.cloned.1.call-update) | async-done | bytes 8388624 | tf_op jit(solution)/shard_map/all_gather | solution.py:232
  603.9 21.7 %multiply_convert_fusion = (bf16[1024,2048]{1,0:T(8,128)(2,1)}, bf16[1024,2048]{1,0:T(8,128)(2,1)}, bf16[1024,2048]{1,0:T(8,128)(2,1)}) fusion(f32[1024,2048]{1,0:T(8,128)} %fusion.84, f32[1024,2048]{1,0:T(8,128)} %fusion.85, bf16[1024,2048]{1,0:T(8,128)(2,1)} %all-gather.26.cloned.1.call-done, bf16[2048,2048]{1,0:T(8,128)(2,1)} %all-gather.24.cloned.1.call-done), kind=kOutput, calls=%fused_computation.32 | convolution fusion | flops 8623489024 | bytes 41943040 | tf_op jit(solution)/shard_map/dot_general | solution.py:85
  625.6 12.9 fusion.86
  638.4 12.9 add_convert_fusion.1
  651.4 76.9 %reduce-scatter.16.cloned.1.call-done = bf16[256,2048]{1,0:T(8,128)(2,1)} async-done(((bf16[1024,2048]{1,0:T(8,128)(2,1)}), bf16[256,2048]{1,0:T(8,128)(2,1)}) %reduce-scatter.16.cloned.1.call-update) | async-done | bytes 1048592 | tf_op jit(solution)/shard_map/reduce_scatter | solution.py:266
  734.9 14.3 %convolution_convert_fusion.1 = bf16[2048,2048]{1,0:T(8,128)(2,1)} fusion(bf16[1024,2048]{1,0:T(8,128)(2,1)} %all-gather.18.cloned.1.call-done, bf16[1024,2048]{1,0:T(8,128)(2,1)} %get-tuple-element.25), kind=kOutput, calls=%fused_computation.39 | convolution fusion | flops 8594128896 | bytes 16777216 | tf_op jit(solution)/shard_map/dot_general | solution.py:91
  749.3 14.1 %convolution_convert_fusion.2 = bf16[2048,2048]{1,0:T(8,128)(2,1)} fusion(bf16[1024,2048]{1,0:T(8,128)(2,1)} %all-gather.18.cloned.1.call-done, bf16[1024,2048]{1,0:T(8,128)(2,1)} %get-tuple-element.26), kind=kOutput, calls=%fused_computation.40 | convolution fusion | flops 8594128896 | bytes 16777216 | tf_op jit(solution)/shard_map/dot_general | solution.py:91
  763.5 14.5 %convolution_convert_fusion = bf16[2048,2048]{1,0:T(8,128)(2,1)} fusion(bf16[1024,2048]{1,0:T(8,128)(2,1)} %get-tuple-element.27, bf16[1024,2048]{1,0:T(8,128)(2,1)} %all-gather.26.cloned.1.call-done), kind=kOutput, calls=%fused_computation.38 | convolution fusion | flops 8594128896 | bytes 16777216 | tf_op jit(solution)/shard_map/dot_general | solution.py:91
  778.8 37.5 %all-gather.28.cloned.1.call-done = bf16[1024,2048]{1,0:T(8,128)(2,1)} async-done(((bf16[256,2048]{1,0:T(8,128)(2,1)}), bf16[1024,2048]{1,0:T(8,128)(2,1)}) %all-gather.28.cloned.1.call-update) | async-done | bytes 4194320 | tf_op jit(solution)/shard_map/all_gather | solution.py:276
  821.9 12.7 fusion.44
  842.8 16.0 %fusion = (f32[2,4,512]{2,1,0:T(4,128)S(1)}, f32[2,1024,512,4]{2,1,3,0:T(8,128)}) fusion(f32[2,4,512,1024]{2,3,1,0:T(8,128)} %get-tuple-element.51, f32[2,4,512]{2,1,0:T(4,128)S(1)} %bitcast.185, bf16[1024,2,64,1]{0,2,3,1:T(8,128)(2,1)} %bitcast.173, bf16[512,2,4,64]{0,3,2,1:T(8,128)(2,1)} %bitcast.164), kind=kOutput, calls=%fused_computation.2 | convolution fusion | flops 549449728 | bytes 34373632 | tf_op jit(solution)/shard_map/qcgd,kcd->cgqk/dot_general | solution.py:154
  858.7 12.4 fusion.2
  884.8 12.1 fusion.5
  937.8 14.0 %convolution_convert_fusion.3 = bf16[1024,2048]{1,0:T(8,128)(2,1)} fusion(bf16[1024,2048]{1,0:T(8,128)(2,1)} %get-tuple-element.27, bf16[2048,2048]{1,0:T(8,128)(2,1)} %all-gather.24.cloned.1.call-done), kind=kOutput, calls=%fused_computation.46 | convolution fusion | flops 8592031744 | bytes 16777216 | tf_op jit(solution)/shard_map/dot_general | solution.py:81
  967.5 72.0 %reduce-scatter.32.cloned.1.call-done = bf16[256,2048]{1,0:T(8,128)(2,1)} async-done(((bf16[2048,2048]{1,0:T(8,128)(2,1)}), bf16[256,2048]{1,0:T(8,128)(2,1)}) %reduce-scatter.32.cloned.1.call-update) | async-done | bytes 1048592 | tf_op jit(solution)/shard_map/reduce_scatter | solution.py:339
  1042.3 34.3 %reduce-scatter.24.cloned.1.call-done = bf16[256,128]{1,0:T(8,128)(2,1)} async-done(((bf16[2048,128]{1,0:T(8,128)(2,1)}), bf16[256,128]{1,0:T(8,128)(2,1)}) %reduce-scatter.24.cloned.1.call-update) | async-done | bytes 65552 | tf_op jit(solution)/shard_map/reduce_scatter | solution.py:324
  1078.1 36.2 %reduce-scatter.22.cloned.1.call-done = bf16[256,128]{1,0:T(8,128)(2,1)} async-done(((bf16[2048,128]{1,0:T(8,128)(2,1)}), bf16[256,128]{1,0:T(8,128)(2,1)}) %reduce-scatter.22.cloned.1.call-update) | async-done | bytes 65552 | tf_op jit(solution)/shard_map/reduce_scatter | solution.py:321
  1115.8 42.8 %reduce-scatter.26.cloned.1.call-done = bf16[64,2048]{1,0:T(8,128)(2,1)} async-done(((bf16[512,2048]{1,0:T(8,128)(2,1)}), bf16[64,2048]{1,0:T(8,128)(2,1)}) %reduce-scatter.26.cloned.1.call-update) | async-done | bytes 262160 | tf_op jit(solution)/shard_map/reduce_scatter | solution.py:327
  1160.3 42.5 %reduce-scatter.20.cloned.1.call-done = bf16[256,512]{1,0:T(8,128)(2,1)} async-done(((bf16[2048,512]{1,0:T(8,128)(2,1)}), bf16[256,512]{1,0:T(8,128)(2,1)}) %reduce-scatter.20.cloned.1.call-update) | async-done | bytes 262160 | tf_op jit(solution)/shard_map/reduce_scatter | solution.py:318
  1204.6 77.3 %reduce-scatter.18.cloned.1.call-done = bf16[256,2048]{1,0:T(8,128)(2,1)} async-done(((bf16[1024,2048]{1,0:T(8,128)(2,1)}), bf16[256,2048]{1,0:T(8,128)(2,1)}) %reduce-scatter.18.cloned.1.call-update) | async-done | bytes 1048592 | tf_op jit(solution)/shard_map/reduce_scatter | solution.py:302
  1284.2 13.6 all-reduce.3
  1298.0 12.5 all-reduce.2
  1310.6 51.1 %reduce-scatter.14.cloned.1.call-done = bf16[256,2048]{1,0:T(8,128)(2,1)} async-done(((bf16[1024,2048]{1,0:T(8,128)(2,1)}), bf16[256,2048]{1,0:T(8,128)(2,1)}) %reduce-scatter.14.cloned.1.call-update) | async-done | bytes 1048592 | tf_op jit(solution)/shard_map/reduce_scatter | solution.py:246
  (280 shorter events, 233.6 us)
Async XLA Ops:
  7.2 97.0 %all-gather.12.cloned.1.call-start = ((), (), s32[]{:S(2)}) async-start(), calls=%async_computation.11 | async-start | bytes 5242880 | tf_op jit(solution)/shard_map/all_gather | solution.py:208
  23.1 109.4 %all-gather.14.cloned.1.call-start = ((), (), s32[]{:S(2)}) async-start(), calls=%async_computation.12 | async-start | bytes 2359296 | tf_op jit(solution)/shard_map/all_gather | solution.py:201
  23.8 165.1 %all-gather.16.cloned.1.call-start = ((), (), s32[]{:S(2)}) async-start(), calls=%async_computation.13 | async-start | bytes 2359296 | tf_op jit(solution)/shard_map/all_gather | solution.py:204
  24.5 248.3 %reduce-scatter.12.cloned.1.call-start = ((), (), s32[]{:S(2)}) async-start(), calls=%async_computation.14 | async-start | bytes 5242880 | tf_op jit(solution)/shard_map/reduce_scatter | solution.py:222
  195.9 133.5 %all-gather.22.cloned.1.call-start = ((), (), s32[]{:S(2)}) async-start(), calls=%async_computation.17 | async-start | bytes 9437184 | tf_op jit(solution)/shard_map/all_gather | solution.py:231
  196.5 215.7 %all-gather.18.cloned.1.call-start = ((), (), s32[]{:S(2)}) async-start(), calls=%async_computation.15 | async-start | bytes 5242880 | tf_op jit(solution)/shard_map/all_gather | solution.py:235
  205.5 525.6 %copy-start.37 = (f32[8,1,256]{2,1,0:T(1,128)}, f32[8,1,256]{2,1,0:T(1,128)S(1)}, u32[]{:S(2)}) copy-start(f32[8,1,256]{2,1,0:T(1,128)S(1)} %convert_element_type.254) | copy-start | bytes 24580
  274.5 456.6 %copy-start.51 = (f32[256]{0:T(256)}, f32[256]{0:T(256)S(1)}, u32[]{:S(2)}) copy-start(f32[256]{0:T(256)S(1)} %fusion.67) | copy-start | bytes 3076
  277.1 189.7 %all-gather.20.cloned.1.call-start = ((), (), s32[]{:S(2)}) async-start(), calls=%async_computation.16 | async-start | bytes 9437184 | tf_op jit(solution)/shard_map/all_gather | solution.py:230
  277.9 271.3 %all-gather.26.cloned.1.call-start = ((), (), s32[]{:S(2)}) async-start(), calls=%async_computation.20 | async-start | bytes 5242880 | tf_op jit(solution)/shard_map/all_gather | solution.py:253
  278.7 325.2 %all-gather.24.cloned.1.call-start = ((), (), s32[]{:S(2)}) async-start(), calls=%async_computation.18 | async-start | bytes 9437184 | tf_op jit(solution)/shard_map/all_gather | solution.py:232
  279.4 448.9 %reduce-scatter.16.cloned.1.call-start = ((), (), s32[]{:S(2)}) async-start(), calls=%async_computation.21 | async-start | bytes 5242880 | tf_op jit(solution)/shard_map/reduce_scatter | solution.py:266
  651.4 164.9 %all-gather.28.cloned.1.call-start = ((), (), s32[]{:S(2)}) async-start(), calls=%async_computation.22 | async-start | bytes 5242880 | tf_op jit(solution)/shard_map/all_gather | solution.py:276
  734.9 218.8 %reduce-scatter.30.cloned.1.call-start = ((), (), s32[]{:S(2)}) async-start(), calls=%async_computation.29 | async-start | bytes 9437184 | tf_op jit(solution)/shard_map/reduce_scatter | solution.py:336
  749.3 215.4 %reduce-scatter.28.cloned.1.call-start = ((), (), s32[]{:S(2)}) async-start(), calls=%async_computation.28 | async-start | bytes 9437184 | tf_op jit(solution)/shard_map/reduce_scatter | solution.py:333
  763.5 276.0 %reduce-scatter.32.cloned.1.call-start = ((), (), s32[]{:S(2)}) async-start(), calls=%async_computation.30 | async-start | bytes 9437184 | tf_op jit(solution)/shard_map/reduce_scatter | solution.py:339
  778.1 298.5 %reduce-scatter.24.cloned.1.call-start = ((), (), s32[]{:S(2)}) async-start(), calls=%async_computation.26 | async-start | bytes 589824 | tf_op jit(solution)/shard_map/reduce_scatter | solution.py:324
  884.8 229.5 %reduce-scatter.22.cloned.1.call-start = ((), (), s32[]{:S(2)}) async-start(), calls=%async_computation.25 | async-start | bytes 589824 | tf_op jit(solution)/shard_map/reduce_scatter | solution.py:321
  904.8 253.8 %reduce-scatter.26.cloned.1.call-start = ((), (), s32[]{:S(2)}) async-start(), calls=%async_computation.27 | async-start | bytes 2359296 | tf_op jit(solution)/shard_map/reduce_scatter | solution.py:327
  911.5 291.3 %reduce-scatter.20.cloned.1.call-start = ((), (), s32[]{:S(2)}) async-start(), calls=%async_computation.24 | async-start | bytes 2359296 | tf_op jit(solution)/shard_map/reduce_scatter | solution.py:318
  930.0 351.9 %reduce-scatter.18.cloned.1.call-start = ((), (), s32[]{:S(2)}) async-start(), calls=%async_computation.23 | async-start | bytes 5242880 | tf_op jit(solution)/shard_map/reduce_scatter | solution.py:302
  937.8 423.9 %reduce-scatter.14.cloned.1.call-start = ((), (), s32[]{:S(2)}) async-start(), calls=%async_computation.19 | async-start | bytes 5242880 | tf_op jit(solution)/shard_map/reduce_scatter | solution.py:246
  956.5 325.4 %copy-start.3 = (bf16[256,2048]{1,0:T(8,128)(2,1)S(1)}, bf16[256,2048]{1,0:T(8,128)(2,1)}, u32[]{:S(2)}) copy-start(bf16[256,2048]{1,0:T(8,128)(2,1)} %param.14) | copy-start | bytes 3145732
  956.5 325.4 %copy-start.44 = (f32[8,1,256]{2,1,0:T(1,128)S(1)}, f32[8,1,256]{2,1,0:T(1,128)}, u32[]{:S(2)}) copy-start(f32[8,1,256]{2,1,0:T(1,128)} %copy-done.43) | copy-start | bytes 24580
  956.5 325.4 %copy-start.55 = (f32[256]{0:T(256)S(1)}, f32[256]{0:T(256)}, u32[]{:S(2)}) copy-start(f32[256]{0:T(256)} %copy-done.54) | copy-start | bytes 3076
  967.4 316.8 %copy-start.53 = (bf16[2048]{0:T(1024)(128)(2,1)S(1)}, bf16[2048]{0:T(1024)(128)(2,1)}, u32[]{:S(2)}) copy-start(bf16[2048]{0:T(1024)(128)(2,1)} %get-tuple-element.11) | copy-start | bytes 12292
  967.4 343.1 %copy-start.57 = (f32[256]{0:T(256)S(1)}, f32[256]{0:T(256)}, u32[]{:S(2)}) copy-start(f32[256]{0:T(256)} %copy-done.56) | copy-start | bytes 3076
  967.4 394.2 %copy-start.5 = (bf16[256,2048]{1,0:T(8,128)(2,1)S(1)}, bf16[256,2048]{1,0:T(8,128)(2,1)}, u32[]{:S(2)}) copy-start(bf16[256,2048]{1,0:T(8,128)(2,1)} %reduce-scatter.12.cloned.1.call-done) | copy-start | bytes 3145732
  967.4 394.2 %copy-start.11 = (bf16[256,2048]{1,0:T(8,128)(2,1)S(1)}, bf16[256,2048]{1,0:T(8,128)(2,1)}, u32[]{:S(2)}) copy-start(bf16[256,2048]{1,0:T(8,128)(2,1)} %param.15) | copy-start | bytes 3145732
  967.5 394.2 %copy-start.38 = (f32[8,1,256]{2,1,0:T(1,128)S(1)}, f32[8,1,256]{2,1,0:T(1,128)}, u32[]{:S(2)}) copy-start(f32[8,1,256]{2,1,0:T(1,128)} %copy-done.37) | copy-start | bytes 24580
  967.5 394.2 %copy-start.52 = (f32[256]{0:T(256)S(1)}, f32[256]{0:T(256)}, u32[]{:S(2)}) copy-start(f32[256]{0:T(256)} %copy-done.51) | copy-start | bytes 3076
  967.5 394.2 %copy-start.59 = (f32[256]{0:T(256)S(1)}, f32[256]{0:T(256)}, u32[]{:S(2)}) copy-start(f32[256]{0:T(256)} %copy-done.58) | copy-start | bytes 3076
  (64 other events, 1162.5 us)
Sparse Core Ops, SparseCore 0:
  23.2 81.0 all-gather.11
  106.1 26.2 all-gather.13
  134.3 27.7 all-gather.15
  196.0 76.7 reduce-scatter.11
  274.6 54.7 all-gather.21
  331.4 80.7 all-gather.17
  414.1 52.7 all-gather.19
  468.4 80.7 all-gather.25
  551.1 52.7 all-gather.23
  651.5 76.7 reduce-scatter.15
  735.0 81.2 all-gather.27
  819.6 69.9 reduce-scatter.29
  893.1 71.4 reduce-scatter.27
  968.0 71.5 reduce-scatter.31
  1042.4 34.1 reduce-scatter.23
  1080.1 34.1 reduce-scatter.21
  1117.4 41.0 reduce-scatter.25
  1161.7 41.1 reduce-scatter.19
  1205.1 76.7 reduce-scatter.17
  1284.1 77.5 reduce-scatter.13
where the time goes:
time: 1380 us; the launch traced here: 1370 us
  waiting for transfers between devices  919 us (67%)
  matrix products  265 us (19%)
  other arithmetic  88.7 us (6%)
  blocking collectives  64.1 us (5%)
  between operations  20.1 us (1%)
  local copies, waits for them, and re-layouts  15.8 us (1%)
    all_gather x1, waiting for transfers between devices, shards(): lax.all_gather(normed_two_f.astype(jnp.bfloat16), 'tensor', axis=0, tiled...  82.8 us
    reduce_scatter x1, waiting for transfers between devices, shards(): lax.psum_scatter((project_back(query_grad, query_back_w) + project_back(k...  77.3 us
    reduce_scatter x1, waiting for transfers between devices, shards(): lax.psum_scatter((project_back(gate_grad, gate_back_w) + project_back(up_...  76.9 us
    reduce_scatter x1, waiting for transfers between devices, shards(): lax.psum_scatter(down_grad.astype(jnp.bfloat16), 'dp', scatter_dimension=...  72 us
    all_gather x1, waiting for transfers between devices, shards(): grad_full = lax.all_gather(cotangent, 'tensor', axis=0, tiled=True)  67.9 us
    reduce_scatter x1, waiting for transfers between devices, shards(): lax.psum_scatter(project(mixed_heads, out_full).astype(jnp.bfloat16), 'te...  67.4 us
    dot_general x7, matrix products, project(): return jnp.dot(left, right, preferred_element_type=jnp.float32)  59.8 us
    dot_general x7, matrix products, project_back(): lax.dot_general(left, right, (((1,), (1,)), ((), ())), preferred_element_...  59.1 us
  transfers between devices with their start and end apart: 20, of which 18 were waited for; matrix products, arithmetic and copies ran while one was open for 21% of the time, Pallas kernels for 0%

commit v1 on v0

v1 whole, which is shorter than its diff:
```python
import functools
import math

import jax
import jax.numpy as jnp
from jax import lax
from jax.experimental import pallas as pl
from jax.experimental.pallas import tpu as pltpu
from jax.sharding import PartitionSpec as P

HEAD_SIZE = 64
MOST_SEQS = 2
SLAB = 128
SPAN = 256

norm_epsilon = 1e-05
rope_theta = 500000.0
rope_factor = 32.0
low_factor = 1.0
high_factor = 4.0
context_span = 8192.0
mask_fill = -1e30

F32 = jnp.float32
BF16 = jnp.bfloat16
VMEM_LIMIT = 60 * 1024 * 1024


def rotary_freqs(head_size):
    exponents = jnp.arange(0, head_size, 2).astype(jnp.float32) / head_size
    inverse = 1.0 / jnp.power(jnp.float32(rope_theta), exponents)
    wavelength = 2.0 * math.pi / inverse
    smooth = (context_span / wavelength - low_factor) / (high_factor - low_factor)
    blended = (1.0 - smooth) * inverse / rope_factor + smooth * inverse
    scaled = jnp.where(wavelength > context_span / low_factor, inverse / rope_factor, blended)
    return jnp.where(wavelength < context_span / high_factor, inverse, scaled)


def slab_tables(positions):
    freqs = rotary_freqs(HEAD_SIZE)
    freqs = jnp.concatenate([freqs] * 4)
    angles = positions.astype(jnp.float32)[:, None] * freqs[None, :]
    low_half = (jnp.arange(SLAB) % HEAD_SIZE) < HEAD_SIZE // 2
    sines = jnp.sin(angles)
    return jnp.cos(angles), jnp.where(low_half[None, :], -sines, sines)


def group_layout(seq_lengths, group_perm, group_starts, group_id, row_total, slot_total):
    bounds = jnp.arange(group_starts.shape[0], dtype=jnp.int32)
    numbers = jnp.arange(group_perm.shape[0], dtype=jnp.int32)
    opening = jnp.sum(jnp.where(bounds == group_id, group_starts, 0))
    closing = jnp.sum(jnp.where(bounds == group_id + 1, group_starts, 0))
    row_ids = jnp.arange(row_total, dtype=jnp.int32)
    offset = jnp.zeros((row_total,), jnp.int32)
    finish = jnp.zeros((), jnp.int32)
    for slot_id in range(slot_total):
        slot_place = opening + slot_id
        sequence = jnp.sum(jnp.where(numbers == slot_place, group_perm, 0))
        length = jnp.sum(jnp.where(numbers == sequence, seq_lengths, 0))
        length = jnp.where(slot_place < closing, length, 0)
        finish = finish + length
        offset = jnp.where(row_ids >= finish, finish, offset)
    return offset, row_ids - offset


def project(left, right):
    return jnp.dot(left, right, preferred_element_type=F32)


def project_back(left, right):
    return lax.dot_general(left, right, (((1,), (1,)), ((), ())), preferred_element_type=F32)


def row_contract(left, right):
    return lax.dot_general(left, right, (((0,), (0,)), ((), ())), preferred_element_type=F32)


def lanes(shape):
    return lax.broadcasted_iota(jnp.int32, shape, len(shape) - 1)


def turned(slab):
    half = HEAD_SIZE // 2
    ahead = pltpu.roll(slab, SLAB - half, 1)
    behind = pltpu.roll(slab, half, 1)
    return jnp.where(lanes(slab.shape) % HEAD_SIZE < half, ahead, behind)


def head_pair(slab):
    left = lanes(slab.shape) < HEAD_SIZE
    zero = jnp.zeros_like(slab)
    return jnp.concatenate([jnp.where(left, slab, zero), jnp.where(left, zero, slab)], axis=0)


def join_pair(stacked):
    half = stacked.shape[0] // 2
    left = lanes((half, SLAB)) < HEAD_SIZE
    return jnp.where(left, stacked[:half], stacked[half:])


def params(**kwargs):
    return pltpu.CompilerParams(vmem_limit_bytes=VMEM_LIMIT, **kwargs)


def vmem_specs(count):
    return [pl.BlockSpec(memory_space=pltpu.VMEM)] * count


def attend_kernel(
    x_ref, w_ref, gain_ref, cos_ref, sin_ref, start_ref,
    normed_ref, q_ref, k_ref, v_ref, mixed_ref, lse_ref, bias_ref, stat_ref,
):
    rows_all = x_ref.shape[0]
    q_width = q_ref.shape[1]
    kv_slabs = v_ref.shape[0] // 2
    slabs = q_width // SLAB
    scale = HEAD_SIZE ** (-0.5)

    @pl.loop(0, rows_all // SPAN)
    def _(step):
        rows = pl.ds(step * SPAN, SPAN)
        x = x_ref[rows, :].astype(F32)
        inverse = lax.rsqrt(jnp.mean(x * x, axis=-1, keepdims=True) + norm_epsilon)
        normed = (x * inverse * gain_ref[...]).astype(BF16)
        normed_ref[rows, :] = normed
        pre = project(normed, w_ref[:, : q_width + 2 * kv_slabs * SLAB])
        cosine, sine = cos_ref[rows, :], sin_ref[rows, :]
        for slab in range(slabs):
            part = pre[:, slab * SLAB : (slab + 1) * SLAB]
            part = (part * cosine + turned(part) * sine).astype(BF16)
            q_ref[rows, slab * SLAB : (slab + 1) * SLAB] = (part.astype(F32) * scale).astype(BF16)
        left = lanes((SPAN, SLAB)) < HEAD_SIZE
        for pair in range(kv_slabs):
            at = q_width + pair * SLAB
            key = pre[:, at : at + SLAB]
            key = key * cosine + turned(key) * sine
            at = at + kv_slabs * SLAB
            value = pre[:, at : at + SLAB]
            for ref, full in ((k_ref, key), (v_ref, value)):
                other = pltpu.roll(full, HEAD_SIZE, 1)
                ref[2 * pair, rows, :] = jnp.where(left, full, other).astype(BF16)
                ref[2 * pair + 1, rows, :] = jnp.where(left, other, full).astype(BF16)

    members = slabs // (2 * kv_slabs)
    for tile in range(rows_all // SPAN):
        first, span = tile * SPAN, (tile + 1) * SPAN
        columns = lanes((SPAN, span))
        row_ids = first + lax.broadcasted_iota(jnp.int32, (SPAN, span), 0)
        allowed = (columns >= start_ref[first : first + SPAN, :]) & (columns <= row_ids)
        bias_ref[:, :span] = jnp.where(allowed, 0.0, mask_fill)

        @pl.loop(0, slabs)
        def _(slab):
            at = pl.ds(pl.multiple_of(slab * SLAB, SLAB), SLAB)
            head = slab // members
            stacked = head_pair(q_ref[first : first + SPAN, at])
            scores = project_back(stacked, k_ref[head, :span, :])
            bias = bias_ref[:, :span]
            scores = scores + jnp.concatenate([bias, bias], axis=0)
            top = jnp.max(scores, axis=-1, keepdims=True)
            weights = jnp.exp(scores - top)
            total = jnp.sum(weights, axis=-1, keepdims=True)
            mixed = project(weights.astype(BF16), v_ref[head, :span, :]) / total
            mixed_ref[first : first + SPAN, at] = join_pair(mixed).astype(BF16)
            logs = top + jnp.log(total)
            old = stat_ref[first : first + SPAN, :]
            lane = lanes(old.shape)
            old = jnp.where(lane == 2 * slab, logs[:SPAN], old)
            stat_ref[first : first + SPAN, :] = jnp.where(lane == 2 * slab + 1, logs[SPAN:], old)

    lse_ref[...] = jnp.transpose(stat_ref[...])[: lse_ref.shape[0], :]


def attend(x_full, w_qkv, gain, cosine, sine, start, q_width, kv_width):
    rows = x_full.shape[0]
    heads = 2 * (kv_width // SLAB)
    flops = 2 * rows * x_full.shape[1] * (q_width + 2 * kv_width) + 8 * rows * rows * q_width
    return pl.pallas_call(
        attend_kernel,
        out_shape=(
            jax.ShapeDtypeStruct(x_full.shape, BF16),
            jax.ShapeDtypeStruct((rows, q_width), BF16),
            jax.ShapeDtypeStruct((heads, rows, SLAB), BF16),
            jax.ShapeDtypeStruct((heads, rows, SLAB), BF16),
            jax.ShapeDtypeStruct((rows, q_width), BF16),
            jax.ShapeDtypeStruct((q_width // HEAD_SIZE, rows), F32),
        ),
        in_specs=vmem_specs(6),
        out_specs=tuple(vmem_specs(6)),
        scratch_shapes=[pltpu.VMEM((SPAN, rows), F32), pltpu.VMEM((rows, SLAB), F32)],
        compiler_params=params(),
        cost_estimate=pl.CostEstimate(flops=flops, bytes_accessed=1 << 24, transcendentals=1 << 23),
        name="attend",
    )(x_full, w_qkv, gain, cosine, sine, start)


def attend_back_kernel(
    branch_ref, w_ref, q_ref, k_ref, v_ref, lse_ref, cos_ref, sin_ref, start_ref,
    dqkv_ref, dmix_ref, bias_ref, dq_ref, dk_ref, dv_ref,
):
    rows_all = branch_ref.shape[0]
    q_width = q_ref.shape[1]
    slabs = q_width // SLAB
    kv_heads = k_ref.shape[0]
    members = slabs // kv_heads
    scale = HEAD_SIZE ** (-0.5)

    @pl.loop(0, rows_all // SPAN)
    def _(step):
        rows = pl.ds(step * SPAN, SPAN)
        dmix_ref[rows, :] = project_back(branch_ref[rows, :], w_ref[...]).astype(BF16)

    dk_ref[...] = jnp.zeros_like(dk_ref)
    dv_ref[...] = jnp.zeros_like(dv_ref)
    for tile in range(rows_all // SPAN):
        first, span = tile * SPAN, (tile + 1) * SPAN
        key_ids = lax.broadcasted_iota(jnp.int32, (span, SPAN), 0)
        row_ids = first + lanes((span, SPAN))
        allowed = (key_ids >= start_ref[:, first : first + SPAN]) & (key_ids <= row_ids)
        bias_ref[:span, :] = jnp.where(allowed, 0.0, mask_fill)

        @pl.loop(0, slabs)
        def _(slab):
            at = pl.ds(pl.multiple_of(slab * SLAB, SLAB), SLAB)
            head = slab // members
            queries = head_pair(q_ref[first : first + SPAN, at])
            grads = head_pair(dmix_ref[first : first + SPAN, at])
            keys = k_ref[head, :span, :]
            scores = project_back(keys, queries)
            bias = bias_ref[:span, :]
            logs = jnp.concatenate(
                [
                    lse_ref[pl.ds(2 * slab, 1), first : first + SPAN],
                    lse_ref[pl.ds(2 * slab + 1, 1), first : first + SPAN],
                ],
                axis=1,
            )
            chances = jnp.exp(scores + jnp.concatenate([bias, bias], axis=1) - logs)
            chances_grad = project_back(v_ref[head, :span, :], grads)
            shared = jnp.sum(chances * chances_grad, axis=0, keepdims=True)
            score_grad = (chances * (chances_grad - shared)).astype(BF16)
            dv_ref[head, :span, :] += project(chances.astype(BF16), grads)
            dk_ref[head, :span, :] += project(score_grad, queries)
            dq_ref[first : first + SPAN, at] = join_pair(row_contract(score_grad, keys)) * scale

    left = lanes((SPAN, SLAB)) < HEAD_SIZE

    @pl.loop(0, rows_all // SPAN)
    def _(step):
        rows = pl.ds(step * SPAN, SPAN)
        cosine, sine = cos_ref[rows, :], sin_ref[rows, :]
        for slab in range(slabs):
            part = dq_ref[rows, slab * SLAB : (slab + 1) * SLAB]
            part = part * cosine - turned(part) * sine
            dqkv_ref[rows, slab * SLAB : (slab + 1) * SLAB] = part.astype(BF16)
        for pair in range(kv_heads // 2):
            joined = []
            for ref in (dk_ref, dv_ref):
                sums = []
                for head in (2 * pair, 2 * pair + 1):
                    full = ref[head, rows, :]
                    sums.append(full + pltpu.roll(full, HEAD_SIZE, 1))
                joined.append(jnp.where(left, sums[0], sums[1]))
            key, value = joined
            key = key * cosine - turned(key) * sine
            at = q_width + pair * SLAB
            dqkv_ref[rows, at : at + SLAB] = key.astype(BF16)
            at = at + (kv_heads // 2) * SLAB
            dqkv_ref[rows, at : at + SLAB] = value.astype(BF16)


def attend_back(branch_full, w_out, queries, keys, values, lse, cosine, sine, start):
    rows, q_width = queries.shape
    kv_heads = keys.shape[0]
    width = q_width + kv_heads * SLAB
    flops = 2 * rows * branch_full.shape[1] * q_width + 20 * rows * rows * q_width
    return pl.pallas_call(
        attend_back_kernel,
        out_shape=jax.ShapeDtypeStruct((rows, width), BF16),
        in_specs=vmem_specs(9),
        out_specs=vmem_specs(1)[0],
        scratch_shapes=[
            pltpu.VMEM((rows, q_width), BF16),
            pltpu.VMEM((rows, SPAN), F32),
            pltpu.VMEM((rows, q_width), F32),
            pltpu.VMEM((kv_heads, rows, SLAB), F32),
            pltpu.VMEM((kv_heads, rows, SLAB), F32),
        ],
        compiler_params=params(),
        cost_estimate=pl.CostEstimate(flops=flops, bytes_accessed=1 << 24, transcendentals=1 << 23),
        name="attend_back",
    )(branch_full, w_out, queries, keys, values, lse, cosine, sine, start)


class Line:
    def __init__(self, count):
        self.count = count
        self.place = lax.axis_index("tensor")
        self.has = (self.place < count - 1, self.place > 0)
        self.neighbour = (self.place + 1, self.place - 1)

    def barrier(self):
        semaphore = pltpu.get_barrier_semaphore()
        for way in (0, 1):
            @pl.when(self.has[way])
            def _(way=way):
                pl.semaphore_signal(semaphore, 1, device_id={"tensor": self.neighbour[way]})
        ends = (self.place == 0) | (self.place == self.count - 1)
        pl.semaphore_wait(semaphore, jnp.where(ends, 1, 2))

    def copy(self, source, target, send, receive, way):
        return pltpu.make_async_remote_copy(
            src_ref=source, dst_ref=target, send_sem=send, recv_sem=receive,
            device_id={"tensor": self.neighbour[way]},
        )


class Gather:
    def __init__(self, line, full, send, receive, chunk_rows, pieces):
        self.line, self.full, self.send, self.receive = line, full, send, receive
        self.chunk_rows, self.size = chunk_rows, chunk_rows // pieces

    def rows(self, chunk, piece):
        start = chunk * self.chunk_rows + piece * self.size
        return pl.ds(pl.multiple_of(start, self.size), self.size)

    def copy(self, chunk, piece, way, source=None):
        target = self.full.at[self.rows(chunk, piece)]
        return self.line.copy(
            target if source is None else source, target,
            self.send.at[way, chunk, piece], self.receive.at[way, chunk, piece], way,
        )

    def start(self, piece, source=None):
        for way in (0, 1):
            @pl.when(self.line.has[way])
            def _(way=way):
                self.copy(self.line.place, piece, way, source).start()

    def pass_on(self, piece, hops=None):
        line = self.line
        for hop in hops or range(1, line.count):
            for way, chunk in ((0, line.place - hop), (1, line.place + hop)):
                @pl.when((chunk >= 0) & (chunk < line.count))
                def _(way=way, chunk=chunk):
                    self.copy(chunk, piece, way).wait_recv()

                    @pl.when(line.has[way])
                    def _():
                        self.copy(chunk, piece, way).start()

    def finish(self, pieces, source=None):
        line = self.line
        for chunk in range(line.count):
            for piece in range(pieces):
                @pl.when(line.has[0] & (chunk <= line.place))
                def _():
                    self.copy(chunk, piece, 0, source).wait_send()

                @pl.when(line.has[1] & (chunk >= line.place))
                def _():
                    self.copy(chunk, piece, 1, source).wait_send()


class Scatter:
    def __init__(self, line, partial, landing, send, receive, chunk_rows, pieces):
        self.line, self.partial, self.landing = line, partial, landing
        self.send, self.receive = send, receive
        self.chunk_rows, self.size = chunk_rows, chunk_rows // pieces

    def rows(self, chunk, piece):
        start = chunk * self.chunk_rows + piece * self.size
        return pl.ds(pl.multiple_of(start, self.size), self.size)

    def copy(self, chunk, piece, way):
        rows = self.rows(chunk, piece)
        return self.line.copy(
            self.partial.at[rows], self.landing.at[way, rows],
            self.send.at[way, chunk, piece], self.receive.at[way, chunk, piece], way,
        )

    def step(self, piece):
        line = self.line
        for turn in range(line.count - 1):
            for way, chunk in ((0, line.count - 1 - turn), (1, turn)):
                beyond = chunk > line.place if way == 0 else chunk < line.place

                @pl.when(beyond)
                def _(way=way, chunk=chunk):
                    @pl.when(line.has[1 - way])
                    def _():
                        self.copy(chunk, piece, way).wait_recv()
                        rows = self.rows(chunk, piece)
                        total = self.partial[rows, :].astype(F32)
                        total = total + self.landing[way, rows, :].astype(F32)
                        self.partial[rows, :] = total.astype(BF16)

                    self.copy(chunk, piece, way).start()

    def arrived(self, piece):
        for way in (0, 1):
            @pl.when(self.line.has[1 - way])
            def _(way=way):
                self.copy(self.line.place, piece, way).wait_recv()

    def total(self, piece, part=None):
        rows = self.rows(self.line.place, piece) if part is None else part
        total = self.partial[rows, :].astype(F32)
        for way in (0, 1):
            got = self.landing[way, rows, :].astype(F32)
            total = total + jnp.where(self.line.has[1 - way], got, 0.0)
        return total

    def finish(self, pieces):
        line = self.line
        for chunk in range(line.count):
            for piece in range(pieces):
                @pl.when(chunk > line.place)
                def _():
                    self.copy(chunk, piece, 0).wait_send()

                @pl.when(chunk < line.place)
                def _():
                    self.copy(chunk, piece, 1).wait_send()


def copy_sems(count, pieces):
    return pltpu.SemaphoreType.DMA((2, count, pieces))


def gather_kernel(count, pieces, x_ref, full_ref, send, receive, local):
    line = Line(count)
    own = pl.ds(pl.multiple_of(line.place * x_ref.shape[0], x_ref.shape[0]), x_ref.shape[0])
    keep = pltpu.make_async_copy(x_ref, full_ref.at[own], local)
    keep.start()
    line.barrier()
    gather = Gather(line, full_ref, send, receive, x_ref.shape[0], pieces)
    for piece in range(pieces):
        gather.start(piece, x_ref.at[gather.rows(0, piece)])
    for hop in range(1, count):
        for piece in range(pieces):
            gather.pass_on(piece, (hop,))
    gather.finish(pieces)
    keep.wait()


def line_gather(x, count, collective_id, pieces=4):
    rows, width = x.shape
    return pl.pallas_call(
        functools.partial(gather_kernel, count, pieces),
        out_shape=jax.ShapeDtypeStruct((count * rows, width), x.dtype),
        in_specs=vmem_specs(1),
        out_specs=pl.BlockSpec(memory_space=pl.ANY),
        scratch_shapes=[
            copy_sems(count, pieces), copy_sems(count, pieces), pltpu.SemaphoreType.DMA
        ],
        compiler_params=params(collective_id=collective_id, has_side_effects=True),
        cost_estimate=pl.CostEstimate(
            flops=0, bytes_accessed=200 * rows * width, transcendentals=0
        ),
        name="line_gather",
    )(x)


def forward_turn_kernel(
    count, pieces, mixed_ref, w_ref, x_ref, gain_ref, middle_ref, full_ref,
    partial, landing, rs_send, rs_receive, ag_send, ag_receive,
):
    line = Line(count)
    chunk_rows = x_ref.shape[0]
    line.barrier()

    @pl.loop(0, partial.shape[0] // SPAN)
    def _(step):
        rows = pl.ds(step * SPAN, SPAN)
        partial[rows, :] = project(mixed_ref[rows, :], w_ref[...]).astype(BF16)

    scatter = Scatter(line, partial, landing, rs_send, rs_receive, chunk_rows, pieces)
    gather = Gather(line, full_ref, ag_send, ag_receive, chunk_rows, pieces)
    size = chunk_rows // pieces

    def settle(piece):
        scatter.arrived(piece)
        local = pl.ds(piece * size, size)
        middle = x_ref[local, :].astype(F32) + scatter.total(piece)
        middle_ref[local, :] = middle
        inverse = lax.rsqrt(jnp.mean(middle * middle, axis=-1, keepdims=True) + norm_epsilon)
        full_ref[gather.rows(line.place, piece), :] = (
            middle * inverse * gain_ref[...]
        ).astype(BF16)
        gather.start(piece)

    pipeline(pieces, scatter.step, settle, gather.pass_on)
    scatter.finish(pieces)
    gather.finish(pieces)


def pipeline(pieces, scatter_step, settle, pass_on):
    for turn in range(pieces + 2):
        if turn < pieces:
            scatter_step(turn)
        if 1 <= turn <= pieces:
            settle(turn - 1)
        if turn >= 2:
            pass_on(turn - 2)


def forward_turn(mixed, w_out, x, gain, count, collective_id, pieces=4):
    chunk_rows, width = x.shape
    rows = count * chunk_rows
    return pl.pallas_call(
        functools.partial(forward_turn_kernel, count, pieces),
        out_shape=(
            jax.ShapeDtypeStruct((chunk_rows, width), F32),
            jax.ShapeDtypeStruct((rows, width), BF16),
        ),
        in_specs=vmem_specs(4),
        out_specs=tuple(vmem_specs(2)),
        scratch_shapes=[
            pltpu.VMEM((rows, width), BF16),
            pltpu.VMEM((2, rows, width), BF16),
        ]
        + [copy_sems(count, pieces)] * 4,
        compiler_params=params(collective_id=collective_id, has_side_effects=True),
        cost_estimate=pl.CostEstimate(
            flops=2 * rows * width * mixed.shape[1],
            bytes_accessed=300 * chunk_rows * width, transcendentals=0,
        ),
        name="forward_turn",
    )(mixed, w_out, x, gain)


def backward_turn_kernel(
    count, pieces, given_ref, dy_ref, middle_ref, gain_ref,
    grad_ref, full_ref, gain_grad_ref,
    partial, landing, rs_send, rs_receive, ag_send, ag_receive, load,
):
    line = Line(count)
    chunk_rows = dy_ref.shape[0]
    fetch = pltpu.make_async_copy(given_ref, partial, load)
    fetch.start()
    line.barrier()
    fetch.wait()
    scatter = Scatter(line, partial, landing, rs_send, rs_receive, chunk_rows, pieces)
    gather = Gather(line, full_ref, ag_send, ag_receive, chunk_rows, pieces)
    size = chunk_rows // pieces
    gain_grad_ref[...] = jnp.zeros_like(gain_grad_ref)

    def settle(piece):
        scatter.arrived(piece)
        local = pl.ds(piece * size, size)
        total = scatter.total(piece)
        middle = middle_ref[local, :]
        grad, gain_grad = norm_back(total, middle, gain_ref[...])
        grad = grad + dy_ref[local, :].astype(F32)
        gain_grad_ref[...] += gain_grad
        grad_ref[local, :] = grad
        full_ref[gather.rows(line.place, piece), :] = grad.astype(BF16)
        gather.start(piece)

    pipeline(pieces, scatter.step, settle, gather.pass_on)
    scatter.finish(pieces)
    gather.finish(pieces)


def norm_back(grad, rows, gain):
    inverse = lax.rsqrt(jnp.mean(rows * rows, axis=-1, keepdims=True) + norm_epsilon)
    scaled = grad * gain
    common = jnp.mean(scaled * rows, axis=-1, keepdims=True) * (inverse * inverse * inverse)
    gain_grad = jnp.sum(grad * (rows * inverse), axis=0, keepdims=True)
    return inverse * scaled - rows * common, gain_grad


def backward_turn(given, dy, middle, gain, count, collective_id, pieces=4):
    chunk_rows, width = dy.shape
    rows = count * chunk_rows
    return pl.pallas_call(
        functools.partial(backward_turn_kernel, count, pieces),
        out_shape=(
            jax.ShapeDtypeStruct((chunk_rows, width), F32),
            jax.ShapeDtypeStruct((rows, width), BF16),
            jax.ShapeDtypeStruct((1, width), F32),
        ),
        in_specs=[pl.BlockSpec(memory_space=pl.ANY)] + vmem_specs(3),
        out_specs=tuple(vmem_specs(3)),
        scratch_shapes=[
            pltpu.VMEM((rows, width), BF16),
            pltpu.VMEM((2, rows, width), BF16),
        ]
        + [copy_sems(count, pieces)] * 4
        + [pltpu.SemaphoreType.DMA],
        compiler_params=params(collective_id=collective_id, has_side_effects=True),
        cost_estimate=pl.CostEstimate(
            flops=0, bytes_accessed=300 * chunk_rows * width, transcendentals=0
        ),
        name="backward_turn",
    )(given, dy, middle, gain)


def last_turn_kernel(
    count, pieces, dqkv_ref, w_ref, middle_grad_ref, x_ref, gain_ref,
    grad_ref, gain_grad_ref,
    partial, landing, rs_send, rs_receive,
):
    line = Line(count)
    chunk_rows = x_ref.shape[0]
    line.barrier()
    width = dqkv_ref.shape[1]

    @pl.loop(0, partial.shape[0] // SPAN)
    def _(step):
        rows = pl.ds(step * SPAN, SPAN)
        partial[rows, :] = project_back(dqkv_ref[rows, :], w_ref[:, :width]).astype(BF16)

    scatter = Scatter(line, partial, landing, rs_send, rs_receive, chunk_rows, pieces)
    size = chunk_rows // pieces
    gain_grad_ref[...] = jnp.zeros_like(gain_grad_ref)

    def settle(piece):
        scatter.arrived(piece)
        local = pl.ds(piece * size, size)
        total = scatter.total(piece)
        grad, gain_grad = norm_back(total, x_ref[local, :].astype(F32), gain_ref[...])
        gain_grad_ref[...] += gain_grad
        grad_ref[local, :] = (grad + middle_grad_ref[local, :]).astype(BF16)

    pipeline(pieces, scatter.step, settle, lambda piece: None)
    scatter.finish(pieces)


def last_turn(dqkv, w_qkv, middle_grad, x, gain, count, collective_id, pieces=4):
    chunk_rows, width = x.shape
    rows = count * chunk_rows
    return pl.pallas_call(
        functools.partial(last_turn_kernel, count, pieces),
        out_shape=(
            jax.ShapeDtypeStruct((chunk_rows, width), BF16),
            jax.ShapeDtypeStruct((1, width), F32),
        ),
        in_specs=vmem_specs(5),
        out_specs=tuple(vmem_specs(2)),
        scratch_shapes=[
            pltpu.VMEM((rows, width), BF16),
            pltpu.VMEM((2, rows, width), BF16),
        ]
        + [copy_sems(count, pieces)] * 2,
        compiler_params=params(collective_id=collective_id, has_side_effects=True),
        cost_estimate=pl.CostEstimate(
            flops=2 * rows * width * dqkv.shape[1],
            bytes_accessed=200 * chunk_rows * width, transcendentals=0,
        ),
        name="last_turn",
    )(dqkv, w_qkv, middle_grad, x, gain)


def scatter_sum(grad, axis):
    return lax.psum_scatter(grad.astype(BF16), axis, scatter_dimension=0, tiled=True)


def shards(
    inputs, cotangent, attn_gain, w_query, w_key, w_value, w_out, mlp_gain, w_gate, w_up, w_down,
    seq_lengths, group_perm, group_starts,
):
    count = lax.axis_size("tensor")
    group_rows = inputs.shape[0] * count
    q_width, kv_width = w_query.shape[1], w_key.shape[1]
    qkv_width = q_width + 2 * kv_width
    start, positions = group_layout(
        seq_lengths, group_perm, group_starts, lax.axis_index("dp"), group_rows, MOST_SEQS
    )
    cosine, sine = slab_tables(positions)

    gains = jnp.stack([attn_gain, mlp_gain], axis=1)
    gains = jnp.pad(gains, ((0, 0), (0, SLAB - 2)))
    packed = jnp.concatenate([w_query, w_key, w_value, gains], axis=1)
    qkv_full = lax.all_gather(packed, "dp", axis=0, tiled=True)
    out_full = lax.all_gather(w_out, "dp", axis=0, tiled=True)
    gate_full = lax.all_gather(w_gate, "dp", axis=0, tiled=True)
    up_full = lax.all_gather(w_up, "dp", axis=0, tiled=True)
    down_full = lax.all_gather(w_down, "dp", axis=0, tiled=True)
    grad_full = lax.all_gather(cotangent, "tensor", axis=0, tiled=True)
    gain_rows = jnp.transpose(qkv_full[:, qkv_width : qkv_width + 2].astype(F32))
    gain_one, gain_two = gain_rows[0:1], gain_rows[1:2]

    x_full = line_gather(inputs, count, 0)
    normed_full, queries, keys, values, mixed, lse = attend(
        x_full, qkv_full, gain_one, cosine, sine, start[:, None], q_width, kv_width
    )
    middle, normed_two_full = forward_turn(mixed, out_full, inputs, gain_two, count, 1)

    gate_pre = project(normed_two_full, gate_full)
    up_pre = project(normed_two_full, up_full)
    active_f, active_back = jax.vjp(
        lambda gate_in, up_in: jax.nn.silu(gate_in) * up_in, gate_pre, up_pre
    )
    active = active_f.astype(BF16)
    outputs = (
        middle
        + lax.psum_scatter(
            project(active, down_full).astype(BF16), "tensor", scatter_dimension=0, tiled=True
        ).astype(F32)
    ).astype(BF16)
    active_grad = project_back(grad_full, down_full)
    gate_grad_f, up_grad_f = active_back(active_grad)
    gate_grad = gate_grad_f.astype(BF16)
    up_grad = up_grad_f.astype(BF16)
    down_grad = scatter_sum(row_contract(active, grad_full), "dp")
    gate_weight_grad = scatter_sum(row_contract(normed_two_full, gate_grad), "dp")
    up_weight_grad = scatter_sum(row_contract(normed_two_full, up_grad), "dp")
    norm_two_grad = (project_back(gate_grad, gate_full) + project_back(up_grad, up_full)).astype(
        BF16
    )
    middle_grad, branch_full, gain_two_grad = backward_turn(
        norm_two_grad, cotangent, middle, gain_two, count, 2
    )
    dqkv = attend_back(
        branch_full, out_full, queries, keys, values, lse, cosine, sine, start[None, :]
    )
    out_grad = scatter_sum(row_contract(mixed, branch_full), "dp")
    qkv_grad = scatter_sum(row_contract(normed_full, dqkv), "dp").astype(F32)
    input_grad, gain_one_grad = last_turn(
        dqkv, qkv_full, middle_grad, inputs, gain_one, count, 3
    )
    gains_grad = lax.psum(
        lax.psum_scatter(
            jnp.concatenate([gain_one_grad, gain_two_grad], axis=0), "dp",
            scatter_dimension=1, tiled=True,
        ),
        "tensor",
    )
    return (
        outputs,
        input_grad,
        gains_grad[0],
        qkv_grad[:, :q_width],
        qkv_grad[:, q_width : q_width + kv_width],
        qkv_grad[:, q_width + kv_width :],
        out_grad.astype(F32),
        gains_grad[1],
        gate_weight_grad.astype(F32),
        up_weight_grad.astype(F32),
        down_grad.astype(F32),
    )


def solution(mesh):
    in_specs = (
        P(("dp", "tensor"), None),
        P(("dp", "tensor"), None),
        P("dp"),
        P("dp", "tensor"),
        P("dp", "tensor"),
        P("dp", "tensor"),
        P(("tensor", "dp"), None),
        P("dp"),
        P("dp", "tensor"),
        P("dp", "tensor"),
        P(("tensor", "dp"), None),
        P(),
        P(),
        P(),
    )
    out_specs = (
        P(("dp", "tensor"), None),
        P(("dp", "tensor"), None),
        P("dp"),
        P("dp", "tensor"),
        P("dp", "tensor"),
        P("dp", "tensor"),
        P(("tensor", "dp"), None),
        P("dp"),
        P("dp", "tensor"),
        P("dp", "tensor"),
        P(("tensor", "dp"), None),
    )
    return jax.shard_map(shards, mesh=mesh, in_specs=in_specs, out_specs=out_specs, check_vma=False)
```

time: 1380 us -> 1140 us (0.83)
  waiting for transfers between devices: 919 us -> 346 us
  Pallas kernels: 0 us -> 565 us
  matrix products: 265 us -> 146 us
  other arithmetic: 88.7 us -> 23.4 us
  blocking collectives: 64.1 us -> 8.35 us
    pallas_call x0 -> x6, Pallas kernels: none -> 565 us  [the longest x1 217 us: forward_turn(): pl.pallas_call(functools.partial(forward_turn_kernel, count, pieces), out...]
    all_gather x8 -> x5, waiting for transfers between devices: 339 us -> 0.03 us  [the longest x1 0.02 us: shards(): gate_full = lax.all_gather(w_gate, 'dp', axis=0, tiled=True)]
    reduce_scatter x11 -> x6, waiting for transfers between devices: 509 us -> 343 us  [the longest x5 268 us: scatter_sum(): lax.psum_scatter(grad.astype(BF16), axis, scatter_dimension=0, tiled=True)]
    dot_general x19 -> x3, matrix products: 147 us -> 43.2 us  [project(): return jnp.dot(left, right, preferred_element_type=F32)]
    all_gather x1, waiting for transfers between devices: 67.9 us -> 0.01 us  [shards(): grad_full = lax.all_gather(cotangent, 'tensor', axis=0, tiled=True)]
    convert_element_type x22 -> x6, other arithmetic: 55.1 us -> 12.6 us  [the longest x1 2.79 us: shards(): gate_weight_grad.astype(F32)]
    all_gather x4 -> x0, blocking collectives: 38 us -> none  [the longest x1 10.4 us: shards(): lax.all_gather(attn_gain, 'dp', axis=0, tiled=True)]
    reduce_sum x6 -> x0, other arithmetic: 24.8 us -> none  [the longest x2 16.6 us: attend(): total_weight = jnp.sum(weights, axis=-1, keepdims=True)]
  transfers between devices with their start and end apart: 20 -> 13, of which waited for: 18 -> 6; matrix products, arithmetic and copies ran while one was open for 21% -> 12% of each run, Pallas kernels for 0% -> 28%
where the time goes in v1:
time: 1140 us; the launch traced here: 1130 us
  Pallas kernels  565 us (50%)
  waiting for transfers between devices  346 us (30%)
  matrix products  146 us (13%)
  other arithmetic  23.4 us (2%)
  between operations  18.5 us (2%)
  local copies, waits for them, and re-layouts  18.4 us (2%)
    reduce_scatter x5, waiting for transfers between devices, scatter_sum(): lax.psum_scatter(grad.astype(BF16), axis, scatter_dimension=0, tiled=True)  268 us
    pallas_call x1, Pallas kernels, forward_turn(): pl.pallas_call(functools.partial(forward_turn_kernel, count, pieces), out...  217 us
    pallas_call x1, Pallas kernels, backward_turn(): pl.pallas_call(functools.partial(backward_turn_kernel, count, pieces), ou...  134 us
    pallas_call x1, Pallas kernels, last_turn(): pl.pallas_call(functools.partial(last_turn_kernel, count, pieces), out_sh...  81.6 us
    reduce_scatter x1, waiting for transfers between devices, shards(): lax.psum_scatter(project(active, down_full).astype(BF16), 'tensor', scatt...  75.5 us
    pallas_call x1, Pallas kernels, line_gather(): pl.pallas_call(functools.partial(gather_kernel, count, pieces), out_shape...  74.4 us
    dot_general x5, matrix products, row_contract(): lax.dot_general(left, right, (((0,), (0,)), ((), ())), preferred_element_...  55.7 us
    dot_general x3, matrix products, project_back(): lax.dot_general(left, right, (((1,), (1,)), ((), ())), preferred_element_...  46.9 us
  transfers between devices with their start and end apart: 13, of which 6 were waited for; matrix products, arithmetic and copies ran while one was open for 12% of the time, Pallas kernels for 28%

profile of v1, /device:TPU:0, one launch (start us, length us, event | category | flops | bytes accessed | tf_op | source)
XLA Modules:
  0.0 1127.3 jit_solution(6717523990621882206)
XLA Ops:
  15.7 74.4 %line_gather.1.x_ref = bf16[1024,2048]{1,0:T(8,128)(2,1)} custom-call(bf16[256,2048]{1,0:T(8,128)(2,1)} %x_ref.5), custom_call_target="tpu_custom_call" | custom-call | bytes 104857600 | tf_op jit(solution)/shard_map/line_gather/pallas_call | solution.py:449
  94.6 1.9 fusion.12
  99.4 3.1 negate_select_fusion
  102.5 6.1 copy.33.w_ref
  109.9 28.2 %attend.1 = (bf16[1024,2048]{1,0:T(8,128)(2,1)}, bf16[1024,512]{1,0:T(8,128)(2,1)}, bf16[2,1024,128]{2,1,0:T(8,128)(2,1)}, bf16[2,1024,128]{2,1,0:T(8,128)(2,1)}...) custom-call(bf16[1024,2048]{1,0:T(8,128)(2,1)} %line_gather.1.x_ref, bf16[2048,896]{1,0:T(8,128)(2,1)} %copy.33.w_ref, ...), custom_call_target="tpu_custom_call" | custom-call | flops 7516192768 | bytes 16777216 | tf_op jit(solution)/shard_map/attend/pallas_call | solution.py:178
  138.1 216.9 %forward_turn.1 = (f32[256,2048]{1,0:T(8,128)}, bf16[1024,2048]{1,0:T(8,128)(2,1)}) custom-call(bf16[1024,512]{1,0:T(8,128)(2,1)} %get-tuple-element.24.mixed_ref, bf16[512,2048]{1,0:T(8,128)(2,1)} %all-gather.9.cloned.1.call-done.w_ref, bf16[256,2048]{1,0:T(8,128)(2,1)} %x_ref.5, f32[1,2048]{1,0:T(1,128)} %get-tuple-element.48.gain_ref), custom_call_target="tpu_custom_call" | custom-call | flops 2147483648 | bytes 157286400 | tf_op jit(solution)/shard_map/forward_turn/pallas_call | solution.py:511
  355.0 14.8 %fusion.17 = f32[1024,2048]{1,0:T(8,128)} fusion(bf16[1024,2048]{1,0:T(8,128)(2,1)} %get-tuple-element.26, bf16[2048,2048]{1,0:T(8,128)(2,1)} %all-gather.11.cloned.1.call-done), kind=kOutput, calls=%fused_computation.54 | convolution fusion | flops 8589934592 | bytes 20971520 | tf_op jit(solution)/shard_map/dot_general | solution.py:67
  369.8 14.6 %fusion.18 = f32[1024,2048]{1,0:T(8,128)} fusion(bf16[1024,2048]{1,0:T(8,128)(2,1)} %get-tuple-element.26, bf16[2048,2048]{1,0:T(8,128)(2,1)} %all-gather.13.cloned.1.call-done), kind=kOutput, calls=%fused_computation.55 | convolution fusion | flops 8589934592 | bytes 20971520 | tf_op jit(solution)/shard_map/dot_general | solution.py:67
  384.4 21.8 %multiply_convert_fusion = (bf16[1024,2048]{1,0:T(8,128)(2,1)}, bf16[1024,2048]{1,0:T(8,128)(2,1)}, bf16[1024,2048]{1,0:T(8,128)(2,1)}) fusion(f32[1024,2048]{1,0:T(8,128)} %fusion.17, f32[1024,2048]{1,0:T(8,128)} %fusion.18, bf16[1024,2048]{1,0:T(8,128)(2,1)} %all-gather.17.cloned.1.call-done, bf16[2048,2048]{1,0:T(8,128)(2,1)} %all-gather.15.cloned.1.call-done), kind=kOutput, calls=%fused_computation.5 | convolution fusion | flops 8623489024 | bytes 41943040 | tf_op jit(solution)/shard_map/dot_general | solution.py:71
  406.2 13.1 %fusion.19 = f32[1024,2048]{1,0:T(8,128)S(1)} fusion(bf16[1024,2048]{1,0:T(8,128)(2,1)} %get-tuple-element.44, bf16[2048,2048]{1,0:T(8,128)(2,1)} %all-gather.11.cloned.1.call-done), kind=kOutput, calls=%fused_computation.56 | convolution fusion | flops 8589934592 | bytes 20971520 | tf_op jit(solution)/shard_map/dot_general | solution.py:71
  419.3 12.0 %add_convert_fusion.given_ref = bf16[1024,2048]{1,0:T(8,128)(2,1)} fusion(f32[1024,2048]{1,0:T(8,128)S(1)} %fusion.19, bf16[1024,2048]{1,0:T(8,128)(2,1)} %get-tuple-element.43, bf16[2048,2048]{1,0:T(8,128)(2,1)S(1)} %copy-done.6), kind=kOutput, calls=%fused_computation.4 | convolution fusion | flops 8594128896 | bytes 25165824 | tf_op jit(solution)/shard_map/dot_general | solution.py:71
  431.3 134.2 %backward_turn.1 = (f32[256,2048]{1,0:T(8,128)}, bf16[1024,2048]{1,0:T(8,128)(2,1)}, f32[1,2048]{1,0:T(1,128)}) custom-call(bf16[1024,2048]{1,0:T(8,128)(2,1)} %add_convert_fusion.given_ref, bf16[256,2048]{1,0:T(8,128)(2,1)} %dy_ref.1, f32[256,2048]{1,0:T(8,128)} %get-tuple-element.25.middle_ref, f32[1,2048]{1,0:T(1,128)} %get-tuple-element.48.gain_ref), custom_call_target="tpu_custom_call" | custom-call | bytes 157286400 | tf_op jit(solution)/shard_map/backward_turn/pallas_call | solution.py:577
  565.5 29.9 %attend_back.1.dqkv_ref = bf16[1024,768]{1,0:T(8,128)(2,1)} custom-call(bf16[1024,2048]{1,0:T(8,128)(2,1)} %get-tuple-element.27.branch_ref, bf16[512,2048]{1,0:T(8,128)(2,1)} %all-gather.9.cloned.1.call-done.w_ref, bf16[1024,512]{1,0:T(8,128)(2,1)} %get-tuple-element.28.q_ref, bf16[2,1024,128]{2,1,0:T(8,128)(2,1)} %get-tuple-element.29.k_ref, ...), custom_call_target="tpu_custom_call" | custom-call | flops 12884901888 | bytes 16777216 | tf_op jit(solution)/shard_map/attend_back/pallas_call | solution.py:277
  595.4 81.6 %last_turn.1 = (bf16[256,2048]{1,0:T(8,128)(2,1)}, f32[1,2048]{1,0:T(1,128)}) custom-call(bf16[1024,768]{1,0:T(8,128)(2,1)} %attend_back.1.dqkv_ref, bf16[2048,896]{1,0:T(8,128)(2,1)} %copy.33.w_ref, f32[256,2048]{1,0:T(8,128)} %get-tuple-element.32.middle_grad_ref, bf16[256,2048]{1,0:T(8,128)(2,1)} %x_ref.5, f32[1,2048]{1,0:T(1,128)} %get-tuple-element.49.gain_ref), custom_call_target="tpu_custom_call" | custom-call | flops 3221225472 | bytes 104857600 | tf_op jit(solution)/shard_map/last_turn/pallas_call | solution.py:634
  679.4 6.0 convolution_convert_fusion.5
  685.5 7.5 convolution_convert_fusion.4
  693.1 13.9 %convolution_convert_fusion.3 = bf16[1024,2048]{1,0:T(8,128)(2,1)} fusion(bf16[1024,2048]{1,0:T(8,128)(2,1)} %get-tuple-element.45, bf16[2048,2048]{1,0:T(8,128)(2,1)} %all-gather.15.cloned.1.call-done), kind=kOutput, calls=%fused_computation.12 | convolution fusion | flops 8592031744 | bytes 16777216 | tf_op jit(solution)/shard_map/dot_general | solution.py:67
  707.3 14.1 %convolution_convert_fusion.2 = bf16[2048,2048]{1,0:T(8,128)(2,1)} fusion(bf16[1024,2048]{1,0:T(8,128)(2,1)} %get-tuple-element.26, bf16[1024,2048]{1,0:T(8,128)(2,1)} %get-tuple-element.44), kind=kOutput, calls=%fused_computation.11 | convolution fusion | flops 8594128896 | bytes 16777216 | tf_op jit(solution)/shard_map/dot_general | solution.py:75
  721.5 14.0 %convolution_convert_fusion.1 = bf16[2048,2048]{1,0:T(8,128)(2,1)} fusion(bf16[1024,2048]{1,0:T(8,128)(2,1)} %get-tuple-element.26, bf16[1024,2048]{1,0:T(8,128)(2,1)} %get-tuple-element.43), kind=kOutput, calls=%fused_computation.10 | convolution fusion | flops 8594128896 | bytes 16777216 | tf_op jit(solution)/shard_map/dot_general | solution.py:75
  735.9 14.1 %convolution_convert_fusion = bf16[2048,2048]{1,0:T(8,128)(2,1)} fusion(bf16[1024,2048]{1,0:T(8,128)(2,1)} %get-tuple-element.45, bf16[1024,2048]{1,0:T(8,128)(2,1)} %all-gather.17.cloned.1.call-done), kind=kOutput, calls=%fused_computation.9 | convolution fusion | flops 8594128896 | bytes 16777216 | tf_op jit(solution)/shard_map/dot_general | solution.py:75
  751.1 8.3 psum.7
  760.0 2.7 reduce-scatter.14.cloned.1.call-done
  764.5 47.7 %reduce-scatter.12.cloned.1.call-done = bf16[256,768]{1,0:T(8,128)(2,1)} async-done(((bf16[2048,768]{1,0:T(8,128)(2,1)}), bf16[256,768]{1,0:T(8,128)(2,1)}) %reduce-scatter.12.cloned.1.call-update) | async-done | bytes 393232 | tf_op jit(solution)/shard_map/reduce_scatter | solution.py:657
  812.2 1.8 slice.36
  815.6 75.5 %reduce-scatter.10.cloned.1.call-done = bf16[256,2048]{1,0:T(8,128)(2,1)} async-done(((bf16[1024,2048]{1,0:T(8,128)(2,1)}), bf16[256,2048]{1,0:T(8,128)(2,1)}) %reduce-scatter.10.cloned.1.call-update) | async-done | bytes 1048592 | tf_op jit(solution)/shard_map/reduce_scatter | solution.py:699
  891.1 2.5 add_convert_fusion.1
  893.6 73.0 %reduce-scatter.16.cloned.1.call-done = bf16[256,2048]{1,0:T(8,128)(2,1)} async-done(((bf16[2048,2048]{1,0:T(8,128)(2,1)}), bf16[256,2048]{1,0:T(8,128)(2,1)}) %reduce-scatter.16.cloned.1.call-update) | async-done | bytes 1048592 | tf_op jit(solution)/shard_map/reduce_scatter | solution.py:657
  966.6 2.8 convert_element_type.84
  969.4 72.1 %reduce-scatter.18.cloned.1.call-done = bf16[256,2048]{1,0:T(8,128)(2,1)} async-done(((bf16[2048,2048]{1,0:T(8,128)(2,1)}), bf16[256,2048]{1,0:T(8,128)(2,1)}) %reduce-scatter.18.cloned.1.call-update) | async-done | bytes 1048592 | tf_op jit(solution)/shard_map/reduce_scatter | solution.py:657
  1041.5 2.8 convert_element_type.86
  1044.3 72.2 %reduce-scatter.20.cloned.1.call-done = bf16[256,2048]{1,0:T(8,128)(2,1)} async-done(((bf16[2048,2048]{1,0:T(8,128)(2,1)}), bf16[256,2048]{1,0:T(8,128)(2,1)}) %reduce-scatter.20.cloned.1.call-update) | async-done | bytes 1048592 | tf_op jit(solution)/shard_map/reduce_scatter | solution.py:657
  1116.5 2.8 convert_element_type.88
  (75 shorter events, 22.5 us)
Async XLA Ops:
  7.2 95.3 %all-gather.7.cloned.1.call-start = ((), (), s32[]{:S(2)}) async-start(), calls=%async_computation.7 | async-start | bytes 4128768 | tf_op jit(solution)/shard_map/all_gather | solution.py:676
  12.4 125.8 %all-gather.9.cloned.1.call-start = ((), (), s32[]{:S(2)}) async-start(), calls=%async_computation.8 | async-start | bytes 2359296 | tf_op jit(solution)/shard_map/all_gather | solution.py:677
  13.1 341.9 %all-gather.11.cloned.1.call-start = ((), (), s32[]{:S(2)}) async-start(), calls=%async_computation.9 | async-start | bytes 9437184 | tf_op jit(solution)/shard_map/all_gather | solution.py:678
  13.8 76.2 %copy-start.3 = (s32[9]{0:T(128)S(1)}, s32[9]{0:T(128)}, u32[]{:S(2)}) copy-start(s32[9]{0:T(128)} %param.27) | copy-start | bytes 112
  13.9 79.5 %copy-start.4 = (s32[12]{0:T(128)S(1)}, s32[12]{0:T(128)}, u32[]{:S(2)}) copy-start(s32[12]{0:T(128)} %param.26) | copy-start | bytes 148
  13.9 80.7 %copy-start.5 = (s32[12]{0:T(128)S(1)}, s32[12]{0:T(128)}, u32[]{:S(2)}) copy-start(s32[12]{0:T(128)} %param.25) | copy-start | bytes 148
  13.9 355.9 %all-gather.13.cloned.1.call-start = ((), (), s32[]{:S(2)}) async-start(), calls=%async_computation.10 | async-start | bytes 9437184 | tf_op jit(solution)/shard_map/all_gather | solution.py:679
  14.5 369.9 %all-gather.17.cloned.1.call-start = ((), (), s32[]{:S(2)}) async-start(), calls=%async_computation.13 | async-start | bytes 5242880 | tf_op jit(solution)/shard_map/all_gather | solution.py:681
  15.0 369.3 %all-gather.15.cloned.1.call-start = ((), (), s32[]{:S(2)}) async-start(), calls=%async_computation.11 | async-start | bytes 9437184 | tf_op jit(solution)/shard_map/all_gather | solution.py:680
  15.6 734.4 %reduce-scatter.22.cloned.1.call-start = ((), (), s32[]{:S(2)}) async-start(), calls=%async_computation.19 | async-start | bytes 1179648
  406.2 13.1 %copy-start.6 = (bf16[2048,2048]{1,0:T(8,128)(2,1)S(1)}, bf16[2048,2048]{1,0:T(8,128)(2,1)}, u32[]{:S(2)}) copy-start(bf16[2048,2048]{1,0:T(8,128)(2,1)} %all-gather.13.cloned.1.call-done) | copy-start | bytes 25165828
  595.4 81.6 %copy-start.2 = (f32[1,2048]{1,0:T(1,128)S(1)}, f32[1,2048]{1,0:T(1,128)}, u32[]{:S(2)}) copy-start(f32[1,2048]{1,0:T(1,128)} %get-tuple-element.35) | copy-start | bytes 24580
  595.4 84.0 %copy-start.7 = (bf16[1024,512]{1,0:T(8,128)(2,1)S(1)}, bf16[1024,512]{1,0:T(8,128)(2,1)}, u32[]{:S(2)}) copy-start(bf16[1024,512]{1,0:T(8,128)(2,1)} %get-tuple-element.24.mixed_ref) | copy-start | bytes 3145732
  679.1 6.4 copy-start.8
  679.1 83.6 %reduce-scatter.14.cloned.1.call-start = ((), (), s32[]{:S(2)}) async-start(), calls=%async_computation.15 | async-start | bytes 2359296 | tf_op jit(solution)/shard_map/reduce_scatter | solution.py:657
  685.4 126.7 %reduce-scatter.12.cloned.1.call-start = ((), (), s32[]{:S(2)}) async-start(), calls=%async_computation.14 | async-start | bytes 3538944 | tf_op jit(solution)/shard_map/reduce_scatter | solution.py:657
  693.1 198.1 %reduce-scatter.10.cloned.1.call-start = ((), (), s32[]{:S(2)}) async-start(), calls=%async_computation.12 | async-start | bytes 5242880 | tf_op jit(solution)/shard_map/reduce_scatter | solution.py:699
  707.0 259.6 %reduce-scatter.16.cloned.1.call-start = ((), (), s32[]{:S(2)}) async-start(), calls=%async_computation.16 | async-start | bytes 9437184 | tf_op jit(solution)/shard_map/reduce_scatter | solution.py:657
  721.4 320.1 %reduce-scatter.18.cloned.1.call-start = ((), (), s32[]{:S(2)}) async-start(), calls=%async_computation.17 | async-start | bytes 9437184 | tf_op jit(solution)/shard_map/reduce_scatter | solution.py:657
  735.5 381.0 %reduce-scatter.20.cloned.1.call-start = ((), (), s32[]{:S(2)}) async-start(), calls=%async_computation.18 | async-start | bytes 9437184 | tf_op jit(solution)/shard_map/reduce_scatter | solution.py:657
  749.9 141.2 %copy-start = (f32[256,2048]{1,0:T(8,128)S(1)}, f32[256,2048]{1,0:T(8,128)}, u32[]{:S(2)}) copy-start(f32[256,2048]{1,0:T(8,128)} %get-tuple-element.25.middle_ref) | copy-start | bytes 6291460
  893.6 225.7 %copy-start.1 = (bf16[256,2048]{1,0:T(8,128)(2,1)S(1)}, bf16[256,2048]{1,0:T(8,128)(2,1)}, u32[]{:S(2)}) copy-start(bf16[256,2048]{1,0:T(8,128)(2,1)} %get-tuple-element.66) | copy-start | bytes 3145732
Sparse Core Ops, SparseCore 0:
  12.5 37.7 all-gather.6
  52.2 27.7 all-gather.8
  81.9 54.2 all-gather.10
  137.9 54.2 all-gather.12
  193.6 99.9 all-gather.16
  295.4 52.4 all-gather.14
  679.2 38.4 reduce-scatter.21
  721.6 41.0 reduce-scatter.13
  766.1 46.0 reduce-scatter.11
  814.3 76.7 reduce-scatter.9
  894.6 72.0 reduce-scatter.15
  970.0 71.4 reduce-scatter.17
  1044.9 71.4 reduce-scatter.19

commit v2 on v1

--- a/solution.py
+++ b/solution.py
@@ -194,10 +194,264 @@
     )(x_full, w_qkv, gain, cosine, sine, start)
 
 
+SUBS = 4
+BLOCK = 1024
+
+
+class Line:
+    def __init__(self, count):
+        self.count = count
+        self.place = lax.axis_index("tensor")
+        self.has = (self.place < count - 1, self.place > 0)
+        self.neighbour = (self.place + 1, self.place - 1)
+        other = count - 1 - self.place
+        self.lag = jnp.where(self.place > other, self.place, other)
+
+    def greet(self, semaphore):
+        for way in (0, 1):
+            @pl.when(self.has[way])
+            def _(way=way):
+                pl.semaphore_signal(semaphore, 1, device_id={"tensor": self.neighbour[way]})
+        ends = (self.place == 0) | (self.place == self.count - 1)
+        return jnp.where(ends, 1, 2)
+
+    def barrier(self):
+        semaphore = pltpu.get_barrier_semaphore()
+        pl.semaphore_wait(semaphore, self.greet(semaphore))
+
+    def copy(self, source, target, send, receive, way):
+        return pltpu.make_async_remote_copy(
+            src_ref=source, dst_ref=target, send_sem=send, recv_sem=receive,
+            device_id={"tensor": self.neighbour[way]},
+        )
+
+
+class Gather:
+    def __init__(self, line, full, send, receive, chunk_rows, pieces, lags=None):
+        self.line, self.full, self.send, self.receive = line, full, send, receive
+        self.chunk_rows, self.size, self.pieces = chunk_rows, chunk_rows // pieces, pieces
+        self.lags = lags or [0] * line.count
+
+    def rows(self, chunk, piece):
+        start = chunk * self.chunk_rows + piece * self.size
+        return pl.ds(pl.multiple_of(start, self.size), self.size)
+
+    def copy(self, chunk, piece, way, source=None):
+        target = self.full.at[self.rows(chunk, piece)]
+        return self.line.copy(
+            target if source is None else source, target,
+            self.send.at[way, chunk, piece], self.receive.at[way, chunk, piece], way,
+        )
+
+    def start(self, piece, source=None):
+        for way in (0, 1):
+            @pl.when(self.line.has[way])
+            def _(way=way):
+                self.copy(self.line.place, piece, way, source).start()
+
+    def turn(self, turn):
+        line = self.line
+        for chunk in range(line.count):
+            for way in (0, 1):
+                hop = line.place - chunk if way == 0 else chunk - line.place
+                piece = turn - self.lags[chunk] - hop
+
+                @pl.when((hop > 0) & (piece >= 0) & (piece < self.pieces))
+                def _(way=way, chunk=chunk, piece=piece):
+                    self.copy(chunk, piece, way).wait_recv()
+
+                    @pl.when(line.has[way])
+                    def _():
+                        self.copy(chunk, piece, way).start()
+
+    def finish(self, source=None):
+        line = self.line
+
+        @pl.loop(0, self.pieces)
+        def _(piece):
+            for chunk in range(line.count):
+                @pl.when(line.has[0] & (chunk <= line.place))
+                def _(chunk=chunk):
+                    self.copy(chunk, piece, 0, source).wait_send()
+
+                @pl.when(line.has[1] & (chunk >= line.place))
+                def _(chunk=chunk):
+                    self.copy(chunk, piece, 1, source).wait_send()
+
+
+class Scatter:
+    def __init__(self, line, partial, landing, send, receive, chunk_rows, pieces):
+        self.line, self.partial, self.landing = line, partial, landing
+        self.send, self.receive = send, receive
+        self.chunk_rows, self.size, self.pieces = chunk_rows, chunk_rows // pieces, pieces
+
+    def rows(self, chunk, piece):
+        start = chunk * self.chunk_rows + piece * self.size
+        return pl.ds(pl.multiple_of(start, self.size), self.size)
+
+    def landed(self, chunk, piece, way, owner):
+        if way == 1:
+            chunk = jnp.where(chunk == owner, self.line.count, chunk)
+        return self.rows(chunk, piece)
+
+    def copy(self, chunk, piece, way, owner=None):
+        owner = self.line.neighbour[way] if owner is None else owner
+        return self.line.copy(
+            self.partial.at[self.rows(chunk, piece)],
+            self.landing.at[self.landed(chunk, piece, way, owner)],
+            self.send.at[way, chunk, piece], self.receive.at[way, chunk, piece], way,
+        )
+
+    def wait(self, chunk, piece, way):
+        self.copy(chunk, piece, way, self.line.place).wait_recv()
+
+    def forward(self, piece, way):
+        line = self.line
+        for step in range(line.count - 1):
+            chunk = line.count - 1 - step if way == 0 else step
+            beyond = chunk > line.place if way == 0 else chunk < line.place
+
+            @pl.when(beyond)
+            def _(chunk=chunk):
+                @pl.when(line.has[1 - way])
+                def _():
+                    self.wait(chunk, piece, way)
+                    rows = self.rows(chunk, piece)
+                    total = self.partial[rows, :].astype(F32)
+                    total = total + self.landing[rows, :].astype(F32)
+                    self.partial[rows, :] = total.astype(BF16)
+
+                self.copy(chunk, piece, way).start()
+
+    def turn(self, turn):
+        line = self.line
+        for way, lag in ((0, line.place), (1, line.count - 1 - line.place)):
+            piece = turn - lag
+
+            @pl.when((piece >= 0) & (piece < self.pieces))
+            def _(way=way, piece=piece):
+                self.forward(piece, way)
+
+    def settle(self, turn, use):
+        piece = turn - self.line.lag
+
+        @pl.when((piece >= 0) & (piece < self.pieces))
+        def _():
+            for way in (0, 1):
+                @pl.when(self.line.has[1 - way])
+                def _(way=way):
+                    self.wait(self.line.place, piece, way)
+            use(piece)
+
+    def total(self, piece):
+        place = self.line.place
+        total = self.partial[self.rows(place, piece), :].astype(F32)
+        for way in (0, 1):
+            got = self.landing[self.landed(place, piece, way, place), :].astype(F32)
+            total = total + jnp.where(self.line.has[1 - way], got, 0.0)
+        return total
+
+    def finish(self):
+        line = self.line
+
+        @pl.loop(0, self.pieces)
+        def _(piece):
+            for chunk in range(line.count):
+                @pl.when(chunk > line.place)
+                def _(chunk=chunk):
+                    self.copy(chunk, piece, 0).wait_send()
+
+                @pl.when(chunk < line.place)
+                def _(chunk=chunk):
+                    self.copy(chunk, piece, 1).wait_send()
+
+
+class Fold:
+    def __init__(self, replicas, sums, traded, arrived, pair_sems, sends, receives):
+        self.halves = replicas // 2
+        self.sums, self.traded, self.arrived = sums, traded, arrived
+        self.pair_sems, self.sends, self.receives = pair_sems, sends, receives
+        replica = lax.axis_index("dp")
+        self.side, self.mine = replica % 2, replica // 2
+        self.partner = replica + 1 - 2 * self.side
+
+    def greet(self, semaphore):
+        pl.semaphore_signal(semaphore, 1, device_id={"dp": self.partner})
+        for step in range(1, self.halves):
+            peer = 2 * ((self.mine + step) % self.halves) + self.side
+            pl.semaphore_signal(semaphore, 1, device_id={"dp": peer})
+        return self.halves
+
+    def pair(self):
+        return pltpu.make_async_remote_copy(
+            src_ref=self.sums.at[:, 1 - self.side], dst_ref=self.traded,
+            send_sem=self.pair_sems.at[0], recv_sem=self.pair_sems.at[1],
+            device_id={"dp": self.partner},
+        )
+
+    def peer(self, half, landing):
+        return pltpu.make_async_remote_copy(
+            src_ref=self.sums.at[half, self.side], dst_ref=self.arrived.at[landing],
+            send_sem=self.sends.at[half], recv_sem=self.receives.at[landing],
+            device_id={"dp": 2 * half + self.side},
+        )
+
+    def others(self):
+        return [(self.mine + step) % self.halves for step in range(1, self.halves)]
+
+    def spread(self):
+        self.pair().wait_recv()
+
+        @pl.loop(0, self.halves)
+        def _(half):
+            total = self.sums[half, self.side].astype(F32) + self.traded[half].astype(F32)
+            self.sums[half, self.side] = total.astype(BF16)
+
+        for half in self.others():
+            self.peer(half, self.mine).start()
+
+    def total(self):
+        total = self.sums[self.mine, self.side].astype(F32)
+        for half in self.others():
+            self.peer(half, half).wait_recv()
+            total = total + self.arrived[half].astype(F32)
+        return total
+
+    def finish(self):
+        self.pair().wait_send()
+        for half in self.others():
+            self.peer(half, self.mine).wait_send()
+
+
+def fold_scratch(replicas, rows, width):
+    halves = replicas // 2
+    return [
+        pltpu.VMEM((halves, 2, rows, width), BF16),
+        pltpu.VMEM((halves, rows, width), BF16),
+        pltpu.VMEM((halves, rows, width), BF16),
+        pltpu.SemaphoreType.DMA((2,)),
+        pltpu.SemaphoreType.DMA((halves,)),
+        pltpu.SemaphoreType.DMA((halves,)),
+    ]
+
+
 def attend_back_kernel(
-    branch_ref, w_ref, q_ref, k_ref, v_ref, lse_ref, cos_ref, sin_ref, start_ref,
-    dqkv_ref, dmix_ref, bias_ref, dq_ref, dk_ref, dv_ref,
+    replicas, branch_ref, w_ref, mixed_ref, q_ref, k_ref, v_ref, lse_ref, cos_ref, sin_ref,
+    start_ref, dqkv_ref, weight_grad_ref, dmix_ref, bias_ref, dq_ref, dk_ref, dv_ref,
+    sums, traded, arrived, pair_sems, sends, receives,
 ):
+    fold = Fold(replicas, sums, traded, arrived, pair_sems, sends, receives)
+    semaphore = pltpu.get_barrier_semaphore()
+    pl.semaphore_wait(semaphore, fold.greet(semaphore))
+    weight_rows = sums.shape[2]
+    for step in range(mixed_ref.shape[1] // SLAB):
+        first = step * SLAB
+        product = row_contract(mixed_ref[:, first : first + SLAB], branch_ref[...]).astype(BF16)
+        for row in range(0, SLAB, weight_rows):
+            owner = (first + row) // weight_rows
+            sums[owner // 2, owner % 2] = product[row : row + weight_rows]
+    fold.pair().start()
+
     rows_all = branch_ref.shape[0]
     q_width = q_ref.shape[1]
     slabs = q_width // SLAB
@@ -210,6 +464,7 @@
         rows = pl.ds(step * SPAN, SPAN)
         dmix_ref[rows, :] = project_back(branch_ref[rows, :], w_ref[...]).astype(BF16)
 
+    fold.spread()
     dk_ref[...] = jnp.zeros_like(dk_ref)
     dv_ref[...] = jnp.zeros_like(dv_ref)
     for tile in range(rows_all // SPAN):
@@ -268,183 +523,72 @@
             at = at + (kv_heads // 2) * SLAB
             dqkv_ref[rows, at : at + SLAB] = value.astype(BF16)
 
-
-def attend_back(branch_full, w_out, queries, keys, values, lse, cosine, sine, start):
+    weight_grad_ref[...] = fold.total()
+    fold.finish()
+
+
+def attend_back(
+    branch_full, w_out, mixed, queries, keys, values, lse, cosine, sine, start,
+    replicas, collective_id,
+):
     rows, q_width = queries.shape
     kv_heads = keys.shape[0]
     width = q_width + kv_heads * SLAB
     flops = 2 * rows * branch_full.shape[1] * q_width + 20 * rows * rows * q_width
     return pl.pallas_call(
-        attend_back_kernel,
-        out_shape=jax.ShapeDtypeStruct((rows, width), BF16),
-        in_specs=vmem_specs(9),
-        out_specs=vmem_specs(1)[0],
+        functools.partial(attend_back_kernel, replicas),
+        out_shape=(
+            jax.ShapeDtypeStruct((rows, width), BF16),
+            jax.ShapeDtypeStruct((q_width // replicas, branch_full.shape[1]), F32),
+        ),
+        in_specs=vmem_specs(10),
+        out_specs=tuple(vmem_specs(2)),
         scratch_shapes=[
             pltpu.VMEM((rows, q_width), BF16),
             pltpu.VMEM((rows, SPAN), F32),
             pltpu.VMEM((rows, q_width), F32),
             pltpu.VMEM((kv_heads, rows, SLAB), F32),
             pltpu.VMEM((kv_heads, rows, SLAB), F32),
-        ],
-        compiler_params=params(),
+        ]
+        + fold_scratch(replicas, q_width // replicas, branch_full.shape[1]),
+        compiler_params=params(collective_id=collective_id, has_side_effects=True),
         cost_estimate=pl.CostEstimate(flops=flops, bytes_accessed=1 << 24, transcendentals=1 << 23),
         name="attend_back",
-    )(branch_full, w_out, queries, keys, values, lse, cosine, sine, start)
-
-
-class Line:
-    def __init__(self, count):
-        self.count = count
-        self.place = lax.axis_index("tensor")
-        self.has = (self.place < count - 1, self.place > 0)
-        self.neighbour = (self.place + 1, self.place - 1)
-
-    def barrier(self):
-        semaphore = pltpu.get_barrier_semaphore()
-        for way in (0, 1):
-            @pl.when(self.has[way])
-            def _(way=way):
-                pl.semaphore_signal(semaphore, 1, device_id={"tensor": self.neighbour[way]})
-        ends = (self.place == 0) | (self.place == self.count - 1)
-        pl.semaphore_wait(semaphore, jnp.where(ends, 1, 2))
-
-    def copy(self, source, target, send, receive, way):
-        return pltpu.make_async_remote_copy(
-            src_ref=source, dst_ref=target, send_sem=send, recv_sem=receive,
-            device_id={"tensor": self.neighbour[way]},
-        )
-
-
-class Gather:
-    def __init__(self, line, full, send, receive, chunk_rows, pieces):
-        self.line, self.full, self.send, self.receive = line, full, send, receive
-        self.chunk_rows, self.size = chunk_rows, chunk_rows // pieces
-
-    def rows(self, chunk, piece):
-        start = chunk * self.chunk_rows + piece * self.size
-        return pl.ds(pl.multiple_of(start, self.size), self.size)
-
-    def copy(self, chunk, piece, way, source=None):
-        target = self.full.at[self.rows(chunk, piece)]
-        return self.line.copy(
-            target if source is None else source, target,
-            self.send.at[way, chunk, piece], self.receive.at[way, chunk, piece], way,
-        )
-
-    def start(self, piece, source=None):
-        for way in (0, 1):
-            @pl.when(self.line.has[way])
-            def _(way=way):
-                self.copy(self.line.place, piece, way, source).start()
-
-    def pass_on(self, piece, hops=None):
-        line = self.line
-        for hop in hops or range(1, line.count):
-            for way, chunk in ((0, line.place - hop), (1, line.place + hop)):
-                @pl.when((chunk >= 0) & (chunk < line.count))
-                def _(way=way, chunk=chunk):
-                    self.copy(chunk, piece, way).wait_recv()
-
-                    @pl.when(line.has[way])
-                    def _():
-                        self.copy(chunk, piece, way).start()
-
-    def finish(self, pieces, source=None):
-        line = self.line
-        for chunk in range(line.count):
-            for piece in range(pieces):
-                @pl.when(line.has[0] & (chunk <= line.place))
-                def _():
-                    self.copy(chunk, piece, 0, source).wait_send()
-
-                @pl.when(line.has[1] & (chunk >= line.place))
-                def _():
-                    self.copy(chunk, piece, 1, source).wait_send()
-
-
-class Scatter:
-    def __init__(self, line, partial, landing, send, receive, chunk_rows, pieces):
-        self.line, self.partial, self.landing = line, partial, landing
-        self.send, self.receive = send, receive
-        self.chunk_rows, self.size = chunk_rows, chunk_rows // pieces
-
-    def rows(self, chunk, piece):
-        start = chunk * self.chunk_rows + piece * self.size
-        return pl.ds(pl.multiple_of(start, self.size), self.size)
-
-    def copy(self, chunk, piece, way):
-        rows = self.rows(chunk, piece)
-        return self.line.copy(
-            self.partial.at[rows], self.landing.at[way, rows],
-            self.send.at[way, chunk, piece], self.receive.at[way, chunk, piece], way,
-        )
-
-    def step(self, piece):
-        line = self.line
-        for turn in range(line.count - 1):
-            for way, chunk in ((0, line.count - 1 - turn), (1, turn)):
-                beyond = chunk > line.place if way == 0 else chunk < line.place
-
-                @pl.when(beyond)
-                def _(way=way, chunk=chunk):
-                    @pl.when(line.has[1 - way])
-                    def _():
-                        self.copy(chunk, piece, way).wait_recv()
-                        rows = self.rows(chunk, piece)
-                        total = self.partial[rows, :].astype(F32)
-                        total = total + self.landing[way, rows, :].astype(F32)
-                        self.partial[rows, :] = total.astype(BF16)
-
-                    self.copy(chunk, piece, way).start()
-
-    def arrived(self, piece):
-        for way in (0, 1):
-            @pl.when(self.line.has[1 - way])
-            def _(way=way):
-                self.copy(self.line.place, piece, way).wait_recv()
-
-    def total(self, piece, part=None):
-        rows = self.rows(self.line.place, piece) if part is None else part
-        total = self.partial[rows, :].astype(F32)
-        for way in (0, 1):
-            got = self.landing[way, rows, :].astype(F32)
-            total = total + jnp.where(self.line.has[1 - way], got, 0.0)
-        return total
-
-    def finish(self, pieces):
-        line = self.line
-        for chunk in range(line.count):
-            for piece in range(pieces):
-                @pl.when(chunk > line.place)
-                def _():
-                    self.copy(chunk, piece, 0).wait_send()
-
-                @pl.when(chunk < line.place)
-                def _():
-                    self.copy(chunk, piece, 1).wait_send()
+    )(branch_full, w_out, mixed, queries, keys, values, lse, cosine, sine, start)
+
+
+def landing_rows(count, chunk_rows):
+    return (count + 1) * chunk_rows
 
 
 def copy_sems(count, pieces):
     return pltpu.SemaphoreType.DMA((2, count, pieces))
 
 
+def settle_lags(count):
+    return [max(place, count - 1 - place) for place in range(count)]
+
+
 def gather_kernel(count, pieces, x_ref, full_ref, send, receive, local):
     line = Line(count)
-    own = pl.ds(pl.multiple_of(line.place * x_ref.shape[0], x_ref.shape[0]), x_ref.shape[0])
+    chunk_rows = x_ref.shape[0]
+    own = pl.ds(pl.multiple_of(line.place * chunk_rows, chunk_rows), chunk_rows)
     keep = pltpu.make_async_copy(x_ref, full_ref.at[own], local)
     keep.start()
     line.barrier()
-    gather = Gather(line, full_ref, send, receive, x_ref.shape[0], pieces)
+    gather = Gather(line, full_ref, send, receive, chunk_rows, pieces)
     for piece in range(pieces):
         gather.start(piece, x_ref.at[gather.rows(0, piece)])
-    for hop in range(1, count):
-        for piece in range(pieces):
-            gather.pass_on(piece, (hop,))
-    gather.finish(pieces)
+
+    @pl.loop(1, pieces + count - 1)
+    def _(turn):
+        gather.turn(turn)
+
+    gather.finish(x_ref.at[gather.rows(0, 0)])
     keep.wait()
 
 
-def line_gather(x, count, collective_id, pieces=4):
+def line_gather(x, count, collective_id, pieces=8):
     rows, width = x.shape
     return pl.pallas_call(
         functools.partial(gather_kernel, count, pieces),
@@ -472,40 +616,35 @@
 
     @pl.loop(0, partial.shape[0] // SPAN)
     def _(step):
-        rows = pl.ds(step * SPAN, SPAN)
+        rows = pl.ds(pl.multiple_of(step * SPAN, SPAN), SPAN)
         partial[rows, :] = project(mixed_ref[rows, :], w_ref[...]).astype(BF16)
 
     scatter = Scatter(line, partial, landing, rs_send, rs_receive, chunk_rows, pieces)
-    gather = Gather(line, full_ref, ag_send, ag_receive, chunk_rows, pieces)
+    gather = Gather(
+        line, full_ref, ag_send, ag_receive, chunk_rows, pieces, settle_lags(count)
+    )
     size = chunk_rows // pieces
 
     def settle(piece):
-        scatter.arrived(piece)
-        local = pl.ds(piece * size, size)
+        local = pl.ds(pl.multiple_of(piece * size, size), size)
         middle = x_ref[local, :].astype(F32) + scatter.total(piece)
         middle_ref[local, :] = middle
         inverse = lax.rsqrt(jnp.mean(middle * middle, axis=-1, keepdims=True) + norm_epsilon)
-        full_ref[gather.rows(line.place, piece), :] = (
-            middle * inverse * gain_ref[...]
-        ).astype(BF16)
+        normed = (middle * inverse * gain_ref[...]).astype(BF16)
+        full_ref[gather.rows(line.place, piece), :] = normed
         gather.start(piece)
 
-    pipeline(pieces, scatter.step, settle, gather.pass_on)
-    scatter.finish(pieces)
-    gather.finish(pieces)
-
-
-def pipeline(pieces, scatter_step, settle, pass_on):
-    for turn in range(pieces + 2):
-        if turn < pieces:
-            scatter_step(turn)
-        if 1 <= turn <= pieces:
-            settle(turn - 1)
-        if turn >= 2:
-            pass_on(turn - 2)
-
-
-def forward_turn(mixed, w_out, x, gain, count, collective_id, pieces=4):
+    @pl.loop(0, pieces + 2 * (count - 1))
+    def _(turn):
+        scatter.turn(turn)
+        gather.turn(turn)
+        scatter.settle(turn, settle)
+
+    scatter.finish()
+    gather.finish()
+
+
+def forward_turn(mixed, w_out, x, gain, count, collective_id, pieces=8):
     chunk_rows, width = x.shape
     rows = count * chunk_rows
     return pl.pallas_call(
@@ -518,7 +657,7 @@
         out_specs=tuple(vmem_specs(2)),
         scratch_shapes=[
             pltpu.VMEM((rows, width), BF16),
-            pltpu.VMEM((2, rows, width), BF16),
+            pltpu.VMEM((landing_rows(count, chunk_rows), width), BF16),
         ]
         + [copy_sems(count, pieces)] * 4,
         compiler_params=params(collective_id=collective_id, has_side_effects=True),
@@ -530,37 +669,299 @@
     )(mixed, w_out, x, gain)
 
 
+def hidden_kernel(
+    count, pieces, normed_ref, own_ref, middle_ref, gate_ref, up_ref, down_ref,
+    full_ref, active_ref, gate_grad_ref, up_grad_ref, back_ref, out_ref,
+    gate, up, down, normed, dy, active, slope, value, up_grad, back,
+    partial, landing, rs_send, rs_receive, ag_send, ag_receive, loads, stores,
+):
+    line = Line(count)
+    chunk_rows = own_ref.shape[0]
+    hidden = gate_ref.shape[1]
+    width = gate_ref.shape[0]
+    sub = chunk_rows // SUBS
+    fetches = [
+        pltpu.make_async_copy(source, target, loads.at[at])
+        for at, (source, target) in enumerate(
+            ((normed_ref, normed), (gate_ref, gate), (up_ref, up), (down_ref, down))
+        )
+    ]
+    for fetch in fetches:
+        fetch.start()
+    line.barrier()
+    gather = Gather(line, dy, ag_send, ag_receive, chunk_rows, SUBS)
+    scatter = Scatter(line, partial, landing, rs_send, rs_receive, chunk_rows, pieces)
+    for piece in range(SUBS):
+        gather.start(piece, own_ref.at[gather.rows(0, piece)])
+    own = pl.ds(pl.multiple_of(line.place * chunk_rows, chunk_rows), chunk_rows)
+    place_own = pltpu.make_async_copy(own_ref, dy.at[own], loads.at[4])
+    place_own.start()
+    gate_grad = active
+    outs = ((active, active_ref), (gate_grad, gate_grad_ref), (up_grad, up_grad_ref),
+            (back, back_ref))
+
+    def store(which, step):
+        source, target = outs[which]
+        rows = pl.ds(pl.multiple_of(step * sub, sub), sub)
+        return pltpu.make_async_copy(source, target.at[:, rows], stores.at[which])
+
+    def rows_of(chunk, step):
+        return pl.ds(pl.multiple_of(chunk * chunk_rows + step * sub, sub), sub)
+
+    def picked(ref, step, at=slice(None)):
+        return jnp.concatenate([ref[rows_of(chunk, step), at] for chunk in range(count)], axis=0)
+
+    def put(ref, at, rows):
+        for chunk in range(count):
+            ref[chunk, :, at] = rows[chunk * sub : (chunk + 1) * sub]
+
+    def whole(ref):
+        return jnp.concatenate([ref[chunk] for chunk in range(count)], axis=0)
+
+    def settle(piece):
+        size = chunk_rows // pieces
+        local = pl.ds(pl.multiple_of(piece * size, size), size)
+        out_ref[local, :] = (middle_ref[local, :] + scatter.total(piece)).astype(BF16)
+
+    def exchange(turn):
+        scatter.turn(turn)
+        gather.turn(turn)
+        scatter.settle(turn, settle)
+
+    for at in range(3):
+        fetches[at].wait()
+
+    @pl.loop(0, SUBS)
+    def _(step):
+        @pl.when(step > 0)
+        def _():
+            store(0, step - 1).wait()
+
+        @pl.loop(0, hidden // BLOCK)
+        def _(block):
+            at = pl.ds(pl.multiple_of(block * BLOCK, BLOCK), BLOCK)
+            source = picked(normed, step)
+            gate_pre = project(source, gate[:, at])
+            up_pre = project(source, up[:, at])
+            chance = 1.0 / (1.0 + jnp.exp(-gate_pre))
+            silu = gate_pre * chance
+            put(active, at, (silu * up_pre).astype(BF16))
+            put(value.at[step], at, silu.astype(BF16))
+            raised = up_pre * chance * (1.0 + gate_pre * (1.0 - chance))
+            put(slope.at[step], at, raised.astype(BF16))
+
+        store(0, step).start()
+
+        @pl.when(step == 0)
+        def _():
+            fetches[3].wait()
+
+        @pl.loop(0, width // BLOCK)
+        def _(block):
+            at = pl.ds(pl.multiple_of(block * BLOCK, BLOCK), BLOCK)
+            product = project(whole(active), down[:, at]).astype(BF16)
+            for chunk in range(count):
+                partial[rows_of(chunk, step), at] = product[chunk * sub : (chunk + 1) * sub]
+
+        exchange(step)
+
+    @pl.loop(0, SUBS)
+    def _(step):
+        @pl.when(step == 0)
+        def _():
+            store(0, SUBS - 1).wait()
+            place_own.wait()
+
+        @pl.when(step > 0)
+        def _():
+            for which in (1, 2, 3):
+                store(which, step - 1).wait()
+
+        @pl.loop(0, hidden // BLOCK)
+        def _(block):
+            at = pl.ds(pl.multiple_of(block * BLOCK, BLOCK), BLOCK)
+            active_grad = project_back(picked(dy, step), down[at, :])
+            for chunk in range(count):
+                grad = active_grad[chunk * sub : (chunk + 1) * sub]
+                here = (grad * slope[step, chunk, :, at].astype(F32)).astype(BF16)
+                gate_grad[chunk, :, at] = here
+                here = (grad * value[step, chunk, :, at].astype(F32)).astype(BF16)
+                up_grad[chunk, :, at] = here
+
+        for which in (1, 2):
+            store(which, step).start()
+        exchange(SUBS + 2 * step)
+
+        @pl.loop(0, width // BLOCK)
+        def _(block):
+            at = pl.ds(pl.multiple_of(block * BLOCK, BLOCK), BLOCK)
+            total = project_back(whole(gate_grad), gate[at, :])
+            total = total + project_back(whole(up_grad), up[at, :])
+            put(back, at, total.astype(BF16))
+
+        store(3, step).start()
+        exchange(SUBS + 2 * step + 1)
+
+    keep = pltpu.make_async_copy(dy, full_ref, loads.at[0])
+    keep.start()
+
+    @pl.loop(3 * SUBS, pieces + count - 1)
+    def _(turn):
+        exchange(turn)
+
+    for which in (1, 2, 3):
+        store(which, SUBS - 1).wait()
+    keep.wait()
+    scatter.finish()
+    gather.finish(own_ref.at[gather.rows(0, 0)])
+
+
+def hidden_layer(normed, own, middle, w_gate, w_up, w_down, count, collective_id, pieces=8):
+    chunk_rows, width = own.shape
+    hidden = w_gate.shape[1]
+    rows = count * chunk_rows
+    sub = chunk_rows // SUBS
+    tall = jax.ShapeDtypeStruct((count, chunk_rows, hidden), BF16)
+    hbm = pl.BlockSpec(memory_space=pl.ANY)
+    outs = pl.pallas_call(
+        functools.partial(hidden_kernel, count, pieces),
+        out_shape=(
+            jax.ShapeDtypeStruct((rows, width), BF16), tall, tall, tall,
+            jax.ShapeDtypeStruct((count, chunk_rows, width), BF16),
+            jax.ShapeDtypeStruct((chunk_rows, width), BF16),
+        ),
+        in_specs=[hbm, hbm] + vmem_specs(1) + [hbm, hbm, hbm],
+        out_specs=(hbm, hbm, hbm, hbm, hbm, vmem_specs(1)[0]),
+        scratch_shapes=[
+            pltpu.VMEM((width, hidden), BF16),
+            pltpu.VMEM((width, hidden), BF16),
+            pltpu.VMEM((hidden, width), BF16),
+            pltpu.VMEM((rows, width), BF16),
+            pltpu.VMEM((rows, width), BF16),
+            pltpu.VMEM((count, sub, hidden), BF16),
+            pltpu.VMEM((SUBS, count, sub, hidden), BF16),
+            pltpu.VMEM((SUBS, count, sub, hidden), BF16),
+            pltpu.VMEM((count, sub, hidden), BF16),
+            pltpu.VMEM((count, sub, width), BF16),
+            pltpu.VMEM((rows, width), BF16),
+            pltpu.VMEM((landing_rows(count, chunk_rows), width), BF16),
+            copy_sems(count, pieces), copy_sems(count, pieces),
+            copy_sems(count, SUBS), copy_sems(count, SUBS),
+            pltpu.SemaphoreType.DMA((5,)), pltpu.SemaphoreType.DMA((4,)),
+        ],
+        compiler_params=params(collective_id=collective_id, has_side_effects=True),
+        cost_estimate=pl.CostEstimate(
+            flops=12 * rows * width * hidden, bytes_accessed=1 << 26, transcendentals=rows * hidden
+        ),
+        name="hidden_layer",
+    )(normed, own, middle, w_gate, w_up, w_down)
+    return [outs[0]] + [out.reshape(rows, out.shape[-1]) for out in outs[1:5]] + [outs[5]]
+
+
 def backward_turn_kernel(
     count, pieces, given_ref, dy_ref, middle_ref, gain_ref,
-    grad_ref, full_ref, gain_grad_ref,
-    partial, landing, rs_send, rs_receive, ag_send, ag_receive, load,
+    normed_full_ref, gate_grad_ref, up_grad_ref, active_ref, dy_full_ref,
+    grad_ref, full_ref, gain_grad_ref, sums_ref, traded_ref,
+    partial, landing, tiles, traded,
+    rs_send, rs_receive, ag_send, ag_receive, load, trade_send, trade_receive, fetches, stores,
 ):
     line = Line(count)
     chunk_rows = dy_ref.shape[0]
     fetch = pltpu.make_async_copy(given_ref, partial, load)
     fetch.start()
-    line.barrier()
+    replica = lax.axis_index("dp")
+    side = replica % 2
+    partner = replica + 1 - 2 * side
+    semaphore = pltpu.get_barrier_semaphore()
+    pl.semaphore_signal(semaphore, 1, device_id={"dp": partner})
+    pl.semaphore_wait(semaphore, line.greet(semaphore) + 1)
     fetch.wait()
     scatter = Scatter(line, partial, landing, rs_send, rs_receive, chunk_rows, pieces)
-    gather = Gather(line, full_ref, ag_send, ag_receive, chunk_rows, pieces)
+    gather = Gather(
+        line, full_ref, ag_send, ag_receive, chunk_rows, pieces, settle_lags(count)
+    )
     size = chunk_rows // pieces
     gain_grad_ref[...] = jnp.zeros_like(gain_grad_ref)
 
     def settle(piece):
-        scatter.arrived(piece)
-        local = pl.ds(piece * size, size)
-        total = scatter.total(piece)
-        middle = middle_ref[local, :]
-        grad, gain_grad = norm_back(total, middle, gain_ref[...])
+        local = pl.ds(pl.multiple_of(piece * size, size), size)
+        grad, gain_grad = norm_back(scatter.total(piece), middle_ref[local, :], gain_ref[...])
         grad = grad + dy_ref[local, :].astype(F32)
         gain_grad_ref[...] += gain_grad
         grad_ref[local, :] = grad
         full_ref[gather.rows(line.place, piece), :] = grad.astype(BF16)
         gather.start(piece)
 
-    pipeline(pieces, scatter.step, settle, gather.pass_on)
-    scatter.finish(pieces)
-    gather.finish(pieces)
+    block = traded.shape[0]
+    width = traded.shape[1]
+    products = (
+        (normed_full_ref, gate_grad_ref), (normed_full_ref, up_grad_ref), (active_ref, dy_full_ref),
+    )
+    halves = sums_ref.shape[0] // block
+    pairs = halves * len(products)
+    theirs = pl.ds(pl.multiple_of((1 - side) * block, block), block)
+    ours = pl.ds(pl.multiple_of(side * block, block), block)
+
+    def trade(pair):
+        return pltpu.make_async_remote_copy(
+            src_ref=tiles.at[pair % 2, theirs], dst_ref=traded_ref.at[pair],
+            send_sem=trade_send.at[pair], recv_sem=trade_receive.at[pair],
+            device_id={"dp": partner},
+        )
+
+    def bring(pair):
+        return pltpu.make_async_copy(traded_ref.at[pair], traded, fetches)
+
+    def put(pair):
+        rows = pl.ds(pl.multiple_of((pair % halves) * block, block), block)
+        columns = pl.ds(pl.multiple_of((pair // halves) * width, width), width)
+        return pltpu.make_async_copy(
+            tiles.at[pair % 2, ours], sums_ref.at[rows, columns], stores.at[pair % 2]
+        )
+
+    def beside(pair):
+        @pl.when((pair >= 2) & (pair < pairs))
+        def _():
+            trade(pair - 2).wait_send()
+            put(pair - 2).wait()
+
+        @pl.when((pair >= 1) & (pair <= pairs))
+        def _():
+            trade(pair - 1).wait_recv()
+            bring(pair - 1).start()
+
+        at = pl.ds(pl.multiple_of((pair % halves) * 2 * block, 2 * block), 2 * block)
+        for which, (left, right) in enumerate(products):
+            @pl.when(pair // halves == which)
+            def _(left=left, right=right):
+                tiles[pair % 2] = row_contract(left[:, at], right[...]).astype(BF16)
+
+        @pl.when(pair < pairs)
+        def _():
+            trade(pair).start()
+
+        @pl.when((pair >= 1) & (pair <= pairs))
+        def _():
+            bring(pair - 1).wait()
+            slot = (pair - 1) % 2
+            kept = tiles[slot, ours].astype(F32) + traded[...].astype(F32)
+            tiles[slot, ours] = kept.astype(BF16)
+            put(pair - 1).start()
+
+    turns = pieces + 2 * (count - 1)
+
+    @pl.loop(0, max(turns, pairs + 1))
+    def _(turn):
+        scatter.turn(turn)
+        gather.turn(turn)
+        scatter.settle(turn, settle)
+        beside(turn)
+
+    for pair in range(pairs - 2, pairs):
+        trade(pair).wait_send()
+        put(pair).wait()
+    scatter.finish()
+    gather.finish()
 
 
 def norm_back(grad, rows, gain):
@@ -571,90 +972,183 @@
     return inverse * scaled - rows * common, gain_grad
 
 
-def backward_turn(given, dy, middle, gain, count, collective_id, pieces=4):
+def backward_turn(
+    given, dy, middle, gain, normed_full, gate_grad, up_grad, active, dy_full,
+    count, replicas, collective_id, pieces=8,
+):
     chunk_rows, width = dy.shape
     rows = count * chunk_rows
+    block = width // replicas
+    kept_rows = width // 2
+    pairs = 3 * kept_rows // block
+    hbm = pl.BlockSpec(memory_space=pl.ANY)
     return pl.pallas_call(
         functools.partial(backward_turn_kernel, count, pieces),
         out_shape=(
             jax.ShapeDtypeStruct((chunk_rows, width), F32),
             jax.ShapeDtypeStruct((rows, width), BF16),
             jax.ShapeDtypeStruct((1, width), F32),
+            jax.ShapeDtypeStruct((kept_rows, 3 * width), BF16),
+            jax.ShapeDtypeStruct((pairs, block, width), BF16),
         ),
-        in_specs=[pl.BlockSpec(memory_space=pl.ANY)] + vmem_specs(3),
+        in_specs=[hbm] + vmem_specs(8),
+        out_specs=tuple(vmem_specs(3)) + (hbm, hbm),
+        scratch_shapes=[
+            pltpu.VMEM((rows, width), BF16),
+            pltpu.VMEM((landing_rows(count, chunk_rows), width), BF16),
+            pltpu.VMEM((2, 2 * block, width), BF16),
+            pltpu.VMEM((block, width), BF16),
+        ]
+        + [copy_sems(count, pieces)] * 4
+        + [
+            pltpu.SemaphoreType.DMA,
+            pltpu.SemaphoreType.DMA((pairs,)),
+            pltpu.SemaphoreType.DMA((pairs,)),
+            pltpu.SemaphoreType.DMA,
+            pltpu.SemaphoreType.DMA((2,)),
+        ],
+        compiler_params=params(collective_id=collective_id, has_side_effects=True),
+        cost_estimate=pl.CostEstimate(
+            flops=6 * rows * width * width, bytes_accessed=1 << 26, transcendentals=0
+        ),
+        name="backward_turn",
+    )(given, dy, middle, gain, normed_full, gate_grad, up_grad, active, dy_full)
+
+
+def last_turn_kernel(
+    count, pieces, replicas, dqkv_ref, w_ref, normed_ref, middle_grad_ref, x_ref, gain_ref, gain_two_ref,
+    grad_ref, weight_grad_ref, gains_ref,
+    partial, landing, sums, traded, arrived, pair_sems, sends, receives,
+    gain_own, gain_row, gain_land, gain_line,
+    rs_send, rs_receive, dp_send, dp_receive, line_send, line_receive,
+):
+    line = Line(count)
+    chunk_rows = x_ref.shape[0]
+    width = dqkv_ref.shape[1]
+    replica = lax.axis_index("dp")
+    semaphore = pltpu.get_barrier_semaphore()
+    for step in range(1, replicas):
+        pl.semaphore_signal(semaphore, 1, device_id={"dp": (replica + step) % replicas})
+    for step in range(1, count):
+        pl.semaphore_signal(semaphore, 1, device_id={"tensor": (line.place + step) % count})
+    pl.semaphore_wait(semaphore, replicas - 1 + count - 1)
+    fold = Fold(replicas, sums, traded, arrived, pair_sems, sends, receives)
+
+    @pl.loop(0, partial.shape[0] // SPAN)
+    def _(step):
+        rows = pl.ds(pl.multiple_of(step * SPAN, SPAN), SPAN)
+        partial[rows, :] = project_back(dqkv_ref[rows, :], w_ref[:, :width]).astype(BF16)
+
+    scatter = Scatter(line, partial, landing, rs_send, rs_receive, chunk_rows, pieces)
+    size = chunk_rows // pieces
+    gain_own[...] = jnp.zeros_like(gain_own)
+
+    def settle(piece):
+        local = pl.ds(pl.multiple_of(piece * size, size), size)
+        total = scatter.total(piece)
+        grad, gain_grad = norm_back(total, x_ref[local, :].astype(F32), gain_ref[...])
+        gain_own[...] += gain_grad
+        grad_ref[local, :] = (grad + middle_grad_ref[local, :]).astype(BF16)
+
+    block = sums.shape[2]
+
+    @pl.loop(0, pieces + count - 1)
+    def _(turn):
+        scatter.turn(turn)
+        scatter.settle(turn, settle)
+
+        @pl.when(turn == 0)
+        def _():
+            @pl.loop(0, replicas // 2)
+            def _(half):
+                at = pl.ds(pl.multiple_of(half * 2 * block, 2 * block), 2 * block)
+                product = row_contract(normed_ref[:, at], dqkv_ref[...]).astype(BF16)
+                for side in range(2):
+                    sums[half, side] = product[side * block : (side + 1) * block]
+
+            fold.pair().start()
+
+        @pl.when(turn == 2)
+        def _():
+            fold.spread()
+
+    gain_row[0:1, :] = gain_own[...]
+    gain_row[1:2, :] = gain_two_ref[...]
+
+    def share(peer, landing):
+        return pltpu.make_async_remote_copy(
+            src_ref=gain_row, dst_ref=gain_land.at[landing],
+            send_sem=dp_send.at[peer], recv_sem=dp_receive.at[landing], device_id={"dp": peer},
+        )
+
+    def pass_line(peer, landing):
+        return pltpu.make_async_remote_copy(
+            src_ref=gains_ref, dst_ref=gain_line.at[landing],
+            send_sem=line_send.at[peer], recv_sem=line_receive.at[landing],
+            device_id={"tensor": peer},
+        )
+
+    peers = [(replica + step) % replicas for step in range(1, replicas)]
+    places = [(line.place + step) % count for step in range(1, count)]
+    for peer in peers:
+        share(peer, replica).start()
+    weight_grad_ref[...] = fold.total()
+    total = gain_row[...]
+    for peer in peers:
+        share(peer, peer).wait_recv()
+        total = total + gain_land[peer]
+    gains_ref[...] = total
+    for peer in places:
+        pass_line(peer, line.place).start()
+    scatter.finish()
+    fold.finish()
+    for peer in peers:
+        share(peer, replica).wait_send()
+    for peer in places:
+        pass_line(peer, peer).wait_recv()
+        total = total + gain_line[peer]
+    for peer in places:
+        pass_line(peer, line.place).wait_send()
+    gains_ref[...] = total
+
+
+def last_turn(
+    dqkv, w_qkv, normed, middle_grad, x, gain, gain_two_grad, count, replicas, collective_id,
+    pieces=8,
+):
+    chunk_rows, width = x.shape
+    rows = count * chunk_rows
+    block = width // replicas
+    return pl.pallas_call(
+        functools.partial(last_turn_kernel, count, pieces, replicas),
+        out_shape=(
+            jax.ShapeDtypeStruct((chunk_rows, width), BF16),
+            jax.ShapeDtypeStruct((block, dqkv.shape[1]), F32),
+            jax.ShapeDtypeStruct((2, width), F32),
+        ),
+        in_specs=vmem_specs(7),
         out_specs=tuple(vmem_specs(3)),
         scratch_shapes=[
             pltpu.VMEM((rows, width), BF16),
-            pltpu.VMEM((2, rows, width), BF16),
+            pltpu.VMEM((landing_rows(count, chunk_rows), width), BF16),
         ]
-        + [copy_sems(count, pieces)] * 4
-        + [pltpu.SemaphoreType.DMA],
+        + fold_scratch(replicas, block, dqkv.shape[1])
+        + [
+            pltpu.VMEM((1, width), F32),
+            pltpu.VMEM((2, width), F32),
+            pltpu.VMEM((replicas, 2, width), F32),
+            pltpu.VMEM((count, 2, width), F32),
+        ]
+        + [copy_sems(count, pieces)] * 2
+        + [pltpu.SemaphoreType.DMA((replicas,))] * 2
+        + [pltpu.SemaphoreType.DMA((count,))] * 2,
         compiler_params=params(collective_id=collective_id, has_side_effects=True),
         cost_estimate=pl.CostEstimate(
-            flops=0, bytes_accessed=300 * chunk_rows * width, transcendentals=0
-        ),
-        name="backward_turn",
-    )(given, dy, middle, gain)
-
-
-def last_turn_kernel(
-    count, pieces, dqkv_ref, w_ref, middle_grad_ref, x_ref, gain_ref,
-    grad_ref, gain_grad_ref,
-    partial, landing, rs_send, rs_receive,
-):
-    line = Line(count)
-    chunk_rows = x_ref.shape[0]
-    line.barrier()
-    width = dqkv_ref.shape[1]
-
-    @pl.loop(0, partial.shape[0] // SPAN)
-    def _(step):
-        rows = pl.ds(step * SPAN, SPAN)
-        partial[rows, :] = project_back(dqkv_ref[rows, :], w_ref[:, :width]).astype(BF16)
-
-    scatter = Scatter(line, partial, landing, rs_send, rs_receive, chunk_rows, pieces)
-    size = chunk_rows // pieces
-    gain_grad_ref[...] = jnp.zeros_like(gain_grad_ref)
-
-    def settle(piece):
-        scatter.arrived(piece)
-        local = pl.ds(piece * size, size)
-        total = scatter.total(piece)
-        grad, gain_grad = norm_back(total, x_ref[local, :].astype(F32), gain_ref[...])
-        gain_grad_ref[...] += gain_grad
-        grad_ref[local, :] = (grad + middle_grad_ref[local, :]).astype(BF16)
-
-    pipeline(pieces, scatter.step, settle, lambda piece: None)
-    scatter.finish(pieces)
-
-
-def last_turn(dqkv, w_qkv, middle_grad, x, gain, count, collective_id, pieces=4):
-    chunk_rows, width = x.shape
-    rows = count * chunk_rows
-    return pl.pallas_call(
-        functools.partial(last_turn_kernel, count, pieces),
-        out_shape=(
-            jax.ShapeDtypeStruct((chunk_rows, width), BF16),
-            jax.ShapeDtypeStruct((1, width), F32),
-        ),
-        in_specs=vmem_specs(5),
-        out_specs=tuple(vmem_specs(2)),
-        scratch_shapes=[
-            pltpu.VMEM((rows, width), BF16),
-            pltpu.VMEM((2, rows, width), BF16),
-        ]
-        + [copy_sems(count, pieces)] * 2,
-        compiler_params=params(collective_id=collective_id, has_side_effects=True),
-        cost_estimate=pl.CostEstimate(
-            flops=2 * rows * width * dqkv.shape[1],
+            flops=4 * rows * width * dqkv.shape[1],
             bytes_accessed=200 * chunk_rows * width, transcendentals=0,
         ),
         name="last_turn",
-    )(dqkv, w_qkv, middle_grad, x, gain)
-
-
-def scatter_sum(grad, axis):
-    return lax.psum_scatter(grad.astype(BF16), axis, scatter_dimension=0, tiled=True)
+    )(dqkv, w_qkv, normed, middle_grad, x, gain, gain_two_grad)
 
 
 def shards(
@@ -678,7 +1172,6 @@
     gate_full = lax.all_gather(w_gate, "dp", axis=0, tiled=True)
     up_full = lax.all_gather(w_up, "dp", axis=0, tiled=True)
     down_full = lax.all_gather(w_down, "dp", axis=0, tiled=True)
-    grad_full = lax.all_gather(cotangent, "tensor", axis=0, tiled=True)
     gain_rows = jnp.transpose(qkv_full[:, qkv_width : qkv_width + 2].astype(F32))
     gain_one, gain_two = gain_rows[0:1], gain_rows[1:2]
 
@@ -686,48 +1179,30 @@
     normed_full, queries, keys, values, mixed, lse = attend(
         x_full, qkv_full, gain_one, cosine, sine, start[:, None], q_width, kv_width
     )
+    replicas = lax.axis_size("dp")
     middle, normed_two_full = forward_turn(mixed, out_full, inputs, gain_two, count, 1)
-
-    gate_pre = project(normed_two_full, gate_full)
-    up_pre = project(normed_two_full, up_full)
-    active_f, active_back = jax.vjp(
-        lambda gate_in, up_in: jax.nn.silu(gate_in) * up_in, gate_pre, up_pre
+    grad_full, active, gate_grad, up_grad, norm_two_grad, outputs = hidden_layer(
+        normed_two_full, cotangent, middle, gate_full, up_full, down_full, count, 4
     )
-    active = active_f.astype(BF16)
-    outputs = (
-        middle
-        + lax.psum_scatter(
-            project(active, down_full).astype(BF16), "tensor", scatter_dimension=0, tiled=True
-        ).astype(F32)
-    ).astype(BF16)
-    active_grad = project_back(grad_full, down_full)
-    gate_grad_f, up_grad_f = active_back(active_grad)
-    gate_grad = gate_grad_f.astype(BF16)
-    up_grad = up_grad_f.astype(BF16)
-    down_grad = scatter_sum(row_contract(active, grad_full), "dp")
-    gate_weight_grad = scatter_sum(row_contract(normed_two_full, gate_grad), "dp")
-    up_weight_grad = scatter_sum(row_contract(normed_two_full, up_grad), "dp")
-    norm_two_grad = (project_back(gate_grad, gate_full) + project_back(up_grad, up_full)).astype(
-        BF16
+    middle_grad, branch_full, gain_two_grad, sums, _ = backward_turn(
+        norm_two_grad, cotangent, middle, gain_two, normed_two_full, gate_grad, up_grad, active,
+        grad_full, count, replicas, 2,
     )
-    middle_grad, branch_full, gain_two_grad = backward_turn(
-        norm_two_grad, cotangent, middle, gain_two, count, 2
+    sides = [list(range(side, replicas, 2)) for side in range(2)]
+    hidden_grads = lax.psum_scatter(
+        sums, "dp", scatter_dimension=0, axis_index_groups=sides, tiled=True
+    ).astype(F32)
+    gate_weight_grad, up_weight_grad, down_grad = jnp.split(hidden_grads, 3, axis=1)
+    dqkv, out_grad = attend_back(
+        branch_full, out_full, mixed, queries, keys, values, lse, cosine, sine, start[None, :],
+        replicas, 5,
     )
-    dqkv = attend_back(
-        branch_full, out_full, queries, keys, values, lse, cosine, sine, start[None, :]
+    input_grad, qkv_grad, gains_grad = last_turn(
+        dqkv, qkv_full, normed_full, middle_grad, inputs, gain_one, gain_two_grad,
+        count, replicas, 3,
     )
-    out_grad = scatter_sum(row_contract(mixed, branch_full), "dp")
-    qkv_grad = scatter_sum(row_contract(normed_full, dqkv), "dp").astype(F32)
-    input_grad, gain_one_grad = last_turn(
-        dqkv, qkv_full, middle_grad, inputs, gain_one, count, 3
-    )
-    gains_grad = lax.psum(
-        lax.psum_scatter(
-            jnp.concatenate([gain_one_grad, gain_two_grad], axis=0), "dp",
-            scatter_dimension=1, tiled=True,
-        ),
-        "tensor",
-    )
+    own = attn_gain.shape[0]
+    gains_grad = lax.dynamic_slice_in_dim(gains_grad, lax.axis_index("dp") * own, own, axis=1)
     return (
         outputs,
         input_grad,
@@ -735,11 +1210,11 @@
         qkv_grad[:, :q_width],
         qkv_grad[:, q_width : q_width + kv_width],
         qkv_grad[:, q_width + kv_width :],
-        out_grad.astype(F32),
+        out_grad,
         gains_grad[1],
-        gate_weight_grad.astype(F32),
-        up_weight_grad.astype(F32),
-        down_grad.astype(F32),
+        gate_weight_grad,
+        up_weight_grad,
+        down_grad,
     )
 
 

time: 1140 us -> 679 us (0.60); the launches traced: 1130 us -> 678 us
  waiting for transfers between devices: 346 us -> 12.7 us
  matrix products: 146 us -> 0 us
  Pallas kernels: 565 us -> 613 us
  other arithmetic: 23.4 us -> 10.1 us
    reduce_scatter x6 -> x1, waiting for transfers between devices: 343 us -> 10.2 us  [shards(): lax.psum_scatter(sums, 'dp', scatter_dimension=0, axis_index_groups=sides...]
    dot_general x11 -> x0, matrix products: 146 us -> none  [the longest x5 55.7 us: row_contract(): lax.dot_general(left, right, (((0,), (0,)), ((), ())), preferred_element_...]
    pallas_call x2 -> x3, Pallas kernels: 111 us -> 251 us  [the longest x1 119 us: hidden_layer(): pl.pallas_call(functools.partial(hidden_kernel, count, pieces), out_shape...]
    pallas_call x1, Pallas kernels: 217 us -> 126 us  [forward_turn(): pl.pallas_call(functools.partial(forward_turn_kernel, count, pieces), out...]
    convert_element_type x5 -> x0, other arithmetic: 12.6 us -> none  [the longest x1 2.79 us: shards(): gate_weight_grad.astype(F32)]
  transfers between devices with their start and end apart: 13 -> 6, of which waited for: 6 -> 1; matrix products, arithmetic and copies ran while one was open for 12% -> 3% of each run, Pallas kernels for 28% -> 53%
where the time goes in v2:
time: 679 us; the launch traced here: 678 us
  Pallas kernels  613 us (90%)
  local copies, waits for them, and re-layouts  23.5 us (3%)
  between operations  18.2 us (3%)
  waiting for transfers between devices  12.7 us (2%)
  other arithmetic  10.1 us (1%)
    pallas_call x1, Pallas kernels, backward_turn(): pl.pallas_call(functools.partial(backward_turn_kernel, count, pieces), ou...  133 us
    pallas_call x1, Pallas kernels, forward_turn(): pl.pallas_call(functools.partial(forward_turn_kernel, count, pieces), out...  126 us
    pallas_call x1, Pallas kernels, hidden_layer(): pl.pallas_call(functools.partial(hidden_kernel, count, pieces), out_shape...  119 us
    pallas_call x1, Pallas kernels, last_turn(): pl.pallas_call(functools.partial(last_turn_kernel, count, pieces, replica...  94.7 us
    pallas_call x1, Pallas kernels, line_gather(): pl.pallas_call(functools.partial(gather_kernel, count, pieces), out_shape...  75 us
    pallas_call x1, Pallas kernels, attend_back(): pl.pallas_call(functools.partial(attend_back_kernel, replicas), out_shape...  37.3 us
    pallas_call x1, Pallas kernels, attend(): pl.pallas_call(attend_kernel, out_shape=(jax.ShapeDtypeStruct(x_full.shap...  28.7 us
  transfers between devices with their start and end apart: 6, of which 1 were waited for; matrix products, arithmetic and copies ran while one was open for 3% of the time, Pallas kernels for 53%

profile of v2, /device:TPU:0, one launch (start us, length us, event | category | flops | bytes accessed | tf_op | source)
XLA Modules:
  0.0 678.2 jit_solution(4478022869057461395)
XLA Ops:
  7.2 0.7 stack.10
  7.9 0.7 stack.9
  8.5 0.9 copy.27
  9.5 0.9 copy.26
  10.4 1.1 copy.25
  11.5 0.8 pad_maximum_fusion
  12.4 0.7 all-gather.8.cloned.1.call-update
  13.2 0.7 all-gather.10.cloned.1.call-update
  15.1 75.0 %line_gather.1.x_ref = bf16[1024,2048]{1,0:T(8,128)(2,1)} custom-call(bf16[256,2048]{1,0:T(8,128)(2,1)} %x_ref.5), custom_call_target="tpu_custom_call" | custom-call | bytes 104857600 | tf_op jit(solution)/shard_map/line_gather/pallas_call | solution.py:593
  90.1 0.6 fusion.4
  93.3 1.3 fusion.7
  94.6 1.9 fusion.8
  98.0 0.9 select_select_fusion.start_ref
  98.8 3.1 negate_select_fusion
  101.9 6.1 copy.28.w_ref
  108.0 0.8 convert_bitcast_fusion
  108.8 0.6 fusion.13
  109.4 28.7 %attend.1 = (bf16[1024,2048]{1,0:T(8,128)(2,1)}, bf16[1024,512]{1,0:T(8,128)(2,1)}, bf16[2,1024,128]{2,1,0:T(8,128)(2,1)}, bf16[2,1024,128]{2,1,0:T(8,128)(2,1)}...) custom-call(bf16[1024,2048]{1,0:T(8,128)(2,1)} %line_gather.1.x_ref, bf16[2048,896]{1,0:T(8,128)(2,1)} %copy.28.w_ref, ...), custom_call_target="tpu_custom_call" | custom-call | flops 7516192768 | bytes 16777216 | tf_op jit(solution)/shard_map/attend/pallas_call | solution.py:178
  138.1 125.8 %forward_turn.1 = (f32[256,2048]{1,0:T(8,128)}, bf16[1024,2048]{1,0:T(8,128)(2,1)}) custom-call(bf16[1024,512]{1,0:T(8,128)(2,1)} %get-tuple-element.34.mixed_ref, bf16[512,2048]{1,0:T(8,128)(2,1)} %all-gather.8.cloned.1.call-done.w_ref, bf16[256,2048]{1,0:T(8,128)(2,1)} %x_ref.5, f32[1,2048]{1,0:T(1,128)} %get-tuple-element.70.gain_ref), custom_call_target="tpu_custom_call" | custom-call | flops 2147483648 | bytes 157286400 | tf_op jit(solution)/shard_map/forward_turn/pallas_call | solution.py:650
  264.0 118.6 %hidden_layer.1 = (bf16[1024,2048]{1,0:T(8,128)(2,1)}, bf16[4,256,2048]{2,1,0:T(8,128)(2,1)}, bf16[4,256,2048]{2,1,0:T(8,128)(2,1)}, bf16[4,256,2048]{2,1,0:T(8,...) custom-call(bf16[1024,2048]{1,0:T(8,128)(2,1)} %get-tuple-element.35.normed_ref.normed_full_ref, ...), custom_call_target="tpu_custom_call" | custom-call | flops 51539607552 | bytes 67108864 | tf_op jit(solution)/shard_map/hidden_layer/pallas_call | solution.py:826
  382.7 133.3 %backward_turn.1 = (f32[256,2048]{1,0:T(8,128)}, bf16[1024,2048]{1,0:T(8,128)(2,1)}, f32[1,2048]{1,0:T(1,128)}, bf16[1024,6144]{1,0:T(8,128)(2,1)}, bf16[12,256,2048]{2,1,0:T(8,128)(2,1)}) custom-call(bf16[1024,2048]{1,0:T(8,128)(2,1)} %bitcast.13, bf16[256,2048]{1,0:T(8,128)(2,1)} %dy_ref.1, f32[256,2048]{1,0:T(8,128)} %get-tuple-element.36.middle_ref, ...), custom_call_target="tpu_custom_call" | custom-call | flops 25769803776 | bytes 67108864 | tf_op jit(solution)/shard_map/backward_turn/pallas_call | solution.py:985
  516.0 0.6 compare_select_fusion.1.start_ref
  516.6 37.3 %attend_back.1 = (bf16[1024,768]{1,0:T(8,128)(2,1)}, f32[64,2048]{1,0:T(8,128)}) custom-call(bf16[1024,2048]{1,0:T(8,128)(2,1)} %get-tuple-element.43.branch_ref, bf16[512,2048]{1,0:T(8,128)(2,1)} %all-gather.8.cloned.1.call-done.w_ref, bf16[1024,512]{1,0:T(8,128)(2,1)} %get-tuple-element.34.mixed_ref, bf16[1024,512]{1,0:T(8,128)(2,1)} %get-tuple-element.44.q_ref, ...), custom_call_target="tpu_custom_call" | custom-call | flops 12884901888 | bytes 16777216 | tf_op jit(solution)/shard_map/attend_back/pallas_call | solution.py:538
  554.0 94.7 %last_turn.1 = (bf16[256,2048]{1,0:T(8,128)(2,1)}, f32[256,768]{1,0:T(8,128)}, f32[2,2048]{1,0:T(2,128)}) custom-call(bf16[1024,768]{1,0:T(8,128)(2,1)} %get-tuple-element.48.dqkv_ref, bf16[2048,896]{1,0:T(8,128)(2,1)} %copy.28.w_ref, bf16[1024,2048]{1,0:T(8,128)(2,1)} %get-tuple-element.49.normed_ref, f32[256,2048]{1,0:T(8,128)} %get-tuple-element.50.middle_grad_ref, ...), custom_call_target="tpu_custom_call" | custom-call | flops 6442450944 | bytes 104857600 | tf_op jit(solution)/shard_map/last_turn/pallas_call | solution.py:1122
  648.6 1.9 slice.28
  650.5 1.4 fusion.12
  651.9 1.7 fusion.11
  653.6 10.2 %reduce-scatter.2.cloned.1.call-done = bf16[256,6144]{1,0:T(8,128)(2,1)} async-done(((bf16[1024,6144]{1,0:T(8,128)(2,1)}), bf16[256,6144]{1,0:T(8,128)(2,1)}) %reduce-scatter.2.cloned.1.call-update) | async-done | bytes 3145744 | tf_op jit(solution)/shard_map/reduce_scatter | solution.py:1192
  663.8 4.8 fusion.10
  668.6 1.0 copy.33
  669.6 1.0 copy.34
  670.5 0.8 copy.35
  (32 shorter events, 1.5 us)
Async XLA Ops:
  7.2 94.7 %all-gather.6.cloned.1.call-start = ((), (), s32[]{:S(2)}) async-start(), calls=%async_computation.1 | async-start | bytes 4128768 | tf_op jit(solution)/shard_map/all_gather | solution.py:1170
  12.4 125.7 %all-gather.8.cloned.1.call-start = ((), (), s32[]{:S(2)}) async-start(), calls=%async_computation.2 | async-start | bytes 2359296 | tf_op jit(solution)/shard_map/all_gather | solution.py:1171
  13.1 250.8 %all-gather.10.cloned.1.call-start = ((), (), s32[]{:S(2)}) async-start(), calls=%async_computation.3 | async-start | bytes 9437184 | tf_op jit(solution)/shard_map/all_gather | solution.py:1172
  13.8 76.2 %copy-start.3 = (s32[9]{0:T(128)S(1)}, s32[9]{0:T(128)}, u32[]{:S(2)}) copy-start(s32[9]{0:T(128)} %param.27) | copy-start | bytes 112
  13.9 79.5 %copy-start.4 = (s32[12]{0:T(128)S(1)}, s32[12]{0:T(128)}, u32[]{:S(2)}) copy-start(s32[12]{0:T(128)} %param.26) | copy-start | bytes 148
  13.9 80.7 %copy-start.5 = (s32[12]{0:T(128)S(1)}, s32[12]{0:T(128)}, u32[]{:S(2)}) copy-start(s32[12]{0:T(128)} %param.25) | copy-start | bytes 148
  13.9 250.1 %all-gather.12.cloned.1.call-start = ((), (), s32[]{:S(2)}) async-start(), calls=%async_computation.4 | async-start | bytes 9437184 | tf_op jit(solution)/shard_map/all_gather | solution.py:1173
  14.5 249.5 %all-gather.14.cloned.1.call-start = ((), (), s32[]{:S(2)}) async-start(), calls=%async_computation.5 | async-start | bytes 9437184 | tf_op jit(solution)/shard_map/all_gather | solution.py:1174
  15.0 648.7 %reduce-scatter.2.cloned.1.call-start = ((), (), s32[]{:S(2)}) async-start(), calls=%async_computation.6 | async-start | bytes 15728640 | tf_op jit(solution)/shard_map/reduce_scatter | solution.py:1192
  653.6 15.0 %copy-start = (bf16[256,2048]{1,0:T(8,128)(2,1)S(1)}, bf16[256,2048]{1,0:T(8,128)(2,1)}, u32[]{:S(2)}) copy-start(bf16[256,2048]{1,0:T(8,128)(2,1)} %get-tuple-element.85) | copy-start | bytes 3145732
  653.6 16.0 %copy-start.1 = (bf16[256,2048]{1,0:T(8,128)(2,1)S(1)}, bf16[256,2048]{1,0:T(8,128)(2,1)}, u32[]{:S(2)}) copy-start(bf16[256,2048]{1,0:T(8,128)(2,1)} %get-tuple-element.86) | copy-start | bytes 3145732
  668.6 2.0 copy-start.2
Sparse Core Ops, SparseCore 0:
  12.5 37.7 all-gather.5
  52.2 27.7 all-gather.7
  81.9 54.2 all-gather.9
  137.9 54.2 all-gather.11
  193.9 54.2 all-gather.13
  516.1 147.5 reduce-scatter.1

commit v3 on v2

--- a/solution.py
+++ b/solution.py
@@ -12,6 +12,7 @@
 MOST_SEQS = 2
 SLAB = 128
 SPAN = 256
+GAIN_ROWS = 16
 
 norm_epsilon = 1e-05
 rope_theta = 500000.0
@@ -26,9 +27,10 @@
 VMEM_LIMIT = 60 * 1024 * 1024
 
 
-def rotary_freqs(head_size):
-    exponents = jnp.arange(0, head_size, 2).astype(jnp.float32) / head_size
-    inverse = 1.0 / jnp.power(jnp.float32(rope_theta), exponents)
+def rotary_freqs():
+    half = HEAD_SIZE // 2
+    index = jnp.tile(jnp.arange(half, dtype=jnp.float32), SLAB // half)
+    inverse = 1.0 / jnp.power(jnp.float32(rope_theta), 2.0 * index / HEAD_SIZE)
     wavelength = 2.0 * math.pi / inverse
     smooth = (context_span / wavelength - low_factor) / (high_factor - low_factor)
     blended = (1.0 - smooth) * inverse / rope_factor + smooth * inverse
@@ -36,31 +38,17 @@
     return jnp.where(wavelength < context_span / high_factor, inverse, scaled)
 
 
-def slab_tables(positions):
-    freqs = rotary_freqs(HEAD_SIZE)
-    freqs = jnp.concatenate([freqs] * 4)
-    angles = positions.astype(jnp.float32)[:, None] * freqs[None, :]
-    low_half = (jnp.arange(SLAB) % HEAD_SIZE) < HEAD_SIZE // 2
-    sines = jnp.sin(angles)
-    return jnp.cos(angles), jnp.where(low_half[None, :], -sines, sines)
-
-
-def group_layout(seq_lengths, group_perm, group_starts, group_id, row_total, slot_total):
-    bounds = jnp.arange(group_starts.shape[0], dtype=jnp.int32)
-    numbers = jnp.arange(group_perm.shape[0], dtype=jnp.int32)
-    opening = jnp.sum(jnp.where(bounds == group_id, group_starts, 0))
-    closing = jnp.sum(jnp.where(bounds == group_id + 1, group_starts, 0))
-    row_ids = jnp.arange(row_total, dtype=jnp.int32)
-    offset = jnp.zeros((row_total,), jnp.int32)
-    finish = jnp.zeros((), jnp.int32)
-    for slot_id in range(slot_total):
-        slot_place = opening + slot_id
-        sequence = jnp.sum(jnp.where(numbers == slot_place, group_perm, 0))
-        length = jnp.sum(jnp.where(numbers == sequence, seq_lengths, 0))
-        length = jnp.where(slot_place < closing, length, 0)
-        finish = finish + length
-        offset = jnp.where(row_ids >= finish, finish, offset)
-    return offset, row_ids - offset
+def segment_starts(lengths_ref, perm_ref, starts_ref, rows):
+    group = lax.axis_index("dp")
+    opening, closing = starts_ref[group], starts_ref[group + 1]
+    finish = jnp.int32(0)
+    start = jnp.zeros_like(rows)
+    for slot in range(MOST_SEQS):
+        place = opening + slot
+        sequence = perm_ref[jnp.minimum(place, perm_ref.shape[0] - 1)]
+        finish = finish + jnp.where(place < closing, lengths_ref[sequence], 0)
+        start = jnp.where(rows >= finish, finish, start)
+    return start
 
 
 def project(left, right):
@@ -106,10 +94,25 @@
     return [pl.BlockSpec(memory_space=pltpu.VMEM)] * count
 
 
+def weight_fetches(packed, target, sems):
+    rows = target.shape[0] // packed.shape[0]
+    return [
+        pltpu.make_async_copy(
+            packed.at[block, :rows], target.at[block * rows : (block + 1) * rows], sems.at[block]
+        )
+        for block in range(packed.shape[0])
+    ]
+
+
 def attend_kernel(
-    x_ref, w_ref, gain_ref, cos_ref, sin_ref, start_ref,
-    normed_ref, q_ref, k_ref, v_ref, mixed_ref, lse_ref, bias_ref, stat_ref,
+    x_ref, packed_ref, gain_ref, cos_ref, sin_ref, start_ref,
+    normed_ref, q_ref, k_ref, v_ref, mixed_ref, lse_ref, bias_ref, stat_ref, w_ref, sems,
 ):
+    fetches = weight_fetches(packed_ref, w_ref, sems)
+    for fetch in fetches:
+        fetch.start()
+    for fetch in fetches:
+        fetch.wait()
     rows_all = x_ref.shape[0]
     q_width = q_ref.shape[1]
     kv_slabs = v_ref.shape[0] // 2
@@ -123,7 +126,7 @@
         inverse = lax.rsqrt(jnp.mean(x * x, axis=-1, keepdims=True) + norm_epsilon)
         normed = (x * inverse * gain_ref[...]).astype(BF16)
         normed_ref[rows, :] = normed
-        pre = project(normed, w_ref[:, : q_width + 2 * kv_slabs * SLAB])
+        pre = project(normed, w_ref[...])
         cosine, sine = cos_ref[rows, :], sin_ref[rows, :]
         for slab in range(slabs):
             part = pre[:, slab * SLAB : (slab + 1) * SLAB]
@@ -185,9 +188,14 @@
             jax.ShapeDtypeStruct((rows, q_width), BF16),
             jax.ShapeDtypeStruct((q_width // HEAD_SIZE, rows), F32),
         ),
-        in_specs=vmem_specs(6),
+        in_specs=vmem_specs(1) + [pl.BlockSpec(memory_space=pl.ANY)] + vmem_specs(4),
         out_specs=tuple(vmem_specs(6)),
-        scratch_shapes=[pltpu.VMEM((SPAN, rows), F32), pltpu.VMEM((rows, SLAB), F32)],
+        scratch_shapes=[
+            pltpu.VMEM((SPAN, rows), F32),
+            pltpu.VMEM((rows, SLAB), F32),
+            pltpu.VMEM((x_full.shape[1], w_qkv.shape[2]), BF16),
+            pltpu.SemaphoreType.DMA((w_qkv.shape[0],)),
+        ],
         compiler_params=params(),
         cost_estimate=pl.CostEstimate(flops=flops, bytes_accessed=1 << 24, transcendentals=1 << 23),
         name="attend",
@@ -227,10 +235,10 @@
 
 
 class Gather:
-    def __init__(self, line, full, send, receive, chunk_rows, pieces, lags=None):
+    def __init__(self, line, full, send, receive, chunk_rows, pieces, lags=None, stride=1):
         self.line, self.full, self.send, self.receive = line, full, send, receive
         self.chunk_rows, self.size, self.pieces = chunk_rows, chunk_rows // pieces, pieces
-        self.lags = lags or [0] * line.count
+        self.lags, self.stride = lags or [0] * line.count, stride
 
     def rows(self, chunk, piece):
         start = chunk * self.chunk_rows + piece * self.size
@@ -254,9 +262,11 @@
         for chunk in range(line.count):
             for way in (0, 1):
                 hop = line.place - chunk if way == 0 else chunk - line.place
-                piece = turn - self.lags[chunk] - hop
-
-                @pl.when((hop > 0) & (piece >= 0) & (piece < self.pieces))
+                since = turn - self.lags[chunk] - hop
+                piece = since // self.stride
+                inside = (since >= 0) & (piece < self.pieces) & (since % self.stride == 0)
+
+                @pl.when((hop > 0) & inside)
                 def _(way=way, chunk=chunk, piece=piece):
                     self.copy(chunk, piece, way).wait_recv()
 
@@ -569,7 +579,10 @@
     return [max(place, count - 1 - place) for place in range(count)]
 
 
-def gather_kernel(count, pieces, x_ref, full_ref, send, receive, local):
+def gather_kernel(
+    count, pieces, x_ref, freqs_ref, lengths_ref, perm_ref, starts_ref,
+    full_ref, cos_ref, sin_ref, column_ref, row_ref, send, receive, local,
+):
     line = Line(count)
     chunk_rows = x_ref.shape[0]
     own = pl.ds(pl.multiple_of(line.place * chunk_rows, chunk_rows), chunk_rows)
@@ -579,22 +592,43 @@
     gather = Gather(line, full_ref, send, receive, chunk_rows, pieces)
     for piece in range(pieces):
         gather.start(piece, x_ref.at[gather.rows(0, piece)])
+    row_ref[...] = segment_starts(lengths_ref, perm_ref, starts_ref, lanes(row_ref.shape))
+    size = count * chunk_rows // pieces
 
     @pl.loop(1, pieces + count - 1)
     def _(turn):
         gather.turn(turn)
 
+        @pl.when(turn <= pieces)
+        def _():
+            first = pl.multiple_of((turn - 1) * size, size)
+            rows = first + lax.broadcasted_iota(jnp.int32, (size, SLAB), 0)
+            start = segment_starts(lengths_ref, perm_ref, starts_ref, rows)
+            angles = (rows - start).astype(F32) * freqs_ref[...]
+            low_half = lanes(rows.shape) % HEAD_SIZE < HEAD_SIZE // 2
+            sines = jnp.sin(angles)
+            cos_ref[pl.ds(first, size), :] = jnp.cos(angles)
+            sin_ref[pl.ds(first, size), :] = jnp.where(low_half, -sines, sines)
+            column_ref[pl.ds(first, size), :] = start[:, 0:1]
+
     gather.finish(x_ref.at[gather.rows(0, 0)])
     keep.wait()
 
 
-def line_gather(x, count, collective_id, pieces=8):
+def line_gather(x, freqs, lengths, perm, starts, count, collective_id, pieces=8):
     rows, width = x.shape
+    total = count * rows
     return pl.pallas_call(
         functools.partial(gather_kernel, count, pieces),
-        out_shape=jax.ShapeDtypeStruct((count * rows, width), x.dtype),
-        in_specs=vmem_specs(1),
-        out_specs=pl.BlockSpec(memory_space=pl.ANY),
+        out_shape=(
+            jax.ShapeDtypeStruct((total, width), x.dtype),
+            jax.ShapeDtypeStruct((total, SLAB), F32),
+            jax.ShapeDtypeStruct((total, SLAB), F32),
+            jax.ShapeDtypeStruct((total, 1), jnp.int32),
+            jax.ShapeDtypeStruct((1, total), jnp.int32),
+        ),
+        in_specs=vmem_specs(2) + [pl.BlockSpec(memory_space=pltpu.SMEM)] * 3,
+        out_specs=(pl.BlockSpec(memory_space=pl.ANY),) + tuple(vmem_specs(4)),
         scratch_shapes=[
             copy_sems(count, pieces), copy_sems(count, pieces), pltpu.SemaphoreType.DMA
         ],
@@ -603,7 +637,7 @@
             flops=0, bytes_accessed=200 * rows * width, transcendentals=0
         ),
         name="line_gather",
-    )(x)
+    )(x, freqs, lengths, perm, starts)
 
 
 def forward_turn_kernel(
@@ -644,7 +678,7 @@
     gather.finish()
 
 
-def forward_turn(mixed, w_out, x, gain, count, collective_id, pieces=8):
+def forward_turn(mixed, w_out, x, gain, count, collective_id, pieces=16):
     chunk_rows, width = x.shape
     rows = count * chunk_rows
     return pl.pallas_call(
@@ -861,20 +895,34 @@
 def backward_turn_kernel(
     count, pieces, given_ref, dy_ref, middle_ref, gain_ref,
     normed_full_ref, gate_grad_ref, up_grad_ref, active_ref, dy_full_ref,
-    grad_ref, full_ref, gain_grad_ref, sums_ref, traded_ref,
-    partial, landing, tiles, traded,
+    grad_ref, full_ref, gain_grad_ref, sums_ref, down_grad_ref, traded_ref,
+    partial, landing, tiles, traded, normed, gate_grad, active, dy_full, kept, arrived,
     rs_send, rs_receive, ag_send, ag_receive, load, trade_send, trade_receive, fetches, stores,
+    peer_send, peer_receive, operands,
 ):
     line = Line(count)
     chunk_rows = dy_ref.shape[0]
     fetch = pltpu.make_async_copy(given_ref, partial, load)
     fetch.start()
+    brought = [
+        pltpu.make_async_copy(source, target, operands.at[at])
+        for at, (source, target) in enumerate((
+            (active_ref, active), (dy_full_ref, dy_full), (normed_full_ref, normed),
+            (gate_grad_ref, gate_grad), (up_grad_ref, active),
+        ))
+    ]
+    for copy in brought[:4]:
+        copy.start()
     replica = lax.axis_index("dp")
-    side = replica % 2
+    side, mine = replica % 2, replica // 2
     partner = replica + 1 - 2 * side
+    halves = kept.shape[0]
+    others = [(mine + step) % halves for step in range(1, halves)]
     semaphore = pltpu.get_barrier_semaphore()
     pl.semaphore_signal(semaphore, 1, device_id={"dp": partner})
-    pl.semaphore_wait(semaphore, line.greet(semaphore) + 1)
+    for half in others:
+        pl.semaphore_signal(semaphore, 1, device_id={"dp": 2 * half + side})
+    pl.semaphore_wait(semaphore, line.greet(semaphore) + halves)
     fetch.wait()
     scatter = Scatter(line, partial, landing, rs_send, rs_receive, chunk_rows, pieces)
     gather = Gather(
@@ -894,10 +942,8 @@
 
     block = traded.shape[0]
     width = traded.shape[1]
-    products = (
-        (normed_full_ref, gate_grad_ref), (normed_full_ref, up_grad_ref), (active_ref, dy_full_ref),
-    )
-    halves = sums_ref.shape[0] // block
+    products = ((active, dy_full), (normed, gate_grad), (normed, active))
+    needed = ((0, 1), (2, 3), (4,))
     pairs = halves * len(products)
     theirs = pl.ds(pl.multiple_of((1 - side) * block, block), block)
     ours = pl.ds(pl.multiple_of(side * block, block), block)
@@ -914,16 +960,26 @@
 
     def put(pair):
         rows = pl.ds(pl.multiple_of((pair % halves) * block, block), block)
-        columns = pl.ds(pl.multiple_of((pair // halves) * width, width), width)
+        columns = pl.ds(pl.multiple_of((pair // halves - 1) * width, width), width)
         return pltpu.make_async_copy(
             tiles.at[pair % 2, ours], sums_ref.at[rows, columns], stores.at[pair % 2]
+        )
+
+    def peer(half, place):
+        return pltpu.make_async_remote_copy(
+            src_ref=kept.at[half], dst_ref=arrived.at[place],
+            send_sem=peer_send.at[half], recv_sem=peer_receive.at[place],
+            device_id={"dp": 2 * half + side},
         )
 
     def beside(pair):
         @pl.when((pair >= 2) & (pair < pairs))
         def _():
             trade(pair - 2).wait_send()
-            put(pair - 2).wait()
+
+            @pl.when(pair - 2 >= halves)
+            def _():
+                put(pair - 2).wait()
 
         @pl.when((pair >= 1) & (pair <= pairs))
         def _():
@@ -932,6 +988,13 @@
 
         at = pl.ds(pl.multiple_of((pair % halves) * 2 * block, 2 * block), 2 * block)
         for which, (left, right) in enumerate(products):
+            @pl.when(pair == which * halves)
+            def _(which=which):
+                for operand in needed[which]:
+                    brought[operand].wait()
+                if which == 1:
+                    brought[4].start()
+
             @pl.when(pair // halves == which)
             def _(left=left, right=right):
                 tiles[pair % 2] = row_contract(left[:, at], right[...]).astype(BF16)
@@ -942,11 +1005,23 @@
 
         @pl.when((pair >= 1) & (pair <= pairs))
         def _():
-            bring(pair - 1).wait()
-            slot = (pair - 1) % 2
-            kept = tiles[slot, ours].astype(F32) + traded[...].astype(F32)
-            tiles[slot, ours] = kept.astype(BF16)
-            put(pair - 1).start()
+            last = pair - 1
+            bring(last).wait()
+            slot = last % 2
+            total = tiles[slot, ours].astype(F32) + traded[...].astype(F32)
+
+            @pl.when(last < halves)
+            def _():
+                kept[last % halves] = total.astype(BF16)
+
+                @pl.when(last != mine)
+                def _():
+                    peer(last, mine).start()
+
+            @pl.when(last >= halves)
+            def _():
+                tiles[slot, ours] = total.astype(BF16)
+                put(last).start()
 
     turns = pieces + 2 * (count - 1)
 
@@ -960,6 +1035,13 @@
     for pair in range(pairs - 2, pairs):
         trade(pair).wait_send()
         put(pair).wait()
+    total = kept[mine].astype(F32)
+    for half in others:
+        peer(half, half).wait_recv()
+        total = total + arrived[half].astype(F32)
+    down_grad_ref[...] = total
+    for half in others:
+        peer(half, mine).wait_send()
     scatter.finish()
     gather.finish()
 
@@ -974,7 +1056,7 @@
 
 def backward_turn(
     given, dy, middle, gain, normed_full, gate_grad, up_grad, active, dy_full,
-    count, replicas, collective_id, pieces=8,
+    count, replicas, collective_id, pieces=16,
 ):
     chunk_rows, width = dy.shape
     rows = count * chunk_rows
@@ -988,17 +1070,20 @@
             jax.ShapeDtypeStruct((chunk_rows, width), F32),
             jax.ShapeDtypeStruct((rows, width), BF16),
             jax.ShapeDtypeStruct((1, width), F32),
-            jax.ShapeDtypeStruct((kept_rows, 3 * width), BF16),
+            jax.ShapeDtypeStruct((kept_rows, 2 * width), BF16),
+            jax.ShapeDtypeStruct((block, width), F32),
             jax.ShapeDtypeStruct((pairs, block, width), BF16),
         ),
-        in_specs=[hbm] + vmem_specs(8),
-        out_specs=tuple(vmem_specs(3)) + (hbm, hbm),
+        in_specs=[hbm] + vmem_specs(3) + [hbm] * 5,
+        out_specs=tuple(vmem_specs(3)) + (hbm, vmem_specs(1)[0], hbm),
         scratch_shapes=[
             pltpu.VMEM((rows, width), BF16),
             pltpu.VMEM((landing_rows(count, chunk_rows), width), BF16),
             pltpu.VMEM((2, 2 * block, width), BF16),
             pltpu.VMEM((block, width), BF16),
         ]
+        + [pltpu.VMEM((rows, width), BF16)] * 4
+        + [pltpu.VMEM((replicas // 2, block, width), BF16)] * 2
         + [copy_sems(count, pieces)] * 4
         + [
             pltpu.SemaphoreType.DMA,
@@ -1006,6 +1091,9 @@
             pltpu.SemaphoreType.DMA((pairs,)),
             pltpu.SemaphoreType.DMA,
             pltpu.SemaphoreType.DMA((2,)),
+            pltpu.SemaphoreType.DMA((replicas // 2,)),
+            pltpu.SemaphoreType.DMA((replicas // 2,)),
+            pltpu.SemaphoreType.DMA((5,)),
         ],
         compiler_params=params(collective_id=collective_id, has_side_effects=True),
         cost_estimate=pl.CostEstimate(
@@ -1016,15 +1104,18 @@
 
 
 def last_turn_kernel(
-    count, pieces, replicas, dqkv_ref, w_ref, normed_ref, middle_grad_ref, x_ref, gain_ref, gain_two_ref,
-    grad_ref, weight_grad_ref, gains_ref,
+    count, pieces, replicas, dqkv_ref, packed_ref, normed_ref, middle_grad_ref, x_ref, gain_ref,
+    gain_two_ref, grad_ref, query_grad_ref, key_grad_ref, value_grad_ref, gain_one_out, gain_two_out,
+    w_ref, sems,
     partial, landing, sums, traded, arrived, pair_sems, sends, receives,
-    gain_own, gain_row, gain_land, gain_line,
+    gain_own, gain_row, gain_land, gains_ref, gain_line,
     rs_send, rs_receive, dp_send, dp_receive, line_send, line_receive,
 ):
     line = Line(count)
     chunk_rows = x_ref.shape[0]
-    width = dqkv_ref.shape[1]
+    fetches = weight_fetches(packed_ref, w_ref, sems)
+    for fetch in fetches:
+        fetch.start()
     replica = lax.axis_index("dp")
     semaphore = pltpu.get_barrier_semaphore()
     for step in range(1, replicas):
@@ -1033,11 +1124,13 @@
         pl.semaphore_signal(semaphore, 1, device_id={"tensor": (line.place + step) % count})
     pl.semaphore_wait(semaphore, replicas - 1 + count - 1)
     fold = Fold(replicas, sums, traded, arrived, pair_sems, sends, receives)
+    for fetch in fetches:
+        fetch.wait()
 
     @pl.loop(0, partial.shape[0] // SPAN)
     def _(step):
         rows = pl.ds(pl.multiple_of(step * SPAN, SPAN), SPAN)
-        partial[rows, :] = project_back(dqkv_ref[rows, :], w_ref[:, :width]).astype(BF16)
+        partial[rows, :] = project_back(dqkv_ref[rows, :], w_ref[...]).astype(BF16)
 
     scatter = Scatter(line, partial, landing, rs_send, rs_receive, chunk_rows, pieces)
     size = chunk_rows // pieces
@@ -1092,7 +1185,11 @@
     places = [(line.place + step) % count for step in range(1, count)]
     for peer in peers:
         share(peer, replica).start()
-    weight_grad_ref[...] = fold.total()
+    total = fold.total()
+    at = 0
+    for ref in (query_grad_ref, key_grad_ref, value_grad_ref):
+        ref[...] = total[:, at : at + ref.shape[1]]
+        at += ref.shape[1]
     total = gain_row[...]
     for peer in peers:
         share(peer, peer).wait_recv()
@@ -1109,12 +1206,18 @@
         total = total + gain_line[peer]
     for peer in places:
         pass_line(peer, line.place).wait_send()
-    gains_ref[...] = total
+    own = gain_one_out.shape[1]
+    kept = jnp.zeros((2, own), F32)
+    for owner in range(replicas):
+        part = total[:, owner * own : (owner + 1) * own]
+        kept = kept + jnp.where(replica == owner, part, 0.0)
+    gain_one_out[...] = kept[0:1]
+    gain_two_out[...] = kept[1:2]
 
 
 def last_turn(
-    dqkv, w_qkv, normed, middle_grad, x, gain, gain_two_grad, count, replicas, collective_id,
-    pieces=8,
+    dqkv, w_qkv, normed, middle_grad, x, gain, gain_two_grad, widths, count, replicas,
+    collective_id, pieces=8,
 ):
     chunk_rows, width = x.shape
     rows = count * chunk_rows
@@ -1123,12 +1226,14 @@
         functools.partial(last_turn_kernel, count, pieces, replicas),
         out_shape=(
             jax.ShapeDtypeStruct((chunk_rows, width), BF16),
-            jax.ShapeDtypeStruct((block, dqkv.shape[1]), F32),
-            jax.ShapeDtypeStruct((2, width), F32),
-        ),
-        in_specs=vmem_specs(7),
-        out_specs=tuple(vmem_specs(3)),
+        )
+        + tuple(jax.ShapeDtypeStruct((block, part), F32) for part in widths)
+        + (jax.ShapeDtypeStruct((1, block), F32),) * 2,
+        in_specs=vmem_specs(1) + [pl.BlockSpec(memory_space=pl.ANY)] + vmem_specs(5),
+        out_specs=tuple(vmem_specs(6)),
         scratch_shapes=[
+            pltpu.VMEM((width, dqkv.shape[1]), BF16),
+            pltpu.SemaphoreType.DMA((replicas,)),
             pltpu.VMEM((rows, width), BF16),
             pltpu.VMEM((landing_rows(count, chunk_rows), width), BF16),
         ]
@@ -1137,6 +1242,7 @@
             pltpu.VMEM((1, width), F32),
             pltpu.VMEM((2, width), F32),
             pltpu.VMEM((replicas, 2, width), F32),
+            pltpu.VMEM((2, width), F32),
             pltpu.VMEM((count, 2, width), F32),
         ]
         + [copy_sems(count, pieces)] * 2
@@ -1156,35 +1262,34 @@
     seq_lengths, group_perm, group_starts,
 ):
     count = lax.axis_size("tensor")
-    group_rows = inputs.shape[0] * count
     q_width, kv_width = w_query.shape[1], w_key.shape[1]
     qkv_width = q_width + 2 * kv_width
-    start, positions = group_layout(
-        seq_lengths, group_perm, group_starts, lax.axis_index("dp"), group_rows, MOST_SEQS
-    )
-    cosine, sine = slab_tables(positions)
-
-    gains = jnp.stack([attn_gain, mlp_gain], axis=1)
-    gains = jnp.pad(gains, ((0, 0), (0, SLAB - 2)))
-    packed = jnp.concatenate([w_query, w_key, w_value, gains], axis=1)
-    qkv_full = lax.all_gather(packed, "dp", axis=0, tiled=True)
+    own = attn_gain.shape[0]
+    gains = jnp.concatenate([attn_gain, mlp_gain])[None]
+    gains = jnp.pad(gains, ((0, GAIN_ROWS - 1), (0, qkv_width - 2 * own)))
+    packed = jnp.concatenate([w_query, w_key, w_value], axis=1)
+    packed = jnp.concatenate([packed, gains], axis=0)
+    qkv_full = lax.all_gather(packed[None], "dp", axis=0, tiled=True)
     out_full = lax.all_gather(w_out, "dp", axis=0, tiled=True)
     gate_full = lax.all_gather(w_gate, "dp", axis=0, tiled=True)
     up_full = lax.all_gather(w_up, "dp", axis=0, tiled=True)
     down_full = lax.all_gather(w_down, "dp", axis=0, tiled=True)
-    gain_rows = jnp.transpose(qkv_full[:, qkv_width : qkv_width + 2].astype(F32))
+    gain_rows = qkv_full[:, own, : 2 * own].reshape(-1, 2, own).astype(F32)
+    gain_rows = jnp.transpose(gain_rows, (1, 0, 2)).reshape(2, -1)
     gain_one, gain_two = gain_rows[0:1], gain_rows[1:2]
 
-    x_full = line_gather(inputs, count, 0)
+    x_full, cosine, sine, start_column, start_row = line_gather(
+        inputs, rotary_freqs()[None], seq_lengths, group_perm, group_starts, count, 0
+    )
     normed_full, queries, keys, values, mixed, lse = attend(
-        x_full, qkv_full, gain_one, cosine, sine, start[:, None], q_width, kv_width
+        x_full, qkv_full, gain_one, cosine, sine, start_column, q_width, kv_width
     )
     replicas = lax.axis_size("dp")
     middle, normed_two_full = forward_turn(mixed, out_full, inputs, gain_two, count, 1)
     grad_full, active, gate_grad, up_grad, norm_two_grad, outputs = hidden_layer(
         normed_two_full, cotangent, middle, gate_full, up_full, down_full, count, 4
     )
-    middle_grad, branch_full, gain_two_grad, sums, _ = backward_turn(
+    middle_grad, branch_full, gain_two_grad, sums, down_grad, _ = backward_turn(
         norm_two_grad, cotangent, middle, gain_two, normed_two_full, gate_grad, up_grad, active,
         grad_full, count, replicas, 2,
     )
@@ -1192,26 +1297,24 @@
     hidden_grads = lax.psum_scatter(
         sums, "dp", scatter_dimension=0, axis_index_groups=sides, tiled=True
     ).astype(F32)
-    gate_weight_grad, up_weight_grad, down_grad = jnp.split(hidden_grads, 3, axis=1)
+    gate_weight_grad, up_weight_grad = jnp.split(hidden_grads, 2, axis=1)
     dqkv, out_grad = attend_back(
-        branch_full, out_full, mixed, queries, keys, values, lse, cosine, sine, start[None, :],
+        branch_full, out_full, mixed, queries, keys, values, lse, cosine, sine, start_row,
         replicas, 5,
     )
-    input_grad, qkv_grad, gains_grad = last_turn(
+    input_grad, query_grad, key_grad, value_grad, gain_one_grad, gain_two_grad = last_turn(
         dqkv, qkv_full, normed_full, middle_grad, inputs, gain_one, gain_two_grad,
-        count, replicas, 3,
+        (q_width, kv_width, kv_width), count, replicas, 3,
     )
-    own = attn_gain.shape[0]
-    gains_grad = lax.dynamic_slice_in_dim(gains_grad, lax.axis_index("dp") * own, own, axis=1)
     return (
         outputs,
         input_grad,
-        gains_grad[0],
-        qkv_grad[:, :q_width],
-        qkv_grad[:, q_width : q_width + kv_width],
-        qkv_grad[:, q_width + kv_width :],
+        gain_one_grad[0],
+        query_grad,
+        key_grad,
+        value_grad,
         out_grad,
-        gains_grad[1],
+        gain_two_grad[0],
         gate_weight_grad,
         up_weight_grad,
         down_grad,

time: 679 us -> 652 us (0.960)
  local copies, waits for them, and re-layouts: 23.5 us -> 13 us
  waiting for transfers between devices: 12.7 us -> 3.92 us
    reduce_scatter x1, waiting for transfers between devices: 10.2 us -> 0.02 us  [shards(): lax.psum_scatter(sums, 'dp', scatter_dimension=0, axis_index_groups=sides...]
    pallas_call x1, Pallas kernels: 133 us -> 126 us  [backward_turn(): pl.pallas_call(functools.partial(backward_turn_kernel, count, pieces), ou...]
  transfers between devices with their start and end apart: 6 -> 6, of which waited for: 1 -> 1; matrix products, arithmetic and copies ran while one was open for 3% -> 0% of each run, Pallas kernels for 53% -> 56%
where the time goes in v3:
time: 652 us; the launch traced here: 645 us
  Pallas kernels  609 us (93%)
  between operations  14.7 us (2%)
  local copies, waits for them, and re-layouts  13 us (2%)
    pallas_call x1, Pallas kernels, backward_turn(): pl.pallas_call(functools.partial(backward_turn_kernel, count, pieces), ou...  126 us
    pallas_call x1, Pallas kernels, hidden_layer(): pl.pallas_call(functools.partial(hidden_kernel, count, pieces), out_shape...  125 us
    pallas_call x1, Pallas kernels, forward_turn(): pl.pallas_call(functools.partial(forward_turn_kernel, count, pieces), out...  122 us
    pallas_call x1, Pallas kernels, last_turn(): pl.pallas_call(functools.partial(last_turn_kernel, count, pieces, replica...  93.7 us
    pallas_call x1, Pallas kernels, line_gather(): pl.pallas_call(functools.partial(gather_kernel, count, pieces), out_shape...  76.1 us
    pallas_call x1, Pallas kernels, attend_back(): pl.pallas_call(functools.partial(attend_back_kernel, replicas), out_shape...  37.5 us
    pallas_call x1, Pallas kernels, attend(): pl.pallas_call(attend_kernel, out_shape=(jax.ShapeDtypeStruct(x_full.shap...  28.7 us
  transfers between devices with their start and end apart: 6, of which 1 were waited for; matrix products, arithmetic and copies ran while one was open for 0% of the time, Pallas kernels for 56%

profile of v3, /device:TPU:0, one launch (start us, length us, event | category | flops | bytes accessed | tf_op | source)
XLA Modules:
  0.0 645.0 jit_solution(17447067839939630486)
XLA Ops:
  7.2 0.7 pad_maximum_fusion
  7.9 1.8 fusion.1
  9.8 0.0 all-gather.7.cloned.1.call-start
  9.8 0.7 all-gather.7.cloned.1.call-update
  10.6 0.7 all-gather.9.cloned.1.call-update
  11.3 0.5 all-gather.11.cloned.1.call-update
  11.9 0.5 all-gather.13.cloned.1.call-update
  12.5 0.1 lt.18
  12.6 0.1 gt.14
  12.7 0.1 pow.16
  12.8 0.5 select_select_fusion.freqs_ref
  13.3 76.1 %line_gather.1 = (bf16[1024,2048]{1,0:T(8,128)(2,1)}, f32[1024,128]{1,0:T(8,128)}, f32[1024,128]{1,0:T(8,128)}, s32[1024,1]{1,0:T(8,128)}, s32[1,1024]{1,0:T(1,128)}) custom-call(bf16[256,2048]{1,0:T(8,128)(2,1)} %x_ref.5, f32[1,128]{1,0:T(1,128)} %select_select_fusion.freqs_ref, s32[12]{0:T(128)} %lengths_ref.1, s32[12]{0:T(128)} %perm_ref.1, s32[9]{0:T(128)} %starts_ref.1), custom_call_target="tpu_custom_call" | custom-call | bytes 104857600 | tf_op jit(solution)/shard_map/line_gather/pallas_call | solution.py:621
  89.5 0.9 fusion.2
  90.4 0.6 copy.27
  91.0 0.6 copy.26
  91.6 28.7 %attend.1 = (bf16[1024,2048]{1,0:T(8,128)(2,1)}, bf16[1024,512]{1,0:T(8,128)(2,1)}, bf16[2,1024,128]{2,1,0:T(8,128)(2,1)}, bf16[2,1024,128]{2,1,0:T(8,128)(2,1)}...) custom-call(bf16[1024,2048]{1,0:T(8,128)(2,1)} %get-tuple-element.43.x_ref, bf16[8,272,768]{2,1,0:T(8,128)(2,1)} %bitcast.24, ...), custom_call_target="tpu_custom_call" | custom-call | flops 7516192768 | bytes 16777216 | tf_op jit(solution)/shard_map/attend/pallas_call | solution.py:181
  120.4 122.4 %forward_turn.1 = (f32[256,2048]{1,0:T(8,128)}, bf16[1024,2048]{1,0:T(8,128)(2,1)}) custom-call(bf16[1024,512]{1,0:T(8,128)(2,1)} %get-tuple-element.47.mixed_ref, bf16[512,2048]{1,0:T(8,128)(2,1)} %all-gather.7.cloned.1.call-done.w_ref, bf16[256,2048]{1,0:T(8,128)(2,1)} %x_ref.5, f32[1,2048]{1,0:T(1,128)} %bitcast.19), custom_call_target="tpu_custom_call" | custom-call | flops 2147483648 | bytes 157286400 | tf_op jit(solution)/shard_map/forward_turn/pallas_call | solution.py:684
  242.8 1.3 all-gather.13.cloned.1.call-done.down_ref
  244.2 124.8 %hidden_layer.1 = (bf16[1024,2048]{1,0:T(8,128)(2,1)}, bf16[4,256,2048]{2,1,0:T(8,128)(2,1)}, bf16[4,256,2048]{2,1,0:T(8,128)(2,1)}, bf16[4,256,2048]{2,1,0:T(8,...) custom-call(bf16[1024,2048]{1,0:T(8,128)(2,1)} %get-tuple-element.48.normed_ref.normed_full_ref, ...), custom_call_target="tpu_custom_call" | custom-call | flops 51539607552 | bytes 67108864 | tf_op jit(solution)/shard_map/hidden_layer/pallas_call | solution.py:860
  369.0 125.9 %backward_turn.1 = (f32[256,2048]{1,0:T(8,128)}, bf16[1024,2048]{1,0:T(8,128)(2,1)}, f32[1,2048]{1,0:T(1,128)}, bf16[1024,4096]{1,0:T(8,128)(2,1)}, f32[256,2048]{1,0:T(8,128)}, /*index=5*/bf16[12,256,2048]{2,1,0:T(8,128)(2,1)}) custom-call(bf16[1024,2048]{1,0:T(8,128)(2,1)} %bitcast.29, bf16[256,2048]{1,0:T(8,128)(2,1)} %dy_ref.1, ...), custom_call_target="tpu_custom_call" | custom-call | flops 25769803776 | bytes 67108864 | tf_op jit(solution)/shard_map/backward_turn/pallas_call | solution.py:1067
  494.9 37.5 %attend_back.1 = (bf16[1024,768]{1,0:T(8,128)(2,1)}, f32[64,2048]{1,0:T(8,128)}) custom-call(bf16[1024,2048]{1,0:T(8,128)(2,1)} %get-tuple-element.56.branch_ref, bf16[512,2048]{1,0:T(8,128)(2,1)} %all-gather.7.cloned.1.call-done.w_ref, bf16[1024,512]{1,0:T(8,128)(2,1)} %get-tuple-element.47.mixed_ref, bf16[1024,512]{1,0:T(8,128)(2,1)} %get-tuple-element.57.q_ref, ...), custom_call_target="tpu_custom_call" | custom-call | flops 12884901888 | bytes 16777216 | tf_op jit(solution)/shard_map/attend_back/pallas_call | solution.py:548
  532.4 93.7 %last_turn.1 = (bf16[256,2048]{1,0:T(8,128)(2,1)}, f32[256,512]{1,0:T(8,128)}, f32[256,128]{1,0:T(8,128)}, f32[256,128]{1,0:T(8,128)}, f32[1,256]{1,0:T(1,128)}, /*index=5*/f32[1,256]{1,0:T(1,128)}) custom-call(bf16[1024,768]{1,0:T(8,128)(2,1)} %get-tuple-element.62.dqkv_ref, bf16[8,272,768]{2,1,0:T(8,128)(2,1)} %bitcast.25, ...), custom_call_target="tpu_custom_call" | custom-call | flops 6442450944 | bytes 104857600 | tf_op jit(solution)/shard_map/last_turn/pallas_call | solution.py:1225
  626.1 4.2 fusion.5
  630.4 1.0 copy.37
  631.4 1.0 copy.38
  632.3 0.6 copy.39
  632.9 0.8 copy.40
  633.7 0.7 copy.41
  634.4 0.7 copy.42
  635.0 0.8 copy.43
  635.8 0.6 copy.44
  636.4 1.3 copy.45
  (35 shorter events, 0.4 us)
Async XLA Ops:
  7.2 82.3 %all-gather.15.cloned.1.call-start = ((), (), s32[]{:S(2)}) async-start(), calls=%async_computation.6 | async-start | bytes 3760128 | tf_op jit(solution)/shard_map/all_gather | solution.py:1272
  9.8 110.6 %all-gather.7.cloned.1.call-start = ((), (), s32[]{:S(2)}) async-start(), calls=%async_computation.1 | async-start | bytes 2359296 | tf_op jit(solution)/shard_map/all_gather | solution.py:1273
  10.5 232.3 %all-gather.9.cloned.1.call-start = ((), (), s32[]{:S(2)}) async-start(), calls=%async_computation.2 | async-start | bytes 9437184 | tf_op jit(solution)/shard_map/all_gather | solution.py:1274
  11.2 231.6 %all-gather.11.cloned.1.call-start = ((), (), s32[]{:S(2)}) async-start(), calls=%async_computation.3 | async-start | bytes 9437184 | tf_op jit(solution)/shard_map/all_gather | solution.py:1275
  11.8 232.4 %all-gather.13.cloned.1.call-start = ((), (), s32[]{:S(2)}) async-start(), calls=%async_computation.4 | async-start | bytes 9437184 | tf_op jit(solution)/shard_map/all_gather | solution.py:1276
  12.4 613.7 %reduce-scatter.2.cloned.1.call-start = ((), (), s32[]{:S(2)}) async-start(), calls=%async_computation.5 | async-start | bytes 10485760 | tf_op jit(solution)/shard_map/reduce_scatter | solution.py:1297
  626.1 4.3 copy-start.1
  626.1 5.3 copy-start.2
  630.3 2.0 copy-start.8
  630.3 2.6 copy-start.4
  630.3 3.4 copy-start.6
  630.3 4.0 copy-start.5
  630.3 4.7 copy-start.3
  630.4 5.5 copy-start.7
  630.4 6.0 copy-start
Sparse Core Ops, SparseCore 0:
  10.4 35.7 all-gather.14
  48.1 27.7 all-gather.6
  77.8 54.2 all-gather.8
  133.9 54.1 all-gather.10
  189.9 54.2 all-gather.12
  495.0 111.3 reduce-scatter.1

commit v4 on v3

--- a/solution.py
+++ b/solution.py
@@ -105,12 +105,17 @@
 
 
 def attend_kernel(
-    x_ref, packed_ref, gain_ref, cos_ref, sin_ref, start_ref,
-    normed_ref, q_ref, k_ref, v_ref, mixed_ref, lse_ref, bias_ref, stat_ref, w_ref, sems,
+    count, x_ref, packed_ref, gain_ref, cos_ref, sin_ref, start_ref, dy_ref,
+    normed_ref, q_ref, k_ref, v_ref, mixed_ref, lse_ref, near_ref, bias_ref, stat_ref, w_ref, sems,
+    near_send, near_receive,
 ):
     fetches = weight_fetches(packed_ref, w_ref, sems)
     for fetch in fetches:
         fetch.start()
+    line = Line(count)
+    line.barrier()
+    gather = Gather(line, near_ref, near_send, near_receive, dy_ref.shape[0], 1)
+    gather.start(0, dy_ref)
     for fetch in fetches:
         fetch.wait()
     rows_all = x_ref.shape[0]
@@ -172,14 +177,25 @@
             stat_ref[first : first + SPAN, :] = jnp.where(lane == 2 * slab + 1, logs[SPAN:], old)
 
     lse_ref[...] = jnp.transpose(stat_ref[...])[: lse_ref.shape[0], :]
-
-
-def attend(x_full, w_qkv, gain, cosine, sine, start, q_width, kv_width):
+    for way in (0, 1):
+        @pl.when(line.has[1 - way])
+        def _(way=way):
+            gather.copy(line.neighbour[1 - way], 0, way).wait_recv()
+
+        @pl.when(line.has[way])
+        def _(way=way):
+            gather.copy(line.place, 0, way, dy_ref).wait_send()
+
+
+def attend(
+    x_full, w_qkv, gain, cosine, sine, start, dy, q_width, kv_width, count, collective_id
+):
     rows = x_full.shape[0]
     heads = 2 * (kv_width // SLAB)
+    hbm = pl.BlockSpec(memory_space=pl.ANY)
     flops = 2 * rows * x_full.shape[1] * (q_width + 2 * kv_width) + 8 * rows * rows * q_width
     return pl.pallas_call(
-        attend_kernel,
+        functools.partial(attend_kernel, count),
         out_shape=(
             jax.ShapeDtypeStruct(x_full.shape, BF16),
             jax.ShapeDtypeStruct((rows, q_width), BF16),
@@ -187,19 +203,21 @@
             jax.ShapeDtypeStruct((heads, rows, SLAB), BF16),
             jax.ShapeDtypeStruct((rows, q_width), BF16),
             jax.ShapeDtypeStruct((q_width // HEAD_SIZE, rows), F32),
+            jax.ShapeDtypeStruct(x_full.shape, BF16),
         ),
-        in_specs=vmem_specs(1) + [pl.BlockSpec(memory_space=pl.ANY)] + vmem_specs(4),
-        out_specs=tuple(vmem_specs(6)),
+        in_specs=vmem_specs(1) + [hbm] + vmem_specs(4) + [hbm],
+        out_specs=tuple(vmem_specs(6)) + (hbm,),
         scratch_shapes=[
             pltpu.VMEM((SPAN, rows), F32),
             pltpu.VMEM((rows, SLAB), F32),
             pltpu.VMEM((x_full.shape[1], w_qkv.shape[2]), BF16),
             pltpu.SemaphoreType.DMA((w_qkv.shape[0],)),
+            copy_sems(count, 1), copy_sems(count, 1),
         ],
-        compiler_params=params(),
+        compiler_params=params(collective_id=collective_id, has_side_effects=True),
         cost_estimate=pl.CostEstimate(flops=flops, bytes_accessed=1 << 24, transcendentals=1 << 23),
         name="attend",
-    )(x_full, w_qkv, gain, cosine, sine, start)
+    )(x_full, w_qkv, gain, cosine, sine, start, dy)
 
 
 SUBS = 4
@@ -235,10 +253,10 @@
 
 
 class Gather:
-    def __init__(self, line, full, send, receive, chunk_rows, pieces, lags=None, stride=1):
+    def __init__(self, line, full, send, receive, chunk_rows, pieces, lags=None, near=0):
         self.line, self.full, self.send, self.receive = line, full, send, receive
         self.chunk_rows, self.size, self.pieces = chunk_rows, chunk_rows // pieces, pieces
-        self.lags, self.stride = lags or [0] * line.count, stride
+        self.lags, self.near = lags or [0] * line.count, near
 
     def rows(self, chunk, piece):
         start = chunk * self.chunk_rows + piece * self.size
@@ -257,16 +275,21 @@
             def _(way=way):
                 self.copy(self.line.place, piece, way, source).start()
 
+    def start_near(self, piece, source):
+        line = self.line
+        for way, chunk in ((0, line.place - 1), (1, line.place + 1)):
+            @pl.when(line.has[0] & line.has[1])
+            def _(way=way, chunk=chunk):
+                self.copy(chunk, piece, way, source.at[self.rows(chunk, piece)]).start()
+
     def turn(self, turn):
         line = self.line
         for chunk in range(line.count):
             for way in (0, 1):
-                hop = line.place - chunk if way == 0 else chunk - line.place
-                since = turn - self.lags[chunk] - hop
-                piece = since // self.stride
-                inside = (since >= 0) & (piece < self.pieces) & (since % self.stride == 0)
-
-                @pl.when((hop > 0) & inside)
+                hop = (line.place - chunk if way == 0 else chunk - line.place) - self.near
+                piece = turn - self.lags[chunk] - hop
+
+                @pl.when((hop > 0) & (piece >= 0) & (piece < self.pieces))
                 def _(way=way, chunk=chunk, piece=piece):
                     self.copy(chunk, piece, way).wait_recv()
 
@@ -280,11 +303,11 @@
         @pl.loop(0, self.pieces)
         def _(piece):
             for chunk in range(line.count):
-                @pl.when(line.has[0] & (chunk <= line.place))
+                @pl.when(line.has[0] & (chunk <= line.place - self.near))
                 def _(chunk=chunk):
                     self.copy(chunk, piece, 0, source).wait_send()
 
-                @pl.when(line.has[1] & (chunk >= line.place))
+                @pl.when(line.has[1] & (chunk >= line.place + self.near))
                 def _(chunk=chunk):
                     self.copy(chunk, piece, 1, source).wait_send()
 
@@ -294,6 +317,7 @@
         self.line, self.partial, self.landing = line, partial, landing
         self.send, self.receive = send, receive
         self.chunk_rows, self.size, self.pieces = chunk_rows, chunk_rows // pieces, pieces
+        self.lag = line.lag
 
     def rows(self, chunk, piece):
         start = chunk * self.chunk_rows + piece * self.size
@@ -343,7 +367,7 @@
                 self.forward(piece, way)
 
     def settle(self, turn, use):
-        piece = turn - self.line.lag
+        piece = turn - self.lag
 
         @pl.when((piece >= 0) & (piece < self.pieces))
         def _():
@@ -374,6 +398,42 @@
                 @pl.when(chunk < line.place)
                 def _(chunk=chunk):
                     self.copy(chunk, piece, 1).wait_send()
+
+
+class Stream(Scatter):
+    def __init__(self, line, partial, landing, send, receive, chunk_rows, pieces, offset, hop):
+        super().__init__(line, partial, landing, send, receive, chunk_rows, pieces)
+        self.offset, self.hop = offset, hop
+        count = line.count
+        self.lag = 0
+        for place in range(count):
+            up = (count - 1 - place) * pieces + hop * place
+            down = (count - 2 - place) * pieces + offset + hop * (count - 1 - place)
+            late = max(up if place > 0 else 0, down if place < count - 1 else 0)
+            self.lag = self.lag + jnp.where(line.place == place, late, 0)
+        self.turns = (count - 1) * (pieces + hop) + offset
+
+    def turn(self, turn):
+        line, pieces = self.line, self.pieces
+        last = line.count - 1
+        lags = (self.hop * line.place, self.offset + self.hop * (last - line.place))
+        for way, lag in enumerate(lags):
+            since = turn - lag
+            piece = since % pieces
+            chunk = last - way - since // pieces
+            beyond = chunk > line.place if way == 0 else chunk < line.place
+
+            @pl.when((since >= 0) & (since < last * pieces) & beyond)
+            def _(way=way, piece=piece, chunk=chunk):
+                @pl.when(line.has[1 - way])
+                def _():
+                    self.wait(chunk, piece, way)
+                    rows = self.rows(chunk, piece)
+                    total = self.partial[rows, :].astype(F32)
+                    total = total + self.landing[rows, :].astype(F32)
+                    self.partial[rows, :] = total.astype(BF16)
+
+                self.copy(chunk, piece, way).start()
 
 
 class Fold:
@@ -443,128 +503,6 @@
         pltpu.SemaphoreType.DMA((halves,)),
         pltpu.SemaphoreType.DMA((halves,)),
     ]
-
-
-def attend_back_kernel(
-    replicas, branch_ref, w_ref, mixed_ref, q_ref, k_ref, v_ref, lse_ref, cos_ref, sin_ref,
-    start_ref, dqkv_ref, weight_grad_ref, dmix_ref, bias_ref, dq_ref, dk_ref, dv_ref,
-    sums, traded, arrived, pair_sems, sends, receives,
-):
-    fold = Fold(replicas, sums, traded, arrived, pair_sems, sends, receives)
-    semaphore = pltpu.get_barrier_semaphore()
-    pl.semaphore_wait(semaphore, fold.greet(semaphore))
-    weight_rows = sums.shape[2]
-    for step in range(mixed_ref.shape[1] // SLAB):
-        first = step * SLAB
-        product = row_contract(mixed_ref[:, first : first + SLAB], branch_ref[...]).astype(BF16)
-        for row in range(0, SLAB, weight_rows):
-            owner = (first + row) // weight_rows
-            sums[owner // 2, owner % 2] = product[row : row + weight_rows]
-    fold.pair().start()
-
-    rows_all = branch_ref.shape[0]
-    q_width = q_ref.shape[1]
-    slabs = q_width // SLAB
-    kv_heads = k_ref.shape[0]
-    members = slabs // kv_heads
-    scale = HEAD_SIZE ** (-0.5)
-
-    @pl.loop(0, rows_all // SPAN)
-    def _(step):
-        rows = pl.ds(step * SPAN, SPAN)
-        dmix_ref[rows, :] = project_back(branch_ref[rows, :], w_ref[...]).astype(BF16)
-
-    fold.spread()
-    dk_ref[...] = jnp.zeros_like(dk_ref)
-    dv_ref[...] = jnp.zeros_like(dv_ref)
-    for tile in range(rows_all // SPAN):
-        first, span = tile * SPAN, (tile + 1) * SPAN
-        key_ids = lax.broadcasted_iota(jnp.int32, (span, SPAN), 0)
-        row_ids = first + lanes((span, SPAN))
-        allowed = (key_ids >= start_ref[:, first : first + SPAN]) & (key_ids <= row_ids)
-        bias_ref[:span, :] = jnp.where(allowed, 0.0, mask_fill)
-
-        @pl.loop(0, slabs)
-        def _(slab):
-            at = pl.ds(pl.multiple_of(slab * SLAB, SLAB), SLAB)
-            head = slab // members
-            queries = head_pair(q_ref[first : first + SPAN, at])
-            grads = head_pair(dmix_ref[first : first + SPAN, at])
-            keys = k_ref[head, :span, :]
-            scores = project_back(keys, queries)
-            bias = bias_ref[:span, :]
-            logs = jnp.concatenate(
-                [
-                    lse_ref[pl.ds(2 * slab, 1), first : first + SPAN],
-                    lse_ref[pl.ds(2 * slab + 1, 1), first : first + SPAN],
-                ],
-                axis=1,
-            )
-            chances = jnp.exp(scores + jnp.concatenate([bias, bias], axis=1) - logs)
-            chances_grad = project_back(v_ref[head, :span, :], grads)
-            shared = jnp.sum(chances * chances_grad, axis=0, keepdims=True)
-            score_grad = (chances * (chances_grad - shared)).astype(BF16)
-            dv_ref[head, :span, :] += project(chances.astype(BF16), grads)
-            dk_ref[head, :span, :] += project(score_grad, queries)
-            dq_ref[first : first + SPAN, at] = join_pair(row_contract(score_grad, keys)) * scale
-
-    left = lanes((SPAN, SLAB)) < HEAD_SIZE
-
-    @pl.loop(0, rows_all // SPAN)
-    def _(step):
-        rows = pl.ds(step * SPAN, SPAN)
-        cosine, sine = cos_ref[rows, :], sin_ref[rows, :]
-        for slab in range(slabs):
-            part = dq_ref[rows, slab * SLAB : (slab + 1) * SLAB]
-            part = part * cosine - turned(part) * sine
-            dqkv_ref[rows, slab * SLAB : (slab + 1) * SLAB] = part.astype(BF16)
-        for pair in range(kv_heads // 2):
-            joined = []
-            for ref in (dk_ref, dv_ref):
-                sums = []
-                for head in (2 * pair, 2 * pair + 1):
-                    full = ref[head, rows, :]
-                    sums.append(full + pltpu.roll(full, HEAD_SIZE, 1))
-                joined.append(jnp.where(left, sums[0], sums[1]))
-            key, value = joined
-            key = key * cosine - turned(key) * sine
-            at = q_width + pair * SLAB
-            dqkv_ref[rows, at : at + SLAB] = key.astype(BF16)
-            at = at + (kv_heads // 2) * SLAB
-            dqkv_ref[rows, at : at + SLAB] = value.astype(BF16)
-
-    weight_grad_ref[...] = fold.total()
-    fold.finish()
-
-
-def attend_back(
-    branch_full, w_out, mixed, queries, keys, values, lse, cosine, sine, start,
-    replicas, collective_id,
-):
-    rows, q_width = queries.shape
-    kv_heads = keys.shape[0]
-    width = q_width + kv_heads * SLAB
-    flops = 2 * rows * branch_full.shape[1] * q_width + 20 * rows * rows * q_width
-    return pl.pallas_call(
-        functools.partial(attend_back_kernel, replicas),
-        out_shape=(
-            jax.ShapeDtypeStruct((rows, width), BF16),
-            jax.ShapeDtypeStruct((q_width // replicas, branch_full.shape[1]), F32),
-        ),
-        in_specs=vmem_specs(10),
-        out_specs=tuple(vmem_specs(2)),
-        scratch_shapes=[
-            pltpu.VMEM((rows, q_width), BF16),
-            pltpu.VMEM((rows, SPAN), F32),
-            pltpu.VMEM((rows, q_width), F32),
-            pltpu.VMEM((kv_heads, rows, SLAB), F32),
-            pltpu.VMEM((kv_heads, rows, SLAB), F32),
-        ]
-        + fold_scratch(replicas, q_width // replicas, branch_full.shape[1]),
-        compiler_params=params(collective_id=collective_id, has_side_effects=True),
-        cost_estimate=pl.CostEstimate(flops=flops, bytes_accessed=1 << 24, transcendentals=1 << 23),
-        name="attend_back",
-    )(branch_full, w_out, mixed, queries, keys, values, lse, cosine, sine, start)
 
 
 def landing_rows(count, chunk_rows):
@@ -704,7 +642,7 @@
 
 
 def hidden_kernel(
-    count, pieces, normed_ref, own_ref, middle_ref, gate_ref, up_ref, down_ref,
+    count, pieces, normed_ref, own_ref, near_ref, middle_ref, gate_ref, up_ref, down_ref,
     full_ref, active_ref, gate_grad_ref, up_grad_ref, back_ref, out_ref,
     gate, up, down, normed, dy, active, slope, value, up_grad, back,
     partial, landing, rs_send, rs_receive, ag_send, ag_receive, loads, stores,
@@ -723,13 +661,24 @@
     for fetch in fetches:
         fetch.start()
     line.barrier()
-    gather = Gather(line, dy, ag_send, ag_receive, chunk_rows, SUBS)
+    gather = Gather(line, dy, ag_send, ag_receive, chunk_rows, SUBS, near=1)
     scatter = Scatter(line, partial, landing, rs_send, rs_receive, chunk_rows, pieces)
     for piece in range(SUBS):
-        gather.start(piece, own_ref.at[gather.rows(0, piece)])
-    own = pl.ds(pl.multiple_of(line.place * chunk_rows, chunk_rows), chunk_rows)
-    place_own = pltpu.make_async_copy(own_ref, dy.at[own], loads.at[4])
+        gather.start_near(piece, near_ref)
+
+    def chunk_at(chunk):
+        return pl.ds(pl.multiple_of(chunk * chunk_rows, chunk_rows), chunk_rows)
+
+    def place_near(way):
+        rows = chunk_at(line.neighbour[way])
+        return pltpu.make_async_copy(near_ref.at[rows], dy.at[rows], loads.at[5 + way])
+
+    place_own = pltpu.make_async_copy(own_ref, dy.at[chunk_at(line.place)], loads.at[4])
     place_own.start()
+    for way in (0, 1):
+        @pl.when(line.has[way])
+        def _(way=way):
+            place_near(way).start()
     gate_grad = active
     outs = ((active, active_ref), (gate_grad, gate_grad_ref), (up_grad, up_grad_ref),
             (back, back_ref))
@@ -805,6 +754,10 @@
         def _():
             store(0, SUBS - 1).wait()
             place_own.wait()
+            for way in (0, 1):
+                @pl.when(line.has[way])
+                def _(way=way):
+                    place_near(way).wait()
 
         @pl.when(step > 0)
         def _():
@@ -847,10 +800,12 @@
         store(which, SUBS - 1).wait()
     keep.wait()
     scatter.finish()
-    gather.finish(own_ref.at[gather.rows(0, 0)])
-
-
-def hidden_layer(normed, own, middle, w_gate, w_up, w_down, count, collective_id, pieces=8):
+    gather.finish()
+
+
+def hidden_layer(
+    normed, own, near, middle, w_gate, w_up, w_down, count, collective_id, pieces=8
+):
     chunk_rows, width = own.shape
     hidden = w_gate.shape[1]
     rows = count * chunk_rows
@@ -864,7 +819,7 @@
             jax.ShapeDtypeStruct((count, chunk_rows, width), BF16),
             jax.ShapeDtypeStruct((chunk_rows, width), BF16),
         ),
-        in_specs=[hbm, hbm] + vmem_specs(1) + [hbm, hbm, hbm],
+        in_specs=[hbm] * 3 + vmem_specs(1) + [hbm] * 3,
         out_specs=(hbm, hbm, hbm, hbm, hbm, vmem_specs(1)[0]),
         scratch_shapes=[
             pltpu.VMEM((width, hidden), BF16),
@@ -881,24 +836,24 @@
             pltpu.VMEM((landing_rows(count, chunk_rows), width), BF16),
             copy_sems(count, pieces), copy_sems(count, pieces),
             copy_sems(count, SUBS), copy_sems(count, SUBS),
-            pltpu.SemaphoreType.DMA((5,)), pltpu.SemaphoreType.DMA((4,)),
+            pltpu.SemaphoreType.DMA((7,)), pltpu.SemaphoreType.DMA((4,)),
         ],
         compiler_params=params(collective_id=collective_id, has_side_effects=True),
         cost_estimate=pl.CostEstimate(
             flops=12 * rows * width * hidden, bytes_accessed=1 << 26, transcendentals=rows * hidden
         ),
         name="hidden_layer",
-    )(normed, own, middle, w_gate, w_up, w_down)
+    )(normed, own, near, middle, w_gate, w_up, w_down)
     return [outs[0]] + [out.reshape(rows, out.shape[-1]) for out in outs[1:5]] + [outs[5]]
 
 
 def backward_turn_kernel(
     count, pieces, given_ref, dy_ref, middle_ref, gain_ref,
     normed_full_ref, gate_grad_ref, up_grad_ref, active_ref, dy_full_ref,
-    grad_ref, full_ref, gain_grad_ref, sums_ref, down_grad_ref, traded_ref,
+    grad_ref, full_ref, gain_grad_ref, sums_ref, down_grad_ref, gate_out_ref, traded_ref,
     partial, landing, tiles, traded, normed, gate_grad, active, dy_full, kept, arrived,
-    rs_send, rs_receive, ag_send, ag_receive, load, trade_send, trade_receive, fetches, stores,
-    peer_send, peer_receive, operands,
+    arrived_two, summed, rs_send, rs_receive, ag_send, ag_receive, load, trade_send, trade_receive, fetches, stores,
+    peer_send, peer_receive, operands, summed_out,
 ):
     line = Line(count)
     chunk_rows = dy_ref.shape[0]
@@ -916,7 +871,7 @@
     replica = lax.axis_index("dp")
     side, mine = replica % 2, replica // 2
     partner = replica + 1 - 2 * side
-    halves = kept.shape[0]
+    halves = kept.shape[0] // traded.shape[0]
     others = [(mine + step) % halves for step in range(1, halves)]
     semaphore = pltpu.get_barrier_semaphore()
     pl.semaphore_signal(semaphore, 1, device_id={"dp": partner})
@@ -960,24 +915,32 @@
 
     def put(pair):
         rows = pl.ds(pl.multiple_of((pair % halves) * block, block), block)
-        columns = pl.ds(pl.multiple_of((pair // halves - 1) * width, width), width)
         return pltpu.make_async_copy(
-            tiles.at[pair % 2, ours], sums_ref.at[rows, columns], stores.at[pair % 2]
+            tiles.at[pair % 2, ours], sums_ref.at[rows], stores.at[pair % 2]
         )
 
-    def peer(half, place):
+    folds = ((kept, arrived), (dy_full, arrived_two))
+
+    def kept_rows(half):
+        return pl.ds(pl.multiple_of(half * block, block), block)
+
+    def peer(which, half, slot):
+        source, landing = folds[which]
         return pltpu.make_async_remote_copy(
-            src_ref=kept.at[half], dst_ref=arrived.at[place],
-            send_sem=peer_send.at[half], recv_sem=peer_receive.at[place],
+            src_ref=source.at[kept_rows(half)], dst_ref=landing.at[slot],
+            send_sem=peer_send.at[which, half], recv_sem=peer_receive.at[which, slot],
             device_id={"dp": 2 * half + side},
         )
+
+    def slot_of(sender, owner):
+        return (sender - owner + halves - 1) % halves
 
     def beside(pair):
         @pl.when((pair >= 2) & (pair < pairs))
         def _():
             trade(pair - 2).wait_send()
 
-            @pl.when(pair - 2 >= halves)
+            @pl.when(pair - 2 >= 2 * halves)
             def _():
                 put(pair - 2).wait()
 
@@ -1010,40 +973,57 @@
             slot = last % 2
             total = tiles[slot, ours].astype(F32) + traded[...].astype(F32)
 
-            @pl.when(last < halves)
-            def _():
-                kept[last % halves] = total.astype(BF16)
-
-                @pl.when(last != mine)
-                def _():
-                    peer(last, mine).start()
-
-            @pl.when(last >= halves)
+            for which in range(2):
+                @pl.when(last // halves == which)
+                def _(which=which):
+                    half = last % halves
+                    folds[which][0][kept_rows(half), :] = total.astype(BF16)
+
+                    @pl.when(half != mine)
+                    def _():
+                        peer(which, half, slot_of(mine, half)).start()
+
+            @pl.when(last >= 2 * halves)
             def _():
                 tiles[slot, ours] = total.astype(BF16)
                 put(last).start()
 
-    turns = pieces + 2 * (count - 1)
-
-    @pl.loop(0, max(turns, pairs + 1))
+    def add_up(which):
+        total = folds[which][0][kept_rows(mine), :].astype(F32)
+        for half in others:
+            slot = slot_of(half, mine)
+            peer(which, half, slot).wait_recv()
+            total = total + folds[which][1][slot].astype(F32)
+        summed[...] = total
+        for half in others:
+            peer(which, half, slot_of(mine, half)).wait_send()
+
+    def hand_out(which):
+        return pltpu.make_async_copy(summed, (down_grad_ref, gate_out_ref)[which], summed_out)
+
+    turns = max(pieces + 2 * (count - 1), pairs + 1)
+
+    @pl.loop(0, turns)
     def _(turn):
         scatter.turn(turn)
         gather.turn(turn)
         scatter.settle(turn, settle)
         beside(turn)
 
+        @pl.when(turn == turns - 1)
+        def _():
+            add_up(0)
+            hand_out(0).start()
+
     for pair in range(pairs - 2, pairs):
         trade(pair).wait_send()
         put(pair).wait()
-    total = kept[mine].astype(F32)
-    for half in others:
-        peer(half, half).wait_recv()
-        total = total + arrived[half].astype(F32)
-    down_grad_ref[...] = total
-    for half in others:
-        peer(half, mine).wait_send()
+    hand_out(0).wait()
+    add_up(1)
+    hand_out(1).start()
     scatter.finish()
     gather.finish()
+    hand_out(1).wait()
 
 
 def norm_back(grad, rows, gain):
@@ -1070,12 +1050,13 @@
             jax.ShapeDtypeStruct((chunk_rows, width), F32),
             jax.ShapeDtypeStruct((rows, width), BF16),
             jax.ShapeDtypeStruct((1, width), F32),
-            jax.ShapeDtypeStruct((kept_rows, 2 * width), BF16),
+            jax.ShapeDtypeStruct((kept_rows, width), BF16),
+            jax.ShapeDtypeStruct((block, width), F32),
             jax.ShapeDtypeStruct((block, width), F32),
             jax.ShapeDtypeStruct((pairs, block, width), BF16),
         ),
         in_specs=[hbm] + vmem_specs(3) + [hbm] * 5,
-        out_specs=tuple(vmem_specs(3)) + (hbm, vmem_specs(1)[0], hbm),
+        out_specs=tuple(vmem_specs(3)) + (hbm,) * 4,
         scratch_shapes=[
             pltpu.VMEM((rows, width), BF16),
             pltpu.VMEM((landing_rows(count, chunk_rows), width), BF16),
@@ -1083,7 +1064,9 @@
             pltpu.VMEM((block, width), BF16),
         ]
         + [pltpu.VMEM((rows, width), BF16)] * 4
-        + [pltpu.VMEM((replicas // 2, block, width), BF16)] * 2
+        + [pltpu.VMEM((kept_rows, width), BF16)]
+        + [pltpu.VMEM((replicas // 2 - 1, block, width), BF16)] * 2
+        + [pltpu.VMEM((block, width), F32)]
         + [copy_sems(count, pieces)] * 4
         + [
             pltpu.SemaphoreType.DMA,
@@ -1091,9 +1074,10 @@
             pltpu.SemaphoreType.DMA((pairs,)),
             pltpu.SemaphoreType.DMA,
             pltpu.SemaphoreType.DMA((2,)),
-            pltpu.SemaphoreType.DMA((replicas // 2,)),
-            pltpu.SemaphoreType.DMA((replicas // 2,)),
+            pltpu.SemaphoreType.DMA((2, replicas // 2)),
+            pltpu.SemaphoreType.DMA((2, replicas // 2)),
             pltpu.SemaphoreType.DMA((5,)),
+            pltpu.SemaphoreType.DMA,
         ],
         compiler_params=params(collective_id=collective_id, has_side_effects=True),
         cost_estimate=pl.CostEstimate(
@@ -1103,17 +1087,33 @@
     )(given, dy, middle, gain, normed_full, gate_grad, up_grad, active, dy_full)
 
 
+STREAM_OFFSET = 4
+STREAM_HOP = 2
+
+
 def last_turn_kernel(
-    count, pieces, replicas, dqkv_ref, packed_ref, normed_ref, middle_grad_ref, x_ref, gain_ref,
-    gain_two_ref, grad_ref, query_grad_ref, key_grad_ref, value_grad_ref, gain_one_out, gain_two_out,
-    w_ref, sems,
-    partial, landing, sums, traded, arrived, pair_sems, sends, receives,
+    count, pieces, replicas, branch_ref, out_ref, mixed_ref, q_ref, k_ref, v_ref, lse_ref, cos_ref,
+    sin_ref, start_ref, packed_ref, normed_in, middle_grad_in, x_in, gain_ref, gain_two_ref,
+    grad_ref, out_grad_ref, query_grad_ref, key_grad_ref, value_grad_ref, gain_one_out, gain_two_out,
+    dqkv_ref, dmix_ref, bias_ref, dq_ref, dk_ref, dv_ref, w_ref, sems,
+    normed_ref, middle_grad_ref, x_ref, operands, partial, landing,
+    out_sums, out_traded, out_arrived, out_pair, out_sends, out_receives,
+    sums, traded, arrived, pair_sems, sends, receives,
     gain_own, gain_row, gain_land, gains_ref, gain_line,
     rs_send, rs_receive, dp_send, dp_receive, line_send, line_receive,
 ):
     line = Line(count)
     chunk_rows = x_ref.shape[0]
+    q_width = q_ref.shape[1]
+    slabs = q_width // SLAB
+    kv_heads = k_ref.shape[0]
+    members = slabs // kv_heads
+    scale = HEAD_SIZE ** (-0.5)
     fetches = weight_fetches(packed_ref, w_ref, sems)
+    for at, (source, target) in enumerate(
+        ((middle_grad_in, middle_grad_ref), (x_in, x_ref), (normed_in, normed_ref))
+    ):
+        fetches.append(pltpu.make_async_copy(source, target, operands.at[at]))
     for fetch in fetches:
         fetch.start()
     replica = lax.axis_index("dp")
@@ -1122,35 +1122,115 @@
         pl.semaphore_signal(semaphore, 1, device_id={"dp": (replica + step) % replicas})
     for step in range(1, count):
         pl.semaphore_signal(semaphore, 1, device_id={"tensor": (line.place + step) % count})
-    pl.semaphore_wait(semaphore, replicas - 1 + count - 1)
+    out_fold = Fold(replicas, out_sums, out_traded, out_arrived, out_pair, out_sends, out_receives)
     fold = Fold(replicas, sums, traded, arrived, pair_sems, sends, receives)
-    for fetch in fetches:
-        fetch.wait()
-
-    @pl.loop(0, partial.shape[0] // SPAN)
-    def _(step):
-        rows = pl.ds(pl.multiple_of(step * SPAN, SPAN), SPAN)
-        partial[rows, :] = project_back(dqkv_ref[rows, :], w_ref[...]).astype(BF16)
-
-    scatter = Scatter(line, partial, landing, rs_send, rs_receive, chunk_rows, pieces)
+    stream = Stream(
+        line, partial, landing, rs_send, rs_receive, chunk_rows, pieces, STREAM_OFFSET, STREAM_HOP
+    )
     size = chunk_rows // pieces
     gain_own[...] = jnp.zeros_like(gain_own)
+    dk_ref[...] = jnp.zeros_like(dk_ref)
+    dv_ref[...] = jnp.zeros_like(dv_ref)
 
     def settle(piece):
         local = pl.ds(pl.multiple_of(piece * size, size), size)
-        total = scatter.total(piece)
+        total = stream.total(piece)
         grad, gain_grad = norm_back(total, x_ref[local, :].astype(F32), gain_ref[...])
         gain_own[...] += gain_grad
         grad_ref[local, :] = (grad + middle_grad_ref[local, :]).astype(BF16)
 
+    def exchange(turn):
+        stream.turn(turn)
+        stream.settle(turn, settle)
+
+    left = lanes((SPAN, SLAB)) < HEAD_SIZE
+
+    def attend_tile(tile, done):
+        first, span = tile * SPAN, (tile + 1) * SPAN
+        rows = slice(first, first + SPAN)
+        dmix_ref[...] = project_back(branch_ref[rows, :], out_ref[...]).astype(BF16)
+        key_ids = lax.broadcasted_iota(jnp.int32, (span, SPAN), 0)
+        row_ids = first + lanes((span, SPAN))
+        allowed = (key_ids >= start_ref[:, rows]) & (key_ids <= row_ids)
+        bias_ref[:span, :] = jnp.where(allowed, 0.0, mask_fill)
+
+        @pl.loop(0, slabs)
+        def _(slab):
+            at = pl.ds(pl.multiple_of(slab * SLAB, SLAB), SLAB)
+            head = slab // members
+            queries = head_pair(q_ref[rows, at])
+            grads = head_pair(dmix_ref[:, at])
+            keys = k_ref[head, :span, :]
+            scores = project_back(keys, queries)
+            bias = bias_ref[:span, :]
+            logs = jnp.concatenate(
+                [lse_ref[pl.ds(2 * slab, 1), rows], lse_ref[pl.ds(2 * slab + 1, 1), rows]], axis=1
+            )
+            chances = jnp.exp(scores + jnp.concatenate([bias, bias], axis=1) - logs)
+            chances_grad = project_back(v_ref[head, :span, :], grads)
+            shared = jnp.sum(chances * chances_grad, axis=0, keepdims=True)
+            score_grad = (chances * (chances_grad - shared)).astype(BF16)
+            dv_ref[head, :span, :] += project(chances.astype(BF16), grads)
+            dk_ref[head, :span, :] += project(score_grad, queries)
+            dq_ref[:, at] = join_pair(row_contract(score_grad, keys)) * scale
+            if done is not None:
+                @pl.when(slab < STREAM_OFFSET - 1)
+                def _():
+                    exchange(done + slab)
+
+        cosine, sine = cos_ref[rows, :], sin_ref[rows, :]
+        for slab in range(slabs):
+            part = dq_ref[:, slab * SLAB : (slab + 1) * SLAB]
+            part = part * cosine - turned(part) * sine
+            dqkv_ref[rows, slab * SLAB : (slab + 1) * SLAB] = part.astype(BF16)
+        for pair in range(kv_heads // 2):
+            joined = []
+            for ref in (dk_ref, dv_ref):
+                both = []
+                for head in (2 * pair, 2 * pair + 1):
+                    full = ref[head, rows, :]
+                    both.append(full + pltpu.roll(full, HEAD_SIZE, 1))
+                joined.append(jnp.where(left, both[0], both[1]))
+            key, value = joined
+            key = key * cosine - turned(key) * sine
+            at = q_width + pair * SLAB
+            dqkv_ref[rows, at : at + SLAB] = key.astype(BF16)
+            at = at + (kv_heads // 2) * SLAB
+            dqkv_ref[rows, at : at + SLAB] = value.astype(BF16)
+        if tile == tiles - 1:
+            for fetch in fetches:
+                fetch.wait()
+            pl.semaphore_wait(semaphore, replicas - 1 + count - 1)
+        partial[rows, :] = project_back(dqkv_ref[rows, :], w_ref[...]).astype(BF16)
+
+    tiles = branch_ref.shape[0] // SPAN
+    done = 0
+    for tile in reversed(range(tiles)):
+        attend_tile(tile, done if tile < tiles - 1 else None)
+        if tile < tiles - 1:
+            done += min(slabs, STREAM_OFFSET - 1)
+        exchange(done)
+        done += 1
+
     block = sums.shape[2]
-
-    @pl.loop(0, pieces + count - 1)
+    out_rows = out_sums.shape[2]
+
+    @pl.loop(done, stream.turns)
     def _(turn):
-        scatter.turn(turn)
-        scatter.settle(turn, settle)
-
-        @pl.when(turn == 0)
+        exchange(turn)
+
+        @pl.when(turn == done)
+        def _():
+            for step in range(q_width // SLAB):
+                first = step * SLAB
+                product = row_contract(mixed_ref[:, first : first + SLAB], branch_ref[...])
+                product = product.astype(BF16)
+                for row in range(0, SLAB, out_rows):
+                    owner = (first + row) // out_rows
+                    out_sums[owner // 2, owner % 2] = product[row : row + out_rows]
+            out_fold.pair().start()
+
+        @pl.when(turn == done + 1)
         def _():
             @pl.loop(0, replicas // 2)
             def _(half):
@@ -1161,7 +1241,11 @@
 
             fold.pair().start()
 
-        @pl.when(turn == 2)
+        @pl.when(turn == done + 3)
+        def _():
+            out_fold.spread()
+
+        @pl.when(turn == done + 4)
         def _():
             fold.spread()
 
@@ -1185,6 +1269,7 @@
     places = [(line.place + step) % count for step in range(1, count)]
     for peer in peers:
         share(peer, replica).start()
+    out_grad_ref[...] = out_fold.total()
     total = fold.total()
     at = 0
     for ref in (query_grad_ref, key_grad_ref, value_grad_ref):
@@ -1197,7 +1282,8 @@
     gains_ref[...] = total
     for peer in places:
         pass_line(peer, line.place).start()
-    scatter.finish()
+    stream.finish()
+    out_fold.finish()
     fold.finish()
     for peer in peers:
         share(peer, replica).wait_send()
@@ -1216,28 +1302,45 @@
 
 
 def last_turn(
-    dqkv, w_qkv, normed, middle_grad, x, gain, gain_two_grad, widths, count, replicas,
-    collective_id, pieces=8,
+    branch, w_out, mixed, queries, keys, values, lse, cosine, sine, start,
+    w_qkv, normed, middle_grad, x, gain, gain_two_grad, widths, count, replicas, collective_id,
+    pieces=8,
 ):
     chunk_rows, width = x.shape
-    rows = count * chunk_rows
+    rows, q_width = queries.shape
+    kv_heads = keys.shape[0]
     block = width // replicas
+    qkv_width = sum(widths)
+    out_rows = q_width // replicas
+    flops = 2 * rows * width * (2 * q_width + 2 * qkv_width) + 20 * rows * rows * q_width
     return pl.pallas_call(
         functools.partial(last_turn_kernel, count, pieces, replicas),
         out_shape=(
             jax.ShapeDtypeStruct((chunk_rows, width), BF16),
+            jax.ShapeDtypeStruct((out_rows, width), F32),
         )
         + tuple(jax.ShapeDtypeStruct((block, part), F32) for part in widths)
         + (jax.ShapeDtypeStruct((1, block), F32),) * 2,
-        in_specs=vmem_specs(1) + [pl.BlockSpec(memory_space=pl.ANY)] + vmem_specs(5),
-        out_specs=tuple(vmem_specs(6)),
+        in_specs=vmem_specs(10) + [pl.BlockSpec(memory_space=pl.ANY)] * 4 + vmem_specs(2),
+        out_specs=tuple(vmem_specs(7)),
         scratch_shapes=[
-            pltpu.VMEM((width, dqkv.shape[1]), BF16),
+            pltpu.VMEM((rows, qkv_width), BF16),
+            pltpu.VMEM((SPAN, q_width), BF16),
+            pltpu.VMEM((rows, SPAN), F32),
+            pltpu.VMEM((SPAN, q_width), F32),
+            pltpu.VMEM((kv_heads, rows, SLAB), F32),
+            pltpu.VMEM((kv_heads, rows, SLAB), F32),
+            pltpu.VMEM((width, qkv_width), BF16),
             pltpu.SemaphoreType.DMA((replicas,)),
+            pltpu.VMEM((rows, width), BF16),
+            pltpu.VMEM((chunk_rows, width), F32),
+            pltpu.VMEM((chunk_rows, width), BF16),
+            pltpu.SemaphoreType.DMA((3,)),
             pltpu.VMEM((rows, width), BF16),
             pltpu.VMEM((landing_rows(count, chunk_rows), width), BF16),
         ]
-        + fold_scratch(replicas, block, dqkv.shape[1])
+        + fold_scratch(replicas, out_rows, width)
+        + fold_scratch(replicas, block, qkv_width)
         + [
             pltpu.VMEM((1, width), F32),
             pltpu.VMEM((2, width), F32),
@@ -1250,11 +1353,13 @@
         + [pltpu.SemaphoreType.DMA((count,))] * 2,
         compiler_params=params(collective_id=collective_id, has_side_effects=True),
         cost_estimate=pl.CostEstimate(
-            flops=4 * rows * width * dqkv.shape[1],
-            bytes_accessed=200 * chunk_rows * width, transcendentals=0,
+            flops=flops, bytes_accessed=1 << 25, transcendentals=1 << 23
         ),
         name="last_turn",
-    )(dqkv, w_qkv, normed, middle_grad, x, gain, gain_two_grad)
+    )(
+        branch, w_out, mixed, queries, keys, values, lse, cosine, sine, start,
+        w_qkv, normed, middle_grad, x, gain, gain_two_grad,
+    )
 
 
 def shards(
@@ -1281,29 +1386,26 @@
     x_full, cosine, sine, start_column, start_row = line_gather(
         inputs, rotary_freqs()[None], seq_lengths, group_perm, group_starts, count, 0
     )
-    normed_full, queries, keys, values, mixed, lse = attend(
-        x_full, qkv_full, gain_one, cosine, sine, start_column, q_width, kv_width
+    normed_full, queries, keys, values, mixed, lse, near = attend(
+        x_full, qkv_full, gain_one, cosine, sine, start_column, cotangent,
+        q_width, kv_width, count, 5,
     )
     replicas = lax.axis_size("dp")
     middle, normed_two_full = forward_turn(mixed, out_full, inputs, gain_two, count, 1)
     grad_full, active, gate_grad, up_grad, norm_two_grad, outputs = hidden_layer(
-        normed_two_full, cotangent, middle, gate_full, up_full, down_full, count, 4
+        normed_two_full, cotangent, near, middle, gate_full, up_full, down_full, count, 4
     )
-    middle_grad, branch_full, gain_two_grad, sums, down_grad, _ = backward_turn(
+    middle_grad, branch_full, gain_two_grad, sums, down_grad, gate_weight_grad, _ = backward_turn(
         norm_two_grad, cotangent, middle, gain_two, normed_two_full, gate_grad, up_grad, active,
         grad_full, count, replicas, 2,
     )
     sides = [list(range(side, replicas, 2)) for side in range(2)]
-    hidden_grads = lax.psum_scatter(
+    up_weight_grad = lax.psum_scatter(
         sums, "dp", scatter_dimension=0, axis_index_groups=sides, tiled=True
     ).astype(F32)
-    gate_weight_grad, up_weight_grad = jnp.split(hidden_grads, 2, axis=1)
-    dqkv, out_grad = attend_back(
+    input_grad, out_grad, query_grad, key_grad, value_grad, gain_one_grad, gain_two_grad = last_turn(
         branch_full, out_full, mixed, queries, keys, values, lse, cosine, sine, start_row,
-        replicas, 5,
-    )
-    input_grad, query_grad, key_grad, value_grad, gain_one_grad, gain_two_grad = last_turn(
-        dqkv, qkv_full, normed_full, middle_grad, inputs, gain_one, gain_two_grad,
+        qkv_full, normed_full, middle_grad, inputs, gain_one, gain_two_grad,
         (q_width, kv_width, kv_width), count, replicas, 3,
     )
     return (

time: 652 us -> 619 us (0.949)
  Pallas kernels: 609 us -> 578 us
    pallas_call x2 -> x1, Pallas kernels: 66.2 us -> 30.6 us  [attend(): pl.pallas_call(functools.partial(attend_kernel, count), out_shape=(jax.Sh...]
    pallas_call x1, Pallas kernels: 93.7 us -> 116 us  [last_turn(): pl.pallas_call(functools.partial(last_turn_kernel, count, pieces, replica...]
    pallas_call x1, Pallas kernels: 125 us -> 102 us  [hidden_layer(): pl.pallas_call(functools.partial(hidden_kernel, count, pieces), out_shape...]
  transfers between devices with their start and end apart: 6 -> 6, of which waited for: 1 -> 0; matrix products, arithmetic and copies ran while one was open for 0% -> 0% of each run, Pallas kernels for 56% -> 56%
where the time goes in v4:
time: 619 us; the launch traced here: 612 us
  Pallas kernels  578 us (93%)
  between operations  14.5 us (2%)
  local copies, waits for them, and re-layouts  10.1 us (2%)
  other arithmetic  6.9 us (1%)
    pallas_call x1, Pallas kernels, backward_turn(): pl.pallas_call(functools.partial(backward_turn_kernel, count, pieces), ou...  130 us
    pallas_call x1, Pallas kernels, forward_turn(): pl.pallas_call(functools.partial(forward_turn_kernel, count, pieces), out...  122 us
    pallas_call x1, Pallas kernels, last_turn(): pl.pallas_call(functools.partial(last_turn_kernel, count, pieces, replica...  116 us
    pallas_call x1, Pallas kernels, hidden_layer(): pl.pallas_call(functools.partial(hidden_kernel, count, pieces), out_shape...  102 us
    pallas_call x1, Pallas kernels, line_gather(): pl.pallas_call(functools.partial(gather_kernel, count, pieces), out_shape...  76.1 us
    pallas_call x1, Pallas kernels, attend(): pl.pallas_call(functools.partial(attend_kernel, count), out_shape=(jax.Sh...  30.6 us
  transfers between devices with their start and end apart: 6, of which 0 were waited for; matrix products, arithmetic and copies ran while one was open for 0% of the time, Pallas kernels for 56%

profile of v4, /device:TPU:0, one launch (start us, length us, event | category | flops | bytes accessed | tf_op | source)
XLA Modules:
  0.0 611.9 jit_solution(10660093335253573632)
XLA Ops:
  7.2 0.7 pad_maximum_fusion
  7.9 1.8 fusion.1
  9.8 0.0 all-gather.7.cloned.1.call-start
  9.8 0.7 all-gather.7.cloned.1.call-update
  10.6 0.7 all-gather.9.cloned.1.call-update
  11.3 0.5 all-gather.11.cloned.1.call-update
  11.9 0.5 all-gather.13.cloned.1.call-update
  12.4 0.0 reduce-scatter.2.cloned.1.call-start
  12.5 0.1 lt.18
  12.6 0.1 gt.14
  12.7 0.1 pow.16
  12.8 0.5 select_select_fusion.freqs_ref
  13.3 76.1 %line_gather.1 = (bf16[1024,2048]{1,0:T(8,128)(2,1)}, f32[1024,128]{1,0:T(8,128)}, f32[1024,128]{1,0:T(8,128)}, s32[1024,1]{1,0:T(8,128)}, s32[1,1024]{1,0:T(1,128)}) custom-call(bf16[256,2048]{1,0:T(8,128)(2,1)} %x_in.1, f32[1,128]{1,0:T(1,128)} %select_select_fusion.freqs_ref, s32[12]{0:T(128)} %lengths_ref.1, s32[12]{0:T(128)} %perm_ref.1, s32[9]{0:T(128)} %starts_ref.1), custom_call_target="tpu_custom_call" | custom-call | bytes 104857600 | tf_op jit(solution)/shard_map/line_gather/pallas_call | solution.py:559
  89.5 0.9 fusion.2
  90.4 0.6 copy.27
  91.0 0.6 copy.26
  91.6 30.6 %attend.1 = (bf16[1024,2048]{1,0:T(8,128)(2,1)}, bf16[1024,512]{1,0:T(8,128)(2,1)}, bf16[2,1024,128]{2,1,0:T(8,128)(2,1)}, bf16[2,1024,128]{2,1,0:T(8,128)(2,1)}...) custom-call(bf16[1024,2048]{1,0:T(8,128)(2,1)} %get-tuple-element.44.x_ref, ...), custom_call_target="tpu_custom_call" | custom-call | flops 7516192768 | bytes 16777216 | tf_op jit(solution)/shard_map/attend/pallas_call | solution.py:197
  122.2 122.4 %forward_turn.1 = (f32[256,2048]{1,0:T(8,128)}, bf16[1024,2048]{1,0:T(8,128)(2,1)}) custom-call(bf16[1024,512]{1,0:T(8,128)(2,1)} %get-tuple-element.48.mixed_ref, bf16[512,2048]{1,0:T(8,128)(2,1)} %all-gather.7.cloned.1.call-done.w_ref.out_ref, bf16[256,2048]{1,0:T(8,128)(2,1)} %x_in.1, f32[1,2048]{1,0:T(1,128)} %bitcast.19), custom_call_target="tpu_custom_call" | custom-call | flops 2147483648 | bytes 157286400 | tf_op jit(solution)/shard_map/forward_turn/pallas_call | solution.py:622
  244.7 102.2 %hidden_layer.1 = (bf16[1024,2048]{1,0:T(8,128)(2,1)}, bf16[4,256,2048]{2,1,0:T(8,128)(2,1)}, bf16[4,256,2048]{2,1,0:T(8,128)(2,1)}, bf16[4,256,2048]{2,1,0:T(8,...) custom-call(bf16[1024,2048]{1,0:T(8,128)(2,1)} %get-tuple-element.49.normed_ref.normed_full_ref, ...), custom_call_target="tpu_custom_call" | custom-call | flops 51539607552 | bytes 67108864 | tf_op jit(solution)/shard_map/hidden_layer/pallas_call | solution.py:815
  346.9 130.0 %backward_turn.1 = (f32[256,2048]{1,0:T(8,128)}, bf16[1024,2048]{1,0:T(8,128)(2,1)}, f32[1,2048]{1,0:T(1,128)}, bf16[1024,2048]{1,0:T(8,128)(2,1)}, f32[256,2048...) custom-call(bf16[1024,2048]{1,0:T(8,128)(2,1)} %bitcast.29, bf16[256,2048]{1,0:T(8,128)(2,1)} %dy_ref.3, ...), custom_call_target="tpu_custom_call" | custom-call | flops 25769803776 | bytes 67108864 | tf_op jit(solution)/shard_map/backward_turn/pallas_call | solution.py:1047
  476.9 116.3 %last_turn.1 = (bf16[256,2048]{1,0:T(8,128)(2,1)}, f32[64,2048]{1,0:T(8,128)}, f32[256,512]{1,0:T(8,128)}, f32[256,128]{1,0:T(8,128)}, f32[256,128]{1,0:T(8,128)}, /*index=5*/f32[1,256]{1,0:T(1,128)}, f32[1,256]{1,0:T(1,128)}) custom-call(bf16[1024,2048]{1,0:T(8,128)(2,1)} %get-tuple-element.58.branch_ref, ...), custom_call_target="tpu_custom_call" | custom-call | flops 21474836480 | bytes 33554432 | tf_op jit(solution)/shard_map/last_turn/pallas_call | solution.py:1316
  593.3 2.9 convert_element_type.10
  596.2 1.0 copy.38
  597.2 1.0 copy.39
  598.2 0.6 copy.40
  598.8 0.8 copy.41
  599.6 0.7 copy.42
  600.2 0.7 copy.43
  600.9 0.8 copy.44
  601.7 0.6 copy.45
  602.2 1.3 copy.46
  603.6 1.3 copy.47
  (37 shorter events, 0.4 us)
Async XLA Ops:
  7.2 82.3 %all-gather.15.cloned.1.call-start = ((), (), s32[]{:S(2)}) async-start(), calls=%async_computation.6 | async-start | bytes 3760128 | tf_op jit(solution)/shard_map/all_gather | solution.py:1377
  9.8 112.5 %all-gather.7.cloned.1.call-start = ((), (), s32[]{:S(2)}) async-start(), calls=%async_computation.1 | async-start | bytes 2359296 | tf_op jit(solution)/shard_map/all_gather | solution.py:1378
  10.5 234.1 %all-gather.9.cloned.1.call-start = ((), (), s32[]{:S(2)}) async-start(), calls=%async_computation.2 | async-start | bytes 9437184 | tf_op jit(solution)/shard_map/all_gather | solution.py:1379
  11.2 233.4 %all-gather.11.cloned.1.call-start = ((), (), s32[]{:S(2)}) async-start(), calls=%async_computation.3 | async-start | bytes 9437184 | tf_op jit(solution)/shard_map/all_gather | solution.py:1380
  11.8 232.9 %all-gather.13.cloned.1.call-start = ((), (), s32[]{:S(2)}) async-start(), calls=%async_computation.4 | async-start | bytes 9437184 | tf_op jit(solution)/shard_map/all_gather | solution.py:1381
  12.4 580.9 %reduce-scatter.2.cloned.1.call-start = ((), (), s32[]{:S(2)}) async-start(), calls=%async_computation.5 | async-start | bytes 5242880 | tf_op jit(solution)/shard_map/reduce_scatter | solution.py:1403
  476.9 119.3 %copy-start.2 = (bf16[256,2048]{1,0:T(8,128)(2,1)S(1)}, bf16[256,2048]{1,0:T(8,128)(2,1)}, u32[]{:S(2)}) copy-start(bf16[256,2048]{1,0:T(8,128)(2,1)} %get-tuple-element.90) | copy-start | bytes 3145732
  593.2 4.0 copy-start.3
  593.2 5.0 copy-start.9
  593.2 5.5 copy-start.5
  593.2 6.3 %copy-start.7 = (f32[256,128]{1,0:T(8,128)S(1)}, f32[256,128]{1,0:T(8,128)}, u32[]{:S(2)}) copy-start(f32[256,128]{1,0:T(8,128)} %get-tuple-element.94) | copy-start | bytes 393220
  593.2 7.0 %copy-start.6 = (f32[256,128]{1,0:T(8,128)S(1)}, f32[256,128]{1,0:T(8,128)}, u32[]{:S(2)}) copy-start(f32[256,128]{1,0:T(8,128)} %get-tuple-element.95) | copy-start | bytes 393220
  593.3 7.6 %copy-start.4 = (f32[64,2048]{1,0:T(8,128)S(1)}, f32[64,2048]{1,0:T(8,128)}, u32[]{:S(2)}) copy-start(f32[64,2048]{1,0:T(8,128)} %get-tuple-element.96) | copy-start | bytes 1572868
  596.2 5.4 copy-start.8
  596.2 6.0 copy-start.1
  597.2 6.3 %copy-start = (f32[256,2048]{1,0:T(8,128)S(1)}, f32[256,2048]{1,0:T(8,128)}, u32[]{:S(2)}) copy-start(f32[256,2048]{1,0:T(8,128)} %get-tuple-element.100) | copy-start | bytes 6291460
Sparse Core Ops, SparseCore 0:
  10.4 35.7 all-gather.14
  48.1 27.7 all-gather.6
  77.8 54.2 all-gather.8
  133.9 54.1 all-gather.10
  189.9 54.2 all-gather.12
  477.0 78.9 reduce-scatter.1

commit v5 on v4

--- a/solution.py
+++ b/solution.py
@@ -253,10 +253,12 @@
 
 
 class Gather:
-    def __init__(self, line, full, send, receive, chunk_rows, pieces, lags=None, near=0):
+    def __init__(
+        self, line, full, send, receive, chunk_rows, pieces, lags=None, near=0, late=True
+    ):
         self.line, self.full, self.send, self.receive = line, full, send, receive
         self.chunk_rows, self.size, self.pieces = chunk_rows, chunk_rows // pieces, pieces
-        self.lags, self.near = lags or [0] * line.count, near
+        self.lags, self.near, self.late = lags or [0] * line.count, near, late
 
     def rows(self, chunk, piece):
         start = chunk * self.chunk_rows + piece * self.size
@@ -291,10 +293,13 @@
 
                 @pl.when((hop > 0) & (piece >= 0) & (piece < self.pieces))
                 def _(way=way, chunk=chunk, piece=piece):
-                    self.copy(chunk, piece, way).wait_recv()
+                    if not self.late:
+                        self.copy(chunk, piece, way).wait_recv()
 
                     @pl.when(line.has[way])
                     def _():
+                        if self.late:
+                            self.copy(chunk, piece, way).wait_recv()
                         self.copy(chunk, piece, way).start()
 
     def finish(self, source=None):
@@ -302,6 +307,14 @@
 
         @pl.loop(0, self.pieces)
         def _(piece):
+            for chunk in range(line.count if self.late else 0):
+                for way, end in ((0, line.count - 1), (1, 0)):
+                    hop = line.place - chunk if way == 0 else chunk - line.place
+
+                    @pl.when((line.place == end) & (hop > self.near))
+                    def _(way=way, chunk=chunk):
+                        self.copy(chunk, piece, way).wait_recv()
+
             for chunk in range(line.count):
                 @pl.when(line.has[0] & (chunk <= line.place - self.near))
                 def _(chunk=chunk):
@@ -518,15 +531,36 @@
 
 
 def gather_kernel(
-    count, pieces, x_ref, freqs_ref, lengths_ref, perm_ref, starts_ref,
-    full_ref, cos_ref, sin_ref, column_ref, row_ref, send, receive, local,
+    count, replicas, pieces, x_ref, freqs_ref, out_ref, lengths_ref, perm_ref, starts_ref,
+    full_ref, cos_ref, sin_ref, column_ref, row_ref, out_full_ref, send, receive, local,
+    deal_send, deal_receive,
 ):
     line = Line(count)
     chunk_rows = x_ref.shape[0]
     own = pl.ds(pl.multiple_of(line.place * chunk_rows, chunk_rows), chunk_rows)
-    keep = pltpu.make_async_copy(x_ref, full_ref.at[own], local)
+    keep = pltpu.make_async_copy(x_ref, full_ref.at[own], local.at[0])
     keep.start()
-    line.barrier()
+    replica = lax.axis_index("dp")
+    peers = [(replica + step) % replicas for step in range(1, replicas)]
+    out_rows = out_ref.shape[0]
+
+    def out_at(owner):
+        return out_full_ref.at[pl.ds(pl.multiple_of(owner * out_rows, out_rows), out_rows)]
+
+    def deal(peer, owner):
+        return pltpu.make_async_remote_copy(
+            src_ref=out_ref, dst_ref=out_at(owner), send_sem=deal_send.at[peer],
+            recv_sem=deal_receive.at[owner], device_id={"dp": peer},
+        )
+
+    keep_out = pltpu.make_async_copy(out_ref, out_at(replica), local.at[1])
+    keep_out.start()
+    semaphore = pltpu.get_barrier_semaphore()
+    for peer in peers:
+        pl.semaphore_signal(semaphore, 1, device_id={"dp": peer})
+    pl.semaphore_wait(semaphore, line.greet(semaphore) + replicas - 1)
+    for peer in peers:
+        deal(peer, replica).start()
     gather = Gather(line, full_ref, send, receive, chunk_rows, pieces)
     for piece in range(pieces):
         gather.start(piece, x_ref.at[gather.rows(0, piece)])
@@ -550,32 +584,41 @@
             column_ref[pl.ds(first, size), :] = start[:, 0:1]
 
     gather.finish(x_ref.at[gather.rows(0, 0)])
+    for peer in peers:
+        deal(peer, peer).wait_recv()
+        deal(peer, replica).wait_send()
     keep.wait()
-
-
-def line_gather(x, freqs, lengths, perm, starts, count, collective_id, pieces=8):
+    keep_out.wait()
+
+
+def line_gather(
+    x, freqs, w_out, lengths, perm, starts, count, replicas, collective_id, pieces=8
+):
     rows, width = x.shape
     total = count * rows
+    hbm = pl.BlockSpec(memory_space=pl.ANY)
     return pl.pallas_call(
-        functools.partial(gather_kernel, count, pieces),
+        functools.partial(gather_kernel, count, replicas, pieces),
         out_shape=(
             jax.ShapeDtypeStruct((total, width), x.dtype),
             jax.ShapeDtypeStruct((total, SLAB), F32),
             jax.ShapeDtypeStruct((total, SLAB), F32),
             jax.ShapeDtypeStruct((total, 1), jnp.int32),
             jax.ShapeDtypeStruct((1, total), jnp.int32),
+            jax.ShapeDtypeStruct((replicas * w_out.shape[0], w_out.shape[1]), w_out.dtype),
         ),
-        in_specs=vmem_specs(2) + [pl.BlockSpec(memory_space=pltpu.SMEM)] * 3,
-        out_specs=(pl.BlockSpec(memory_space=pl.ANY),) + tuple(vmem_specs(4)),
+        in_specs=vmem_specs(2) + [hbm] + [pl.BlockSpec(memory_space=pltpu.SMEM)] * 3,
+        out_specs=(hbm,) + tuple(vmem_specs(4)) + (hbm,),
         scratch_shapes=[
-            copy_sems(count, pieces), copy_sems(count, pieces), pltpu.SemaphoreType.DMA
+            copy_sems(count, pieces), copy_sems(count, pieces), pltpu.SemaphoreType.DMA((2,)),
+            pltpu.SemaphoreType.DMA((replicas,)), pltpu.SemaphoreType.DMA((replicas,)),
         ],
         compiler_params=params(collective_id=collective_id, has_side_effects=True),
         cost_estimate=pl.CostEstimate(
             flops=0, bytes_accessed=200 * rows * width, transcendentals=0
         ),
         name="line_gather",
-    )(x, freqs, lengths, perm, starts)
+    )(x, freqs, w_out, lengths, perm, starts)
 
 
 def forward_turn_kernel(
@@ -661,7 +704,9 @@
     for fetch in fetches:
         fetch.start()
     line.barrier()
-    gather = Gather(line, dy, ag_send, ag_receive, chunk_rows, SUBS, near=1)
+    gather = Gather(
+        line, dy, ag_send, ag_receive, chunk_rows, SUBS, near=1, late=False
+    )
     scatter = Scatter(line, partial, landing, rs_send, rs_receive, chunk_rows, pieces)
     for piece in range(SUBS):
         gather.start_near(piece, near_ref)
@@ -1375,7 +1420,6 @@
     packed = jnp.concatenate([w_query, w_key, w_value], axis=1)
     packed = jnp.concatenate([packed, gains], axis=0)
     qkv_full = lax.all_gather(packed[None], "dp", axis=0, tiled=True)
-    out_full = lax.all_gather(w_out, "dp", axis=0, tiled=True)
     gate_full = lax.all_gather(w_gate, "dp", axis=0, tiled=True)
     up_full = lax.all_gather(w_up, "dp", axis=0, tiled=True)
     down_full = lax.all_gather(w_down, "dp", axis=0, tiled=True)
@@ -1383,14 +1427,15 @@
     gain_rows = jnp.transpose(gain_rows, (1, 0, 2)).reshape(2, -1)
     gain_one, gain_two = gain_rows[0:1], gain_rows[1:2]
 
-    x_full, cosine, sine, start_column, start_row = line_gather(
-        inputs, rotary_freqs()[None], seq_lengths, group_perm, group_starts, count, 0
+    replicas = lax.axis_size("dp")
+    x_full, cosine, sine, start_column, start_row, out_full = line_gather(
+        inputs, rotary_freqs()[None], w_out, seq_lengths, group_perm, group_starts,
+        count, replicas, 0,
     )
     normed_full, queries, keys, values, mixed, lse, near = attend(
         x_full, qkv_full, gain_one, cosine, sine, start_column, cotangent,
         q_width, kv_width, count, 5,
     )
-    replicas = lax.axis_size("dp")
     middle, normed_two_full = forward_turn(mixed, out_full, inputs, gain_two, count, 1)
     grad_full, active, gate_grad, up_grad, norm_two_grad, outputs = hidden_layer(
         normed_two_full, cotangent, near, middle, gate_full, up_full, down_full, count, 4

time: 619 us -> 612 us (0.989)
    pallas_call x1, Pallas kernels: 130 us -> 123 us  [backward_turn(): pl.pallas_call(functools.partial(backward_turn_kernel, count, pieces), ou...]
  transfers between devices with their start and end apart: 6 -> 5, of which waited for: 0 -> 0; matrix products, arithmetic and copies ran while one was open for 0% -> 0% of each run, Pallas kernels for 56% -> 58%
where the time goes in v5:
time: 612 us; the launch traced here: 605 us
  Pallas kernels  572 us (93%)
  between operations  14.2 us (2%)
  local copies, waits for them, and re-layouts  10.1 us (2%)
  other arithmetic  6.9 us (1%)
    pallas_call x1, Pallas kernels, backward_turn(): pl.pallas_call(functools.partial(backward_turn_kernel, count, pieces), ou...  123 us
    pallas_call x1, Pallas kernels, last_turn(): pl.pallas_call(functools.partial(last_turn_kernel, count, pieces, replica...  121 us
    pallas_call x1, Pallas kernels, forward_turn(): pl.pallas_call(functools.partial(forward_turn_kernel, count, pieces), out...  119 us
    pallas_call x1, Pallas kernels, hidden_layer(): pl.pallas_call(functools.partial(hidden_kernel, count, pieces), out_shape...  99.7 us
    pallas_call x1, Pallas kernels, line_gather(): pl.pallas_call(functools.partial(gather_kernel, count, replicas, pieces),...  77.8 us
    pallas_call x1, Pallas kernels, attend(): pl.pallas_call(functools.partial(attend_kernel, count), out_shape=(jax.Sh...  30.9 us
  transfers between devices with their start and end apart: 5, of which 0 were waited for; matrix products, arithmetic and copies ran while one was open for 0% of the time, Pallas kernels for 58%

profile of v5, /device:TPU:0, one launch (start us, length us, event | category | flops | bytes accessed | tf_op | source)
XLA Modules:
  0.0 605.0 jit_solution(1110065727789179742)
XLA Ops:
  7.2 0.7 pad_maximum_fusion
  7.9 1.8 fusion.1
  9.8 0.0 all-gather.6.cloned.1.call-start
  9.8 0.7 all-gather.6.cloned.1.call-update
  10.5 0.0 all-gather.8.cloned.1.call-start
  10.6 0.7 all-gather.8.cloned.1.call-update
  11.3 0.5 all-gather.10.cloned.1.call-update
  11.8 0.0 reduce-scatter.2.cloned.1.call-start
  11.9 0.1 lt.18
  12.0 0.1 gt.14
  12.1 0.1 pow.16
  12.2 0.5 select_select_fusion.freqs_ref
  12.7 77.8 %line_gather.1 = (bf16[1024,2048]{1,0:T(8,128)(2,1)}, f32[1024,128]{1,0:T(8,128)}, f32[1024,128]{1,0:T(8,128)}, s32[1024,1]{1,0:T(8,128)}, s32[1,1024]{1,0:T(1,128)}, /*index=5*/bf16[512,2048]{1,0:T(8,128)(2,1)}) custom-call(bf16[256,2048]{1,0:T(8,128)(2,1)} %x_in.1, f32[1,128]{1,0:T(1,128)} %select_select_fusion.freqs_ref, bf16[64,2048]{1,0:T(8,128)(2,1)} %out_ref.1, ...), custom_call_target="tpu_custom_call" | custom-call | bytes 104857600 | tf_op jit(solution)/shard_map/line_gather/pallas_call | solution.py:600
  90.5 0.9 fusion.2
  91.4 0.6 copy.27
  92.0 0.6 copy.26
  92.6 30.9 %attend.1 = (bf16[1024,2048]{1,0:T(8,128)(2,1)}, bf16[1024,512]{1,0:T(8,128)(2,1)}, bf16[2,1024,128]{2,1,0:T(8,128)(2,1)}, bf16[2,1024,128]{2,1,0:T(8,128)(2,1)}...) custom-call(bf16[1024,2048]{1,0:T(8,128)(2,1)} %get-tuple-element.45.x_ref, ...), custom_call_target="tpu_custom_call" | custom-call | flops 7516192768 | bytes 16777216 | tf_op jit(solution)/shard_map/attend/pallas_call | solution.py:197
  123.5 119.0 %forward_turn.1 = (f32[256,2048]{1,0:T(8,128)}, bf16[1024,2048]{1,0:T(8,128)(2,1)}) custom-call(bf16[1024,512]{1,0:T(8,128)(2,1)} %get-tuple-element.49.mixed_ref, bf16[512,2048]{1,0:T(8,128)(2,1)} %get-tuple-element.50.w_ref.out_ref, bf16[256,2048]{1,0:T(8,128)(2,1)} %x_in.1, f32[1,2048]{1,0:T(1,128)} %bitcast.19), custom_call_target="tpu_custom_call" | custom-call | flops 2147483648 | bytes 157286400 | tf_op jit(solution)/shard_map/forward_turn/pallas_call | solution.py:665
  242.6 99.7 %hidden_layer.1 = (bf16[1024,2048]{1,0:T(8,128)(2,1)}, bf16[4,256,2048]{2,1,0:T(8,128)(2,1)}, bf16[4,256,2048]{2,1,0:T(8,128)(2,1)}, bf16[4,256,2048]{2,1,0:T(8,...) custom-call(bf16[1024,2048]{1,0:T(8,128)(2,1)} %get-tuple-element.51.normed_ref.normed_full_ref, ...), custom_call_target="tpu_custom_call" | custom-call | flops 51539607552 | bytes 67108864 | tf_op jit(solution)/shard_map/hidden_layer/pallas_call | solution.py:860
  342.4 122.7 %backward_turn.1 = (f32[256,2048]{1,0:T(8,128)}, bf16[1024,2048]{1,0:T(8,128)(2,1)}, f32[1,2048]{1,0:T(1,128)}, bf16[1024,2048]{1,0:T(8,128)(2,1)}, f32[256,2048...) custom-call(bf16[1024,2048]{1,0:T(8,128)(2,1)} %bitcast.29, bf16[256,2048]{1,0:T(8,128)(2,1)} %dy_ref.3, ...), custom_call_target="tpu_custom_call" | custom-call | flops 25769803776 | bytes 67108864 | tf_op jit(solution)/shard_map/backward_turn/pallas_call | solution.py:1092
  465.1 121.4 %last_turn.1 = (bf16[256,2048]{1,0:T(8,128)(2,1)}, f32[64,2048]{1,0:T(8,128)}, f32[256,512]{1,0:T(8,128)}, f32[256,128]{1,0:T(8,128)}, f32[256,128]{1,0:T(8,128)}, /*index=5*/f32[1,256]{1,0:T(1,128)}, f32[1,256]{1,0:T(1,128)}) custom-call(bf16[1024,2048]{1,0:T(8,128)(2,1)} %get-tuple-element.60.branch_ref, ...), custom_call_target="tpu_custom_call" | custom-call | flops 21474836480 | bytes 33554432 | tf_op jit(solution)/shard_map/last_turn/pallas_call | solution.py:1361
  586.6 2.9 convert_element_type.10
  589.6 1.0 copy.38
  590.6 1.0 copy.39
  591.5 0.6 copy.40
  592.1 0.8 copy.41
  592.9 0.7 copy.42
  593.5 0.7 copy.43
  594.2 0.8 copy.44
  595.0 0.6 copy.45
  595.6 1.3 copy.46
  596.9 1.3 copy.47
  (34 shorter events, 0.3 us)
Async XLA Ops:
  7.2 83.3 %all-gather.12.cloned.1.call-start = ((), (), s32[]{:S(2)}) async-start(), calls=%async_computation.5 | async-start | bytes 3760128 | tf_op jit(solution)/shard_map/all_gather | solution.py:1422
  9.8 232.8 %all-gather.6.cloned.1.call-start = ((), (), s32[]{:S(2)}) async-start(), calls=%async_computation.1 | async-start | bytes 9437184 | tf_op jit(solution)/shard_map/all_gather | solution.py:1423
  10.5 232.1 %all-gather.8.cloned.1.call-start = ((), (), s32[]{:S(2)}) async-start(), calls=%async_computation.2 | async-start | bytes 9437184 | tf_op jit(solution)/shard_map/all_gather | solution.py:1424
  11.2 231.4 %all-gather.10.cloned.1.call-start = ((), (), s32[]{:S(2)}) async-start(), calls=%async_computation.3 | async-start | bytes 9437184 | tf_op jit(solution)/shard_map/all_gather | solution.py:1425
  11.8 574.8 %reduce-scatter.2.cloned.1.call-start = ((), (), s32[]{:S(2)}) async-start(), calls=%async_computation.4 | async-start | bytes 5242880 | tf_op jit(solution)/shard_map/reduce_scatter | solution.py:1448
  465.1 124.4 %copy-start.2 = (bf16[256,2048]{1,0:T(8,128)(2,1)S(1)}, bf16[256,2048]{1,0:T(8,128)(2,1)}, u32[]{:S(2)}) copy-start(bf16[256,2048]{1,0:T(8,128)(2,1)} %get-tuple-element.92) | copy-start | bytes 3145732
  586.5 4.0 copy-start.3
  586.6 5.0 copy-start.9
  586.6 5.5 copy-start.5
  586.6 6.3 %copy-start.7 = (f32[256,128]{1,0:T(8,128)S(1)}, f32[256,128]{1,0:T(8,128)}, u32[]{:S(2)}) copy-start(f32[256,128]{1,0:T(8,128)} %get-tuple-element.96) | copy-start | bytes 393220
  586.6 7.0 %copy-start.6 = (f32[256,128]{1,0:T(8,128)S(1)}, f32[256,128]{1,0:T(8,128)}, u32[]{:S(2)}) copy-start(f32[256,128]{1,0:T(8,128)} %get-tuple-element.97) | copy-start | bytes 393220
  586.6 7.6 %copy-start.4 = (f32[64,2048]{1,0:T(8,128)S(1)}, f32[64,2048]{1,0:T(8,128)}, u32[]{:S(2)}) copy-start(f32[64,2048]{1,0:T(8,128)} %get-tuple-element.98) | copy-start | bytes 1572868
  589.6 5.4 copy-start.8
  589.6 6.0 copy-start.1
  590.6 6.3 %copy-start = (f32[256,2048]{1,0:T(8,128)S(1)}, f32[256,2048]{1,0:T(8,128)}, u32[]{:S(2)}) copy-start(f32[256,2048]{1,0:T(8,128)} %get-tuple-element.102) | copy-start | bytes 6291460
Sparse Core Ops, SparseCore 0:
  10.4 47.9 all-gather.11
  60.3 54.2 all-gather.5
  116.5 54.2 all-gather.7
  172.5 54.2 all-gather.9
  465.2 84.3 reduce-scatter.1
